TPU v7x, 32 devices: a whole 2x2x4 slice. The times are simulated.
32 devices in a mesh: shot: 4 (over z), pair: 2 (over y), space: 4 (over x, core).
Axes of the slice: x: 2, y: 2, z: 4, core: 2. Of those that a mesh axis runs over, the one named last changes fastest.
Arguments:
- states: float32 [4, 2, 2, 64, 128, 128], P('shot', 'pair', None, 'space'), may hold values from -4 to 4
- courant: float32 [64, 128, 128], P('space'), may hold values from 0.05 to 0.2
- records: float32 [4, 12, 64, 128], P('shot', None, 'space'), may hold values from -6 to 6
Outputs:
- imaging: float32 [64, 128, 128], P('space', 'shot', 'pair')
All inputs are finite; a program needn't handle non-finite values.
Results may differ from a plain program's by a relative error of at most 0.00002.
Values sent between devices are 32-bit elements; how exact they have to be, the bound alone decides.
No kernel may reach another device: no remote copies, remote signals or barrier semaphores. Data moves between devices by JAX's collectives and lax.ppermute only.
A program may use at most 64 MiB of HBM per device.

v0:
```python
import jax
import jax.numpy as jnp
from jax import lax
from jax.sharding import PartitionSpec as P

STEPS = 12
IMAGE_EVERY = 2


def extended_2(array, sides, width):
    for axis, dim in sides:
        peers, length = (lax.axis_size(axis), array.shape[dim])
        up = [(i, (i + 1) % peers) for i in range(peers - 1)]
        down = [(j, i) for i, j in up]
        last = lax.slice_in_dim(array, length - width, length, axis=dim)
        first = lax.slice_in_dim(array, 0, width, axis=dim)
        before = lax.ppermute(last, axis, up)
        after = lax.ppermute(first, axis, down)
        array = jnp.concatenate([before, array, after], axis=dim)
    return array


def partner_2(value, axis, distance):
    mask = 2**distance
    pairs = [(source, source ^ mask) for source in range(lax.axis_size(axis))]
    return lax.ppermute(value, axis, pairs)


def laplacian(extended, center):
    base = center.ndim - 3

    def along(whole, dim_axis, extent):

        def shifted(start):
            return lax.slice_in_dim(whole, start, start + extent, axis=dim_axis)

        return (
            -shifted(0) + 16.0 * shifted(1) - 30.0 * shifted(2) + 16.0 * shifted(3) - shifted(4)
        ) / 12.0

    widths_y = [(0, 0)] * base + [(0, 0), (2, 2), (0, 0)]
    widths_z = [(0, 0)] * base + [(0, 0), (0, 0), (2, 2)]
    total = along(extended, base, center.shape[base])
    total = total + along(jnp.pad(center, widths_y), base + 1, center.shape[base + 1])
    total = total + along(jnp.pad(center, widths_z), base + 2, center.shape[base + 2])
    return total


def on_device(states, courant, records):
    row_role = lax.axis_index("pair")
    inject = (row_role == 1).astype(jnp.float32)
    own_states = states[0, 0]
    rounds = STEPS // IMAGE_EVERY
    weight = IMAGE_EVERY / STEPS
    halfway = courant.shape[2] // 2
    mine_start = row_role * halfway
    other_start = (1 - row_role) * halfway
    blank = jnp.zeros((courant.shape[0], courant.shape[1], halfway), jnp.float32)

    def advance(earlier, current, tick_index):
        extended = extended_2(current, (("space", 0),), 2)
        advanced = 2.0 * current - earlier + courant * laplacian(extended, current)
        record = lax.dynamic_index_in_dim(records[0], tick_index, 0, keepdims=False)
        advanced = advanced.at[:, :, 0].add(inject * record)
        return (current, advanced)

    def one_round(index_round, carry):
        earlier, current, imaging = carry
        for inner in range(IMAGE_EVERY):
            earlier, current = advance(earlier, current, index_round * IMAGE_EVERY + inner)
        outgoing = lax.dynamic_slice_in_dim(current, other_start, halfway, 2)
        partner = partner_2(outgoing, "pair", 0)
        kept = lax.dynamic_slice_in_dim(current, mine_start, halfway, 2)
        return (earlier, current, imaging + kept * partner)

    carry = (own_states[0], own_states[1], blank)
    carry = lax.fori_loop(0, rounds, one_round, carry)
    imaging = carry[2]
    scaled = imaging * weight
    return lax.psum_scatter(scaled, "shot", scatter_dimension=1, tiled=True)


def solution(mesh):
    placed = (
        P("shot", "pair", None, "space", None, None),
        P("space", None, None),
        P("shot", None, "space", None),
    )
    return jax.shard_map(
        on_device, mesh=mesh, in_specs=placed, out_specs=P("space", "shot", "pair"), check_vma=False
    )
```

profile of v0, /device:TPU:0, one launch (start us, length us, event | category | flops | bytes accessed | tf_op | source)
XLA Modules:
  0.0 302.1 jit_solution(8155652060473405264)
XLA Ops:
  6.5 1.8 fusion.52
  9.3 1.7 copy.30
  11.1 249.8 %while.22 = (s32[]{:T(128)}, f32[16,128,128]{1,0,2:T(8,128)S(1)}, f32[16,128,128]{1,0,2:T(8,128)S(1)}, f32[16,128,64]{1,0,2:T(8,128)}, f32[16,128,128]{1,0,2:T(8...) while((s32[]{:T(128)}, f32[16,128,128]{1,0,2:T(8,128)S(1)}, ...), condition=%wide.region_1.2_spmd.clone, body=%wide.region_0.1_spmd.clone.sunk | while | flops 17178628 | bytes 21676496 | solution.py:77
  11.8 2.4 collective-permute-start
  16.6 3.1 %collective-permute-done.1 = f32[2,128,128]{1,0,2:T(2,128)S(1)} collective-permute-done((f32[2,128,128]{1,0,2:T(2,128)}, f32[2,128,128]{1,0,2:T(2,128)S(1)}, u32[]{:S(2)}, u32[]{:S(2)}) %collective-permute-start.1) | collective-permute-done | bytes 131104 | tf_op jit(solution)/shard_map/while/body/eval_jaxpr/ppermute | solution.py:18
  20.5 3.6 %fusion.60 = f32[16,128,128]{1,0,2:T(8,128)S(1)} fusion(f32[16,128,128]{1,0,2:T(8,128)S(1)} %get-tuple-element.465, f32[2,128,128]{1,0,2:T(2,128)S(1)} %collective-permute-done, f32[16,128,128]{1,0,2:T(8,128)S(1)} %get-tuple-element.449, f32[18,128,128]{1,0,2:T(8,128)} %constant_dynamic-update-slice_fusion.5, f32[16,128,128]{1,0,2:T(8,128)S(1)} %get-tuple-element.448), kind=kLoop, calls=%fused_computation.37.clone.1 | loop fusion | flops 8126464 | bytes 6422528 | tf_op jit(solution)/shard_map/while/body/eval_jaxpr/add | solution.py:62
  26.9 6.1 %collective-permute-start.3 = (f32[2,128,128]{1,0,2:T(2,128)S(1)}, f32[2,128,128]{1,0,2:T(2,128)S(1)}, u32[]{:S(2)}, u32[]{:S(2)}) collective-permute-start(f32[2,128,128]{1,0,2:T(2,128)S(1)} %get-tuple-element.432), channel_id=1, source_target_pairs={{0,1},{1,2},{2,3},{4,5},{5,6},{6,7},{8,9},{9,10},{10,11},{12,13},{... | collective-permute-start | bytes 393224 | tf_op jit(solution)/shard_map/while/body/eval_jaxpr/ppermute | solution.py:17
  33.9 2.0 fusion.63
  39.0 11.9 %collective-permute-done.4 = f32[16,128,64]{1,0,2:T(8,128)} collective-permute-done((f32[16,128,64]{1,0,2:T(8,128)}, f32[16,128,64]{1,0,2:T(8,128)}, u32[]{:S(2)}, u32[]{:S(2)}) %collective-permute-start.4) | collective-permute-done | bytes 524320 | tf_op jit(solution)/shard_map/while/body/eval_jaxpr/ppermute | solution.py:26
  50.8 1.9 select_add_fusion.2
  53.5 3.4 %collective-permute-start = (f32[2,128,128]{1,0,2:T(2,128)S(1)}, f32[2,128,128]{1,0,2:T(2,128)S(1)}, u32[]{:S(2)}, u32[]{:S(2)}) collective-permute-start(f32[2,128,128]{1,0,2:T(2,128)S(1)} %get-tuple-element.429), channel_id=1, source_target_pairs={{0,1},{1,2},{2,3},{4,5},{5,6},{6,7},{8,9},{9,10},{10,11},{12,13},{... | collective-permute-start | bytes 393224 | tf_op jit(solution)/shard_map/while/body/eval_jaxpr/ppermute | solution.py:17
  59.4 1.9 collective-permute-done.1
  62.0 3.6 %fusion.60 = f32[16,128,128]{1,0,2:T(8,128)S(1)} fusion(f32[16,128,128]{1,0,2:T(8,128)S(1)} %get-tuple-element.465, f32[2,128,128]{1,0,2:T(2,128)S(1)} %collective-permute-done, f32[16,128,128]{1,0,2:T(8,128)S(1)} %get-tuple-element.449, f32[18,128,128]{1,0,2:T(8,128)} %constant_dynamic-update-slice_fusion.5, f32[16,128,128]{1,0,2:T(8,128)S(1)} %get-tuple-element.448), kind=kLoop, calls=%fused_computation.37.clone.1 | loop fusion | flops 8126464 | bytes 6422528 | tf_op jit(solution)/shard_map/while/body/eval_jaxpr/add | solution.py:62
  68.4 6.1 %collective-permute-start.3 = (f32[2,128,128]{1,0,2:T(2,128)S(1)}, f32[2,128,128]{1,0,2:T(2,128)S(1)}, u32[]{:S(2)}, u32[]{:S(2)}) collective-permute-start(f32[2,128,128]{1,0,2:T(2,128)S(1)} %get-tuple-element.432), channel_id=1, source_target_pairs={{0,1},{1,2},{2,3},{4,5},{5,6},{6,7},{8,9},{9,10},{10,11},{12,13},{... | collective-permute-start | bytes 393224 | tf_op jit(solution)/shard_map/while/body/eval_jaxpr/ppermute | solution.py:17
  75.4 2.0 fusion.63
  80.4 11.9 %collective-permute-done.4 = f32[16,128,64]{1,0,2:T(8,128)} collective-permute-done((f32[16,128,64]{1,0,2:T(8,128)}, f32[16,128,64]{1,0,2:T(8,128)}, u32[]{:S(2)}, u32[]{:S(2)}) %collective-permute-start.4) | collective-permute-done | bytes 524320 | tf_op jit(solution)/shard_map/while/body/eval_jaxpr/ppermute | solution.py:26
  92.3 2.1 select_add_fusion.2
  95.1 3.4 %collective-permute-start = (f32[2,128,128]{1,0,2:T(2,128)S(1)}, f32[2,128,128]{1,0,2:T(2,128)S(1)}, u32[]{:S(2)}, u32[]{:S(2)}) collective-permute-start(f32[2,128,128]{1,0,2:T(2,128)S(1)} %get-tuple-element.429), channel_id=1, source_target_pairs={{0,1},{1,2},{2,3},{4,5},{5,6},{6,7},{8,9},{9,10},{10,11},{12,13},{... | collective-permute-start | bytes 393224 | tf_op jit(solution)/shard_map/while/body/eval_jaxpr/ppermute | solution.py:17
  101.0 1.9 collective-permute-done.1
  103.6 3.6 %fusion.60 = f32[16,128,128]{1,0,2:T(8,128)S(1)} fusion(f32[16,128,128]{1,0,2:T(8,128)S(1)} %get-tuple-element.465, f32[2,128,128]{1,0,2:T(2,128)S(1)} %collective-permute-done, f32[16,128,128]{1,0,2:T(8,128)S(1)} %get-tuple-element.449, f32[18,128,128]{1,0,2:T(8,128)} %constant_dynamic-update-slice_fusion.5, f32[16,128,128]{1,0,2:T(8,128)S(1)} %get-tuple-element.448), kind=kLoop, calls=%fused_computation.37.clone.1 | loop fusion | flops 8126464 | bytes 6422528 | tf_op jit(solution)/shard_map/while/body/eval_jaxpr/add | solution.py:62
  110.0 6.1 %collective-permute-start.3 = (f32[2,128,128]{1,0,2:T(2,128)S(1)}, f32[2,128,128]{1,0,2:T(2,128)S(1)}, u32[]{:S(2)}, u32[]{:S(2)}) collective-permute-start(f32[2,128,128]{1,0,2:T(2,128)S(1)} %get-tuple-element.432), channel_id=1, source_target_pairs={{0,1},{1,2},{2,3},{4,5},{5,6},{6,7},{8,9},{9,10},{10,11},{12,13},{... | collective-permute-start | bytes 393224 | tf_op jit(solution)/shard_map/while/body/eval_jaxpr/ppermute | solution.py:17
  117.0 2.0 fusion.63
  122.1 11.9 %collective-permute-done.4 = f32[16,128,64]{1,0,2:T(8,128)} collective-permute-done((f32[16,128,64]{1,0,2:T(8,128)}, f32[16,128,64]{1,0,2:T(8,128)}, u32[]{:S(2)}, u32[]{:S(2)}) %collective-permute-start.4) | collective-permute-done | bytes 524320 | tf_op jit(solution)/shard_map/while/body/eval_jaxpr/ppermute | solution.py:26
  133.9 2.1 select_add_fusion.2
  136.8 3.4 %collective-permute-start = (f32[2,128,128]{1,0,2:T(2,128)S(1)}, f32[2,128,128]{1,0,2:T(2,128)S(1)}, u32[]{:S(2)}, u32[]{:S(2)}) collective-permute-start(f32[2,128,128]{1,0,2:T(2,128)S(1)} %get-tuple-element.429), channel_id=1, source_target_pairs={{0,1},{1,2},{2,3},{4,5},{5,6},{6,7},{8,9},{9,10},{10,11},{12,13},{... | collective-permute-start | bytes 393224 | tf_op jit(solution)/shard_map/while/body/eval_jaxpr/ppermute | solution.py:17
  142.6 1.9 collective-permute-done.1
  145.2 3.6 %fusion.60 = f32[16,128,128]{1,0,2:T(8,128)S(1)} fusion(f32[16,128,128]{1,0,2:T(8,128)S(1)} %get-tuple-element.465, f32[2,128,128]{1,0,2:T(2,128)S(1)} %collective-permute-done, f32[16,128,128]{1,0,2:T(8,128)S(1)} %get-tuple-element.449, f32[18,128,128]{1,0,2:T(8,128)} %constant_dynamic-update-slice_fusion.5, f32[16,128,128]{1,0,2:T(8,128)S(1)} %get-tuple-element.448), kind=kLoop, calls=%fused_computation.37.clone.1 | loop fusion | flops 8126464 | bytes 6422528 | tf_op jit(solution)/shard_map/while/body/eval_jaxpr/add | solution.py:62
  151.6 6.1 %collective-permute-start.3 = (f32[2,128,128]{1,0,2:T(2,128)S(1)}, f32[2,128,128]{1,0,2:T(2,128)S(1)}, u32[]{:S(2)}, u32[]{:S(2)}) collective-permute-start(f32[2,128,128]{1,0,2:T(2,128)S(1)} %get-tuple-element.432), channel_id=1, source_target_pairs={{0,1},{1,2},{2,3},{4,5},{5,6},{6,7},{8,9},{9,10},{10,11},{12,13},{... | collective-permute-start | bytes 393224 | tf_op jit(solution)/shard_map/while/body/eval_jaxpr/ppermute | solution.py:17
  158.7 2.0 fusion.63
  163.7 11.9 %collective-permute-done.4 = f32[16,128,64]{1,0,2:T(8,128)} collective-permute-done((f32[16,128,64]{1,0,2:T(8,128)}, f32[16,128,64]{1,0,2:T(8,128)}, u32[]{:S(2)}, u32[]{:S(2)}) %collective-permute-start.4) | collective-permute-done | bytes 524320 | tf_op jit(solution)/shard_map/while/body/eval_jaxpr/ppermute | solution.py:26
  175.5 2.1 select_add_fusion.2
  178.4 3.4 %collective-permute-start = (f32[2,128,128]{1,0,2:T(2,128)S(1)}, f32[2,128,128]{1,0,2:T(2,128)S(1)}, u32[]{:S(2)}, u32[]{:S(2)}) collective-permute-start(f32[2,128,128]{1,0,2:T(2,128)S(1)} %get-tuple-element.429), channel_id=1, source_target_pairs={{0,1},{1,2},{2,3},{4,5},{5,6},{6,7},{8,9},{9,10},{10,11},{12,13},{... | collective-permute-start | bytes 393224 | tf_op jit(solution)/shard_map/while/body/eval_jaxpr/ppermute | solution.py:17
  184.2 1.9 collective-permute-done.1
  186.9 3.6 %fusion.60 = f32[16,128,128]{1,0,2:T(8,128)S(1)} fusion(f32[16,128,128]{1,0,2:T(8,128)S(1)} %get-tuple-element.465, f32[2,128,128]{1,0,2:T(2,128)S(1)} %collective-permute-done, f32[16,128,128]{1,0,2:T(8,128)S(1)} %get-tuple-element.449, f32[18,128,128]{1,0,2:T(8,128)} %constant_dynamic-update-slice_fusion.5, f32[16,128,128]{1,0,2:T(8,128)S(1)} %get-tuple-element.448), kind=kLoop, calls=%fused_computation.37.clone.1 | loop fusion | flops 8126464 | bytes 6422528 | tf_op jit(solution)/shard_map/while/body/eval_jaxpr/add | solution.py:62
  193.2 6.1 %collective-permute-start.3 = (f32[2,128,128]{1,0,2:T(2,128)S(1)}, f32[2,128,128]{1,0,2:T(2,128)S(1)}, u32[]{:S(2)}, u32[]{:S(2)}) collective-permute-start(f32[2,128,128]{1,0,2:T(2,128)S(1)} %get-tuple-element.432), channel_id=1, source_target_pairs={{0,1},{1,2},{2,3},{4,5},{5,6},{6,7},{8,9},{9,10},{10,11},{12,13},{... | collective-permute-start | bytes 393224 | tf_op jit(solution)/shard_map/while/body/eval_jaxpr/ppermute | solution.py:17
  200.3 2.0 fusion.63
  205.3 11.9 %collective-permute-done.4 = f32[16,128,64]{1,0,2:T(8,128)} collective-permute-done((f32[16,128,64]{1,0,2:T(8,128)}, f32[16,128,64]{1,0,2:T(8,128)}, u32[]{:S(2)}, u32[]{:S(2)}) %collective-permute-start.4) | collective-permute-done | bytes 524320 | tf_op jit(solution)/shard_map/while/body/eval_jaxpr/ppermute | solution.py:26
  217.2 2.1 select_add_fusion.2
  220.0 3.4 %collective-permute-start = (f32[2,128,128]{1,0,2:T(2,128)S(1)}, f32[2,128,128]{1,0,2:T(2,128)S(1)}, u32[]{:S(2)}, u32[]{:S(2)}) collective-permute-start(f32[2,128,128]{1,0,2:T(2,128)S(1)} %get-tuple-element.429), channel_id=1, source_target_pairs={{0,1},{1,2},{2,3},{4,5},{5,6},{6,7},{8,9},{9,10},{10,11},{12,13},{... | collective-permute-start | bytes 393224 | tf_op jit(solution)/shard_map/while/body/eval_jaxpr/ppermute | solution.py:17
  225.9 1.9 collective-permute-done.1
  228.5 3.6 %fusion.60 = f32[16,128,128]{1,0,2:T(8,128)S(1)} fusion(f32[16,128,128]{1,0,2:T(8,128)S(1)} %get-tuple-element.465, f32[2,128,128]{1,0,2:T(2,128)S(1)} %collective-permute-done, f32[16,128,128]{1,0,2:T(8,128)S(1)} %get-tuple-element.449, f32[18,128,128]{1,0,2:T(8,128)} %constant_dynamic-update-slice_fusion.5, f32[16,128,128]{1,0,2:T(8,128)S(1)} %get-tuple-element.448), kind=kLoop, calls=%fused_computation.37.clone.1 | loop fusion | flops 8126464 | bytes 6422528 | tf_op jit(solution)/shard_map/while/body/eval_jaxpr/add | solution.py:62
  234.8 6.1 %collective-permute-start.3 = (f32[2,128,128]{1,0,2:T(2,128)S(1)}, f32[2,128,128]{1,0,2:T(2,128)S(1)}, u32[]{:S(2)}, u32[]{:S(2)}) collective-permute-start(f32[2,128,128]{1,0,2:T(2,128)S(1)} %get-tuple-element.432), channel_id=1, source_target_pairs={{0,1},{1,2},{2,3},{4,5},{5,6},{6,7},{8,9},{9,10},{10,11},{12,13},{... | collective-permute-start | bytes 393224 | tf_op jit(solution)/shard_map/while/body/eval_jaxpr/ppermute | solution.py:17
  241.9 2.0 fusion.63
  245.4 1.5 collective-permute-start.4
  246.9 11.9 %collective-permute-done.4 = f32[16,128,64]{1,0,2:T(8,128)} collective-permute-done((f32[16,128,64]{1,0,2:T(8,128)}, f32[16,128,64]{1,0,2:T(8,128)}, u32[]{:S(2)}, u32[]{:S(2)}) %collective-permute-start.4) | collective-permute-done | bytes 524320 | tf_op jit(solution)/shard_map/while/body/eval_jaxpr/ppermute | solution.py:26
  258.8 2.1 select_add_fusion.2
  263.5 30.0 %reduce-scatter.2.cloned.1.call-done = f32[16,32,64]{2,0,1:T(8,128)} async-done(((f32[16,128,64]{2,0,1:T(8,128)}), f32[16,32,64]{2,0,1:T(8,128)}) %reduce-scatter.2.cloned.1.call-update) | async-done | bytes 131088 | tf_op jit(solution)/shard_map/reduce_scatter | solution.py:80
  293.5 1.7 copy.33
  (84 shorter events, 65.7 us)
Async XLA Ops:
  6.5 286.9 %reduce-scatter.2.cloned.1.call-start = ((), (), s32[]{:S(2)}) async-start(), calls=%async_computation.1 | async-start | bytes 1310720 | tf_op jit(solution)/shard_map/reduce_scatter | solution.py:80
  11.8 8.7 %collective-permute-start = (f32[2,128,128]{1,0,2:T(2,128)S(1)}, f32[2,128,128]{1,0,2:T(2,128)S(1)}, u32[]{:S(2)}, u32[]{:S(2)}) collective-permute-start(f32[2,128,128]{1,0,2:T(2,128)S(1)} %get-tuple-element.429), channel_id=1, source_target_pairs={{0,1},{1,2},{2,3},{4,5},{5,6},{6,7},{8,9},{9,10},{10,11},{12,13},{... | collective-permute-start | bytes 393224 | tf_op jit(solution)/shard_map/while/body/eval_jaxpr/ppermute | solution.py:17
  14.2 5.5 %collective-permute-start.1 = (f32[2,128,128]{1,0,2:T(2,128)}, f32[2,128,128]{1,0,2:T(2,128)S(1)}, u32[]{:S(2)}, u32[]{:S(2)}) collective-permute-start(f32[2,128,128]{1,0,2:T(2,128)} %get-tuple-element.430), channel_id=1, source_target_pairs={{1,0},{2,1},{3,2},{5,4},{6,5},{7,6},{9,8},{10,9},{11,10},{13,12},{... | collective-permute-start | bytes 393224 | tf_op jit(solution)/shard_map/while/body/eval_jaxpr/ppermute | solution.py:18
  25.6 7.4 %collective-permute-start.2 = (f32[2,128,128]{1,0,2:T(2,128)}, f32[2,128,128]{1,0,2:T(2,128)S(1)}, u32[]{:S(2)}, u32[]{:S(2)}) collective-permute-start(f32[2,128,128]{1,0,2:T(2,128)} %get-tuple-element.431), channel_id=1, source_target_pairs={{1,0},{2,1},{3,2},{5,4},{6,5},{7,6},{9,8},{10,9},{11,10},{13,12},{... | collective-permute-start | bytes 393224 | tf_op jit(solution)/shard_map/while/body/eval_jaxpr/ppermute | solution.py:18
  26.9 7.1 %collective-permute-start.3 = (f32[2,128,128]{1,0,2:T(2,128)S(1)}, f32[2,128,128]{1,0,2:T(2,128)S(1)}, u32[]{:S(2)}, u32[]{:S(2)}) collective-permute-start(f32[2,128,128]{1,0,2:T(2,128)S(1)} %get-tuple-element.432), channel_id=1, source_target_pairs={{0,1},{1,2},{2,3},{4,5},{5,6},{6,7},{8,9},{9,10},{10,11},{12,13},{... | collective-permute-start | bytes 393224 | tf_op jit(solution)/shard_map/while/body/eval_jaxpr/ppermute | solution.py:17
  37.5 13.4 %collective-permute-start.4 = (f32[16,128,64]{1,0,2:T(8,128)}, f32[16,128,64]{1,0,2:T(8,128)}, u32[]{:S(2)}, u32[]{:S(2)}) collective-permute-start(f32[16,128,64]{1,0,2:T(8,128)} %constant_dynamic-slice_fusion.2), channel_id=1, source_target_pairs={{0,4},{4,0},{1,5},{5,1},{2,6},{6,2},{3,7},{7,3},{8,12},{12,8},{9,1... | collective-permute-start | bytes 1572872 | tf_op jit(solution)/shard_map/while/body/eval_jaxpr/ppermute | solution.py:26
  53.5 8.5 %collective-permute-start = (f32[2,128,128]{1,0,2:T(2,128)S(1)}, f32[2,128,128]{1,0,2:T(2,128)S(1)}, u32[]{:S(2)}, u32[]{:S(2)}) collective-permute-start(f32[2,128,128]{1,0,2:T(2,128)S(1)} %get-tuple-element.429), channel_id=1, source_target_pairs={{0,1},{1,2},{2,3},{4,5},{5,6},{6,7},{8,9},{9,10},{10,11},{12,13},{... | collective-permute-start | bytes 393224 | tf_op jit(solution)/shard_map/while/body/eval_jaxpr/ppermute | solution.py:17
  57.0 4.3 %collective-permute-start.1 = (f32[2,128,128]{1,0,2:T(2,128)}, f32[2,128,128]{1,0,2:T(2,128)S(1)}, u32[]{:S(2)}, u32[]{:S(2)}) collective-permute-start(f32[2,128,128]{1,0,2:T(2,128)} %get-tuple-element.430), channel_id=1, source_target_pairs={{1,0},{2,1},{3,2},{5,4},{6,5},{7,6},{9,8},{10,9},{11,10},{13,12},{... | collective-permute-start | bytes 393224 | tf_op jit(solution)/shard_map/while/body/eval_jaxpr/ppermute | solution.py:18
  67.1 7.4 %collective-permute-start.2 = (f32[2,128,128]{1,0,2:T(2,128)}, f32[2,128,128]{1,0,2:T(2,128)S(1)}, u32[]{:S(2)}, u32[]{:S(2)}) collective-permute-start(f32[2,128,128]{1,0,2:T(2,128)} %get-tuple-element.431), channel_id=1, source_target_pairs={{1,0},{2,1},{3,2},{5,4},{6,5},{7,6},{9,8},{10,9},{11,10},{13,12},{... | collective-permute-start | bytes 393224 | tf_op jit(solution)/shard_map/while/body/eval_jaxpr/ppermute | solution.py:18
  68.4 7.1 %collective-permute-start.3 = (f32[2,128,128]{1,0,2:T(2,128)S(1)}, f32[2,128,128]{1,0,2:T(2,128)S(1)}, u32[]{:S(2)}, u32[]{:S(2)}) collective-permute-start(f32[2,128,128]{1,0,2:T(2,128)S(1)} %get-tuple-element.432), channel_id=1, source_target_pairs={{0,1},{1,2},{2,3},{4,5},{5,6},{6,7},{8,9},{9,10},{10,11},{12,13},{... | collective-permute-start | bytes 393224 | tf_op jit(solution)/shard_map/while/body/eval_jaxpr/ppermute | solution.py:17
  78.9 13.4 %collective-permute-start.4 = (f32[16,128,64]{1,0,2:T(8,128)}, f32[16,128,64]{1,0,2:T(8,128)}, u32[]{:S(2)}, u32[]{:S(2)}) collective-permute-start(f32[16,128,64]{1,0,2:T(8,128)} %constant_dynamic-slice_fusion.2), channel_id=1, source_target_pairs={{0,4},{4,0},{1,5},{5,1},{2,6},{6,2},{3,7},{7,3},{8,12},{12,8},{9,1... | collective-permute-start | bytes 1572872 | tf_op jit(solution)/shard_map/while/body/eval_jaxpr/ppermute | solution.py:26
  95.1 8.5 %collective-permute-start = (f32[2,128,128]{1,0,2:T(2,128)S(1)}, f32[2,128,128]{1,0,2:T(2,128)S(1)}, u32[]{:S(2)}, u32[]{:S(2)}) collective-permute-start(f32[2,128,128]{1,0,2:T(2,128)S(1)} %get-tuple-element.429), channel_id=1, source_target_pairs={{0,1},{1,2},{2,3},{4,5},{5,6},{6,7},{8,9},{9,10},{10,11},{12,13},{... | collective-permute-start | bytes 393224 | tf_op jit(solution)/shard_map/while/body/eval_jaxpr/ppermute | solution.py:17
  98.6 4.3 %collective-permute-start.1 = (f32[2,128,128]{1,0,2:T(2,128)}, f32[2,128,128]{1,0,2:T(2,128)S(1)}, u32[]{:S(2)}, u32[]{:S(2)}) collective-permute-start(f32[2,128,128]{1,0,2:T(2,128)} %get-tuple-element.430), channel_id=1, source_target_pairs={{1,0},{2,1},{3,2},{5,4},{6,5},{7,6},{9,8},{10,9},{11,10},{13,12},{... | collective-permute-start | bytes 393224 | tf_op jit(solution)/shard_map/while/body/eval_jaxpr/ppermute | solution.py:18
  108.7 7.4 %collective-permute-start.2 = (f32[2,128,128]{1,0,2:T(2,128)}, f32[2,128,128]{1,0,2:T(2,128)S(1)}, u32[]{:S(2)}, u32[]{:S(2)}) collective-permute-start(f32[2,128,128]{1,0,2:T(2,128)} %get-tuple-element.431), channel_id=1, source_target_pairs={{1,0},{2,1},{3,2},{5,4},{6,5},{7,6},{9,8},{10,9},{11,10},{13,12},{... | collective-permute-start | bytes 393224 | tf_op jit(solution)/shard_map/while/body/eval_jaxpr/ppermute | solution.py:18
  110.0 7.1 %collective-permute-start.3 = (f32[2,128,128]{1,0,2:T(2,128)S(1)}, f32[2,128,128]{1,0,2:T(2,128)S(1)}, u32[]{:S(2)}, u32[]{:S(2)}) collective-permute-start(f32[2,128,128]{1,0,2:T(2,128)S(1)} %get-tuple-element.432), channel_id=1, source_target_pairs={{0,1},{1,2},{2,3},{4,5},{5,6},{6,7},{8,9},{9,10},{10,11},{12,13},{... | collective-permute-start | bytes 393224 | tf_op jit(solution)/shard_map/while/body/eval_jaxpr/ppermute | solution.py:17
  120.5 13.4 %collective-permute-start.4 = (f32[16,128,64]{1,0,2:T(8,128)}, f32[16,128,64]{1,0,2:T(8,128)}, u32[]{:S(2)}, u32[]{:S(2)}) collective-permute-start(f32[16,128,64]{1,0,2:T(8,128)} %constant_dynamic-slice_fusion.2), channel_id=1, source_target_pairs={{0,4},{4,0},{1,5},{5,1},{2,6},{6,2},{3,7},{7,3},{8,12},{12,8},{9,1... | collective-permute-start | bytes 1572872 | tf_op jit(solution)/shard_map/while/body/eval_jaxpr/ppermute | solution.py:26
  136.8 8.5 %collective-permute-start = (f32[2,128,128]{1,0,2:T(2,128)S(1)}, f32[2,128,128]{1,0,2:T(2,128)S(1)}, u32[]{:S(2)}, u32[]{:S(2)}) collective-permute-start(f32[2,128,128]{1,0,2:T(2,128)S(1)} %get-tuple-element.429), channel_id=1, source_target_pairs={{0,1},{1,2},{2,3},{4,5},{5,6},{6,7},{8,9},{9,10},{10,11},{12,13},{... | collective-permute-start | bytes 393224 | tf_op jit(solution)/shard_map/while/body/eval_jaxpr/ppermute | solution.py:17
  140.2 4.3 %collective-permute-start.1 = (f32[2,128,128]{1,0,2:T(2,128)}, f32[2,128,128]{1,0,2:T(2,128)S(1)}, u32[]{:S(2)}, u32[]{:S(2)}) collective-permute-start(f32[2,128,128]{1,0,2:T(2,128)} %get-tuple-element.430), channel_id=1, source_target_pairs={{1,0},{2,1},{3,2},{5,4},{6,5},{7,6},{9,8},{10,9},{11,10},{13,12},{... | collective-permute-start | bytes 393224 | tf_op jit(solution)/shard_map/while/body/eval_jaxpr/ppermute | solution.py:18
  150.3 7.4 %collective-permute-start.2 = (f32[2,128,128]{1,0,2:T(2,128)}, f32[2,128,128]{1,0,2:T(2,128)S(1)}, u32[]{:S(2)}, u32[]{:S(2)}) collective-permute-start(f32[2,128,128]{1,0,2:T(2,128)} %get-tuple-element.431), channel_id=1, source_target_pairs={{1,0},{2,1},{3,2},{5,4},{6,5},{7,6},{9,8},{10,9},{11,10},{13,12},{... | collective-permute-start | bytes 393224 | tf_op jit(solution)/shard_map/while/body/eval_jaxpr/ppermute | solution.py:18
  151.6 7.1 %collective-permute-start.3 = (f32[2,128,128]{1,0,2:T(2,128)S(1)}, f32[2,128,128]{1,0,2:T(2,128)S(1)}, u32[]{:S(2)}, u32[]{:S(2)}) collective-permute-start(f32[2,128,128]{1,0,2:T(2,128)S(1)} %get-tuple-element.432), channel_id=1, source_target_pairs={{0,1},{1,2},{2,3},{4,5},{5,6},{6,7},{8,9},{9,10},{10,11},{12,13},{... | collective-permute-start | bytes 393224 | tf_op jit(solution)/shard_map/while/body/eval_jaxpr/ppermute | solution.py:17
  162.2 13.4 %collective-permute-start.4 = (f32[16,128,64]{1,0,2:T(8,128)}, f32[16,128,64]{1,0,2:T(8,128)}, u32[]{:S(2)}, u32[]{:S(2)}) collective-permute-start(f32[16,128,64]{1,0,2:T(8,128)} %constant_dynamic-slice_fusion.2), channel_id=1, source_target_pairs={{0,4},{4,0},{1,5},{5,1},{2,6},{6,2},{3,7},{7,3},{8,12},{12,8},{9,1... | collective-permute-start | bytes 1572872 | tf_op jit(solution)/shard_map/while/body/eval_jaxpr/ppermute | solution.py:26
  178.4 8.5 %collective-permute-start = (f32[2,128,128]{1,0,2:T(2,128)S(1)}, f32[2,128,128]{1,0,2:T(2,128)S(1)}, u32[]{:S(2)}, u32[]{:S(2)}) collective-permute-start(f32[2,128,128]{1,0,2:T(2,128)S(1)} %get-tuple-element.429), channel_id=1, source_target_pairs={{0,1},{1,2},{2,3},{4,5},{5,6},{6,7},{8,9},{9,10},{10,11},{12,13},{... | collective-permute-start | bytes 393224 | tf_op jit(solution)/shard_map/while/body/eval_jaxpr/ppermute | solution.py:17
  181.8 4.3 %collective-permute-start.1 = (f32[2,128,128]{1,0,2:T(2,128)}, f32[2,128,128]{1,0,2:T(2,128)S(1)}, u32[]{:S(2)}, u32[]{:S(2)}) collective-permute-start(f32[2,128,128]{1,0,2:T(2,128)} %get-tuple-element.430), channel_id=1, source_target_pairs={{1,0},{2,1},{3,2},{5,4},{6,5},{7,6},{9,8},{10,9},{11,10},{13,12},{... | collective-permute-start | bytes 393224 | tf_op jit(solution)/shard_map/while/body/eval_jaxpr/ppermute | solution.py:18
  191.9 7.4 %collective-permute-start.2 = (f32[2,128,128]{1,0,2:T(2,128)}, f32[2,128,128]{1,0,2:T(2,128)S(1)}, u32[]{:S(2)}, u32[]{:S(2)}) collective-permute-start(f32[2,128,128]{1,0,2:T(2,128)} %get-tuple-element.431), channel_id=1, source_target_pairs={{1,0},{2,1},{3,2},{5,4},{6,5},{7,6},{9,8},{10,9},{11,10},{13,12},{... | collective-permute-start | bytes 393224 | tf_op jit(solution)/shard_map/while/body/eval_jaxpr/ppermute | solution.py:18
  193.2 7.1 %collective-permute-start.3 = (f32[2,128,128]{1,0,2:T(2,128)S(1)}, f32[2,128,128]{1,0,2:T(2,128)S(1)}, u32[]{:S(2)}, u32[]{:S(2)}) collective-permute-start(f32[2,128,128]{1,0,2:T(2,128)S(1)} %get-tuple-element.432), channel_id=1, source_target_pairs={{0,1},{1,2},{2,3},{4,5},{5,6},{6,7},{8,9},{9,10},{10,11},{12,13},{... | collective-permute-start | bytes 393224 | tf_op jit(solution)/shard_map/while/body/eval_jaxpr/ppermute | solution.py:17
  203.8 13.4 %collective-permute-start.4 = (f32[16,128,64]{1,0,2:T(8,128)}, f32[16,128,64]{1,0,2:T(8,128)}, u32[]{:S(2)}, u32[]{:S(2)}) collective-permute-start(f32[16,128,64]{1,0,2:T(8,128)} %constant_dynamic-slice_fusion.2), channel_id=1, source_target_pairs={{0,4},{4,0},{1,5},{5,1},{2,6},{6,2},{3,7},{7,3},{8,12},{12,8},{9,1... | collective-permute-start | bytes 1572872 | tf_op jit(solution)/shard_map/while/body/eval_jaxpr/ppermute | solution.py:26
  220.0 8.5 %collective-permute-start = (f32[2,128,128]{1,0,2:T(2,128)S(1)}, f32[2,128,128]{1,0,2:T(2,128)S(1)}, u32[]{:S(2)}, u32[]{:S(2)}) collective-permute-start(f32[2,128,128]{1,0,2:T(2,128)S(1)} %get-tuple-element.429), channel_id=1, source_target_pairs={{0,1},{1,2},{2,3},{4,5},{5,6},{6,7},{8,9},{9,10},{10,11},{12,13},{... | collective-permute-start | bytes 393224 | tf_op jit(solution)/shard_map/while/body/eval_jaxpr/ppermute | solution.py:17
  223.5 4.3 %collective-permute-start.1 = (f32[2,128,128]{1,0,2:T(2,128)}, f32[2,128,128]{1,0,2:T(2,128)S(1)}, u32[]{:S(2)}, u32[]{:S(2)}) collective-permute-start(f32[2,128,128]{1,0,2:T(2,128)} %get-tuple-element.430), channel_id=1, source_target_pairs={{1,0},{2,1},{3,2},{5,4},{6,5},{7,6},{9,8},{10,9},{11,10},{13,12},{... | collective-permute-start | bytes 393224 | tf_op jit(solution)/shard_map/while/body/eval_jaxpr/ppermute | solution.py:18
  233.6 7.4 %collective-permute-start.2 = (f32[2,128,128]{1,0,2:T(2,128)}, f32[2,128,128]{1,0,2:T(2,128)S(1)}, u32[]{:S(2)}, u32[]{:S(2)}) collective-permute-start(f32[2,128,128]{1,0,2:T(2,128)} %get-tuple-element.431), channel_id=1, source_target_pairs={{1,0},{2,1},{3,2},{5,4},{6,5},{7,6},{9,8},{10,9},{11,10},{13,12},{... | collective-permute-start | bytes 393224 | tf_op jit(solution)/shard_map/while/body/eval_jaxpr/ppermute | solution.py:18
  234.8 7.1 %collective-permute-start.3 = (f32[2,128,128]{1,0,2:T(2,128)S(1)}, f32[2,128,128]{1,0,2:T(2,128)S(1)}, u32[]{:S(2)}, u32[]{:S(2)}) collective-permute-start(f32[2,128,128]{1,0,2:T(2,128)S(1)} %get-tuple-element.432), channel_id=1, source_target_pairs={{0,1},{1,2},{2,3},{4,5},{5,6},{6,7},{8,9},{9,10},{10,11},{12,13},{... | collective-permute-start | bytes 393224 | tf_op jit(solution)/shard_map/while/body/eval_jaxpr/ppermute | solution.py:17
  245.4 13.4 %collective-permute-start.4 = (f32[16,128,64]{1,0,2:T(8,128)}, f32[16,128,64]{1,0,2:T(8,128)}, u32[]{:S(2)}, u32[]{:S(2)}) collective-permute-start(f32[16,128,64]{1,0,2:T(8,128)} %constant_dynamic-slice_fusion.2), channel_id=1, source_target_pairs={{0,4},{4,0},{1,5},{5,1},{2,6},{6,2},{3,7},{7,3},{8,12},{12,8},{9,1... | collective-permute-start | bytes 1572872 | tf_op jit(solution)/shard_map/while/body/eval_jaxpr/ppermute | solution.py:26
Sparse Core Ops, SparseCore 0:
  263.6 29.7 reduce-scatter.1
where the time goes:
time: 304 us; the launch traced here: 302 us
  waiting for transfers between devices  119 us (39%)
  starting transfers between devices  80.7 us (27%)
  other arithmetic  55.7 us (18%)
  local copies, waits for them, and re-layouts  32.4 us (11%)
  between operations  13.4 us (4%)
    ppermute x6, waiting for transfers between devices, partner_2(): return lax.ppermute(value, axis, pairs)  71.1 us
    ppermute x12, starting transfers between devices, extended_2(): before = lax.ppermute(last, axis, up)  56.1 us
    add x12, other arithmetic, advance(): advanced = 2.0 * current - earlier + courant * laplacian(extended, current)  33.6 us
    reduce_scatter x1, waiting for transfers between devices, on_device(): return lax.psum_scatter(scaled, 'shot', scatter_dimension=1, tiled=True)  30 us
    ppermute x12, starting transfers between devices, extended_2(): after = lax.ppermute(first, axis, down)  15.4 us
    ppermute x12, waiting for transfers between devices, extended_2(): after = lax.ppermute(first, axis, down)  12.5 us
    add x6, other arithmetic, one_round(): return (earlier, current, imaging + kept * partner)  12.4 us
    ppermute x6, starting transfers between devices, partner_2(): return lax.ppermute(value, axis, pairs)  9.17 us
  transfers between devices with their start and end apart: 31, of which 19 were waited for; matrix products, arithmetic and copies ran while one was open for 4% of the time, Pallas kernels for 0%

commit v1 on v0

v1 whole, which is shorter than its diff:
```python
import functools

import jax
import jax.numpy as jnp
from jax import lax
from jax.experimental import pallas as pl
from jax.experimental.pallas import tpu as pltpu
from jax.sharding import PartitionSpec as P

STEPS = 12
IMAGE_EVERY = 2
GROUP = 4
F32 = jnp.float32
VM = pl.BlockSpec(memory_space=pltpu.VMEM)
SM = pl.BlockSpec(memory_space=pltpu.SMEM)
LIMIT = 56 << 20
HC = 6
DEPTH = 8
TPAD = 16


def sds(*shape):
    return jax.ShapeDtypeStruct(shape, F32)


def call(kernel, outs, scratch, *args, flops=1, name=None):
    moved = sum(4 * a.size for a in args) + sum(4 * o.size for o in outs)
    return pl.pallas_call(
        kernel,
        out_shape=outs,
        in_specs=[SM] + [VM] * (len(args) - 1),
        out_specs=[VM] * len(outs),
        scratch_shapes=scratch,
        compiler_params=pltpu.CompilerParams(vmem_limit_bytes=LIMIT),
        cost_estimate=pl.CostEstimate(flops=flops, bytes_accessed=moved, transcendentals=0),
        name=name,
    )(*args)


def ext_ref(planes, rows):
    return pltpu.VMEM((planes, rows // 8, 8, 128), F32)


def fill_band(band):
    row = lax.broadcasted_iota(jnp.int32, (128, 128), 0)
    col = lax.broadcasted_iota(jnp.int32, (128, 128), 1)
    away = jnp.abs(row - col)
    taps = jnp.where(away == 0, -90.0, jnp.where(away == 1, 16.0, jnp.where(away == 2, -1.0, 0.0)))
    band[0:128] = taps.astype(jnp.bfloat16)
    band[128:256] = taps.astype(jnp.bfloat16)


def load(dst, at, src, x, base, width):
    for j in range(width):
        dst[at, j] = src[x, pl.ds(base + j, 8, stride=width), :]


def store(dst, at, src, x, width):
    for j in range(width):
        dst[at, pl.ds(j, 8, stride=width), :] = src[x, j]


def sweep(field, coef, band, first, count, c_first, put):
    width = field.shape[1]
    sub = lax.broadcasted_iota(jnp.int32, (8, 128), 0)
    top, bottom = sub < 1, sub >= 7
    zero = jnp.zeros((8, 128), F32)

    @pl.loop(0, count, step=GROUP)
    def _(k):
        x = first + k
        flat = field[pl.ds(x, GROUP)].reshape(GROUP * width * 8, 128)
        high = flat.astype(jnp.bfloat16)
        rest = flat - high.astype(F32)
        middle = rest.astype(jnp.bfloat16)
        low = (rest - middle.astype(F32)).astype(jnp.bfloat16)
        lanes = jnp.dot(
            jnp.concatenate([high, middle], 1), band[...], preferred_element_type=F32
        ) + jnp.dot(low, band[0:128], preferred_element_type=F32)
        for p in range(GROUP):
            own = [field[x + p, j] for j in range(width)]
            rows = (
                [jnp.where(top, zero, pltpu.roll(own[width - 2], 1, 0)),
                 jnp.where(top, zero, pltpu.roll(own[width - 1], 1, 0))]
                + own
                + [jnp.where(bottom, zero, pltpu.roll(own[0], 7, 0)),
                   jnp.where(bottom, zero, pltpu.roll(own[1], 7, 0))]
            )
            for j in range(width):
                near = (field[x + p - 1, j] + field[x + p + 1, j]) + (rows[j + 1] + rows[j + 3])
                far = (field[x + p - 2, j] + field[x + p + 2, j]) + (rows[j] + rows[j + 4])
                at = (p * width + j) * 8
                total = 16.0 * near - far + lanes[at : at + 8]
                v = own[j]
                put(k + p, j, (v + v) + coef[c_first + k + p, j] * total)


def pulse(rec, x, tick, flag):
    sub = lax.broadcasted_iota(jnp.int32, (8, 128), 0)
    row = rec[x, pl.ds(tick, 1), :] * flag
    return jnp.where(sub < 1, jnp.broadcast_to(row, (8, 128)), 0.0)


def turn(dst, src, planes, scale=None):
    @pl.loop(0, planes)
    def _(x):
        value = src[x].T
        dst[x] = value if scale is None else value * scale


def prepare_now(ids, now, nowt, give):
    n = now.shape[0]
    turn(nowt, now, n)
    start = pl.multiple_of((1 - ids[1]) * (128 - give.shape[1]), 8)

    @pl.loop(0, n)
    def _(x):
        give[x] = nowt[x, pl.ds(start, give.shape[1]), :]


def prepare_rest(ids, old, coef, rec, nowt, oldt, coeft, send_a, send_b):
    n = old.shape[0]
    turn(oldt, old, n)
    turn(coeft, coef, n, 1.0 / 12.0)
    odd = ids[0]

    def pack(send, high):
        def tail(h):
            return jnp.where(high, n - h, 0)

        for k in range(4):
            send[k] = nowt[tail(4) + k]
        for k in range(2):
            send[4 + k] = oldt[tail(2) + k]
        for k in range(HC):
            send[6 + k] = coeft[tail(HC) + k]
        for k in range(HC):
            send[6 + HC, TPAD * k : TPAD * (k + 1), :] = rec[tail(HC) + k]

    pack(send_a, odd == 0)
    pack(send_b, odd == 1)


def place(odd, n, halo, depth):
    after, before = halo + n, halo - depth
    return jnp.where(odd == 0, after, before), jnp.where(odd == 0, before, after)


def first_block(ids, nowt, oldt, coeft, rec, got_a, got_b,
                give, one, was, cfull, rfull, send_a, send_b,
                cur, old, mid, new, cx, band):
    n = nowt.shape[0]
    odd, role = ids[0], ids[1]
    flag = role.astype(F32)
    rows = one.shape[1]
    base = pl.multiple_of(role * (128 - rows), 8)
    other = pl.multiple_of((1 - role) * (128 - rows), 8)
    fill_band(band)

    @pl.loop(0, n)
    def _(x):
        load(cur, x + 4, nowt, x, 0, 16)
        load(old, x + 2, oldt, x, 0, 16)
        load(cx, x + 2, coeft, x, 0, 16)
        was[x + 4] = nowt[x, pl.ds(base, rows), :]
        cfull[x + HC] = coeft[x, pl.ds(base, rows), :]
        rfull[x + HC] = rec[x]

    a4, b4 = place(odd, n, 4, 4)
    a2, b2 = place(odd, n, 2, 2)
    ac, bc = place(odd, n, HC, HC)
    for got, at4, at2, atc, before in ((got_a, a4, a2, ac, odd == 1), (got_b, b4, b2, bc, odd == 0)):
        near_c = 6 + jnp.where(before, HC - 2, 0)
        for k in range(4):
            load(cur, at4 + k, got, k, 0, 16)
            was[at4 + k] = got[k, pl.ds(base, rows), :]
        for k in range(2):
            load(old, at2 + k, got, 4 + k, 0, 16)
            load(cx, at2 + k, got, near_c + k, 0, 16)
        for k in range(HC):
            cfull[atc + k] = got[6 + k, pl.ds(base, rows), :]
            rfull[atc + k] = got[6 + HC, TPAD * k : TPAD * (k + 1), :]

    def put0(x, j, value):
        value = value - old[x, j]
        if j == 0:
            value = value + pulse(rfull, x + HC - 2, 0, flag)
        mid[x, j] = value

    sweep(cur, cx, band, 2, n + 4, 0, put0)

    def put1(x, j, value):
        value = value - cur[x + 4, j]
        if j == 0:
            value = value + pulse(rfull, x + HC, 1, flag)
        new[x, j] = value

    sweep(mid, cx, band, 2, n, 2, put1)

    @pl.loop(0, n)
    def _(x):
        store(nowt, x, new, x, 16)
        one[x] = nowt[x, pl.ds(base, rows), :]
        give[x] = nowt[x, pl.ds(other, rows), :]

    pack_ends(one, send_a, send_b, odd, role)


def pack_ends(field, send_a, send_b, odd, role):
    n = field.shape[0]
    depth, rows = send_a.shape[0], send_a.shape[1]
    base = pl.multiple_of(role * (field.shape[1] - rows), 8)
    high = n - depth
    for send, start in ((send_a, jnp.where(odd == 0, high, 0)), (send_b, jnp.where(odd == 0, 0, high))):

        @pl.loop(0, depth)
        def _(k):
            send[k] = field[start + k, pl.ds(base, rows), :]


def block(rows, steps, tick, lit, fresh, last, shots, ids, *refs):
    it = iter(refs)
    take = lambda count: [next(it) for _ in range(count)]
    u, got_a, got_b, was = take(4)
    was_a, was_b = take(2) if fresh else (None, None)
    cfull, rfull = take(2)
    mates = take(steps) if lit else []
    first_mate = take(1)[0] if lit and fresh else None
    image_in = take(1)[0] if lit and not fresh else None
    inner = take(1)[0] if steps == 2 else None
    out = take(1)[0] if not (lit and last) else None
    send_a, send_b = take(2) if not last else (None, None)
    image = take(1)[0] if lit and not last else None
    pieces = take(shots) if lit and last else []
    cur, old, mid, cx, band = take(5)
    if lit and last:
        out, image = take(2)

    odd, role = ids[0], ids[1]
    n = u.shape[0]
    width = rows // 8
    halo = 4 * steps
    flag = (1 - role).astype(F32)
    fill_band(band)

    def window(ref):
        return pl.multiple_of(role * (ref.shape[1] - rows), 8)

    reach_old = halo - 4
    if fresh:
        @pl.loop(0, n)
        def _(x):
            load(old, x + reach_old, was, x, window(was), width)

        old_a, old_b = place(odd, n, reach_old, reach_old)

        @pl.loop(0, reach_old)
        def _(k):
            load(old, old_a + k, was_a, k, window(was_a), width)
            load(old, old_b + k, was_b, k, window(was_b), width)
    else:
        shift = (was.shape[0] - n) // 2 - reach_old

        @pl.loop(0, n + 2 * reach_old)
        def _(x):
            load(old, x, was, x + shift, window(was), width)

    @pl.loop(0, n + 2 * (halo - 2))
    def _(x):
        load(cx, x, cfull, x + HC - (halo - 2), window(cfull), width)

    @pl.loop(0, n)
    def _(x):
        load(cur, x + halo, u, x, window(u), width)

    at_a, at_b = place(odd, n, halo, halo)

    @pl.loop(0, halo)
    def _(k):
        load(cur, at_a + k, got_a, k, 0, width)
        load(cur, at_b + k, got_b, k, 0, width)

    now, before = cur, old
    results = []
    for s in range(steps):
        reach = halo - 4 * s
        time = tick + 2 * s

        def put_mid(x, j, value):
            if lit and j == 0:
                value = value + pulse(rfull, x + HC - (reach - 2), time + 1, flag)
            mid[x, j] = value

        sweep(now, cx, band, 2, n + 2 * (reach - 2), halo - reach, put_mid)

        def put_new(x, j, value):
            keep = now[x + 4, j]
            value = value - (keep + keep) - before[x, j]
            if lit and j == 0:
                at = x + HC - (reach - 4)
                value = value + (pulse(rfull, at, time, flag) + pulse(rfull, at, time + 2, flag))
            before[x, j] = value

        sweep(mid, cx, band, 2, n + 2 * (reach - 4), halo - reach + 2, put_new)
        results.append(before)
        if s < steps - 1:
            now, before = before, now.at[pl.ds(8, n + 2 * (reach - 8))]

    if steps == 2:
        @pl.loop(0, n + 8)
        def _(x):
            store(inner, x, results[0], x, width)

    @pl.loop(0, n)
    def _(x):
        store(out, x, results[-1], x, width)

    if not last:
        pack_ends(out, send_a, send_b, odd, role)

    if lit:
        half, pairs = 64, n // 2
        mine = ([inner] if steps == 2 else []) + [out]

        @pl.loop(0, pairs)
        def _(k):
            for side in range(2):
                x = k + side * pairs

                def part(ref, extra):
                    start = pl.multiple_of(role * (ref.shape[1] - half), 8)
                    return ref[x + extra, pl.ds(start, half), :]

                total = None
                for field, mate in zip(mine, mates):
                    product = part(field, (field.shape[0] - n) // 2) * part(mate, (mate.shape[0] - n) // 2)
                    total = product if total is None else total + product
                if fresh:
                    total = total + part(u, 0) * part(first_mate, 0)
                else:
                    total = total + image_in[k, side * half : (side + 1) * half, :]
                image[k, side * half : (side + 1) * half, :] = total

        if last:
            piece = 128 // shots
            weight = IMAGE_EVERY / STEPS

            @pl.loop(0, pairs)
            def _(k):
                image[k] = image[k].T * weight
                for index in range(shots):
                    target = jnp.bitwise_xor(ids[2], index)
                    pieces[index][k] = image[k, pl.ds(pl.multiple_of(target * piece, 8), piece), :]


def combine(count, ids, *refs):
    out = refs[count]
    pairs = refs[0].shape[0]

    @pl.loop(0, pairs)
    def _(k):
        total = refs[0][k]
        for index in range(1, count):
            total = total + refs[index][k]
        out[k] = total[:, :64]
        out[k + pairs] = pltpu.roll(total, 64, 1)[:, :64]


def on_device(states, courant, records):
    states, records = states[0, 0], records[0]
    n = courant.shape[0]
    shots, spaces = lax.axis_size("shot"), lax.axis_size("space")
    role, place_x = lax.axis_index("pair"), lax.axis_index("space")
    odd = place_x % 2
    ids = jnp.stack([odd, role, lax.axis_index("shot")]).astype(jnp.int32)
    rec = jnp.pad(jnp.swapaxes(records, 0, 1), ((0, 0), (0, TPAD - STEPS), (0, 0)))

    pairs_a = [(i, i ^ 1) for i in range(spaces)]
    pairs_b = [(i, i + 1) for i in range(1, spaces - 1, 2)]
    pairs_b = pairs_b + [(j, i) for i, j in pairs_b]

    def swap(send_a, send_b):
        got_b = lax.ppermute(send_b, "space", pairs_b)
        return lax.ppermute(send_a, "space", pairs_a), got_b

    def across(value):
        return lax.ppermute(value, "pair", [(0, 1), (1, 0)])

    def ends(value, depth):
        low, high = value[:depth], value[n - depth :]
        high_first = odd == 0
        return jnp.where(high_first, high, low), jnp.where(high_first, low, high)

    wide, mid_rows, thin = 88, 80, 72
    band = pltpu.VMEM((256, 128), jnp.bfloat16)

    nowt, give_now = call(
        prepare_now, (sds(n, 128, 128), sds(n, wide, 128)), [], ids, states[1], name="prepare_now"
    )
    other_was = across(give_now)
    oldt, coeft, send_a, send_b = call(
        prepare_rest,
        (sds(n, 128, 128), sds(n, 128, 128), sds(7 + HC, 128, 128), sds(7 + HC, 128, 128)),
        [], ids, states[0], courant, rec, nowt, name="prepare_rest",
    )
    got_a, got_b = swap(send_a, send_b)
    give_one, one, was, cfull, rfull, send_a, send_b = call(
        first_block,
        (sds(n, wide, 128), sds(n, wide, 128), sds(n + 8, wide, 128), sds(n + 2 * HC, wide, 128),
         sds(n + 2 * HC, TPAD, 128), sds(DEPTH, wide, 128), sds(DEPTH, wide, 128)),
        [ext_ref(n + 8, 128), ext_ref(n + 4, 128), ext_ref(n + 4, 128), ext_ref(n, 128), ext_ref(n + 4, 128), band],
        ids, nowt, oldt, coeft, rec, got_a, got_b, name="first_block",
    )
    other_one = across(give_one)

    def run(rows, steps, tick, lit, fresh, last, depth, *args):
        outs = []
        if steps == 2:
            outs.append(sds(n + 8, rows, 128))
        if not (lit and last):
            outs.append(sds(n, rows, 128))
        if not last:
            outs += [sds(depth, rows - 8, 128)] * 2
        if lit:
            outs += [sds(n // 2, 128 // shots, 128)] * shots if last else [sds(n // 2, 128, 128)]
        halo = 4 * steps
        scratch = [ext_ref(n + 2 * halo, rows), ext_ref(n + 2 * (halo - 4), rows), ext_ref(n + 2 * (halo - 2), rows),
                   ext_ref(n + 2 * (halo - 2), rows), band]
        if lit and last:
            scratch += [pltpu.VMEM((n, rows, 128), F32), pltpu.VMEM((n // 2, 128, 128), F32)]
        kernel = functools.partial(block, rows, steps, tick, lit, fresh, last, shots)
        return call(kernel, tuple(outs), scratch, ids, *args, name=f"{'other' if lit else 'own'}_{tick}")

    got = swap(send_a, send_b)
    three, five, send_a, send_b = run(wide, 2, 1, False, False, False, 8, one, *got, was, cfull, rfull)
    got = swap(send_a, send_b)
    seven, nine, send_a, send_b = run(mid_rows, 2, 5, False, False, False, 4, five, *got, three, cfull, rfull)
    got = swap(send_a, send_b)
    (eleven,) = run(thin, 1, 9, False, False, True, 0, nine, *got, seven, cfull, rfull)

    got_was = swap(*ends(other_was, 4))
    got = swap(*ends(other_one, 8))
    o_three, o_five, send_a, send_b, image = run(
        wide, 2, 1, True, True, False, 8, other_one, *got, other_was, *got_was, cfull, rfull, three, five, one)
    got = swap(send_a, send_b)
    o_seven, o_nine, send_a, send_b, image = run(
        mid_rows, 2, 5, True, False, False, 4, o_five, *got, o_three, cfull, rfull, seven, nine, image)
    got = swap(send_a, send_b)
    pieces = run(thin, 1, 9, True, False, True, 0, o_nine, *got, o_seven, cfull, rfull, eleven, image)

    arrived = [pieces[0]]
    for index in range(1, shots):
        arrived.append(lax.ppermute(pieces[index], "shot", [(i, i ^ index) for i in range(shots)]))
    (result,) = call(
        functools.partial(combine, shots), (sds(n, 128 // shots, 64),), [], ids, *arrived, name="combine"
    )
    return result


def solution(mesh):
    placed = (
        P("shot", "pair", None, "space", None, None),
        P("space", None, None),
        P("shot", None, "space", None),
    )
    return jax.shard_map(
        on_device, mesh=mesh, in_specs=placed, out_specs=P("space", "shot", "pair"), check_vma=False
    )
```

time: 304 us -> 152 us (0.50)
  waiting for transfers between devices: 119 us -> 10.5 us
  Pallas kernels: 0 us -> 73.1 us
  other arithmetic: 55.7 us -> 0.67 us
  starting transfers between devices: 80.7 us -> 53.1 us
  local copies, waits for them, and re-layouts: 32.4 us -> 11.7 us
  between operations: 13.4 us -> 0.32 us
    ppermute x30 -> x21, waiting for transfers between devices: 89.4 us -> 10.5 us  [the longest x3 8.91 us: on_device(): lax.ppermute(pieces[index], 'shot', [(i, i ^ index) for i in range(shots)])]
    pallas_call x0 -> x10, Pallas kernels: none -> 73.1 us  [call(): pl.pallas_call(kernel, out_shape=outs, in_specs=[SM] + [VM] * (len(args)...]
    add x18 -> x0, other arithmetic: 46 us -> none  [the longest x12 33.6 us: advance(): advanced = 2.0 * current - earlier + courant * laplacian(extended, current)]
    reduce_scatter x1 -> x0, waiting for transfers between devices: 30 us -> none  [on_device(): return lax.psum_scatter(scaled, 'shot', scatter_dimension=1, tiled=True)]
    ppermute x30 -> x21, starting transfers between devices: 80.7 us -> 53.1 us  [the longest x8 40.1 us: swap(): return (lax.ppermute(send_a, 'space', pairs_a), got_b)]
    slice x13 -> x0, local copies, waits for them, and re-layouts: 10.7 us -> none  [the longest x6 4.48 us: extended_2(): last = lax.slice_in_dim(array, length - width, length, axis=dim)]
    scatter-add x12 -> x0, other arithmetic: 8.49 us -> none  [advance(): advanced = advanced.at[:, :, 0].add(inject * record)]
    while x6 -> x0, local copies, waits for them, and re-layouts: 6.56 us -> none
  transfers between devices with their start and end apart: 31 -> 21, of which waited for: 19 -> 4; matrix products, arithmetic and copies ran while one was open for 4% -> 0% of each run, Pallas kernels for 0% -> 29%
where the time goes in v1:
time: 152 us; the launch traced here: 149 us
  Pallas kernels  73.1 us (48%)
  starting transfers between devices  53.1 us (35%)
  local copies, waits for them, and re-layouts  11.7 us (8%)
  waiting for transfers between devices  10.5 us (7%)
    pallas_call x10, Pallas kernels, call(): pl.pallas_call(kernel, out_shape=outs, in_specs=[SM] + [VM] * (len(args)...  73.1 us
    ppermute x8, starting transfers between devices, swap(): return (lax.ppermute(send_a, 'space', pairs_a), got_b)  40.1 us
    ppermute x3, waiting for transfers between devices, on_device(): lax.ppermute(pieces[index], 'shot', [(i, i ^ index) for i in range(shots)])  8.91 us
    unnamed x47, local copies, waits for them, and re-layouts  7.86 us
    ppermute x8, starting transfers between devices, swap(): got_b = lax.ppermute(send_b, 'space', pairs_b)  5.36 us
    ppermute x3, starting transfers between devices, on_device(): lax.ppermute(pieces[index], 'shot', [(i, i ^ index) for i in range(shots)])  4.58 us
    squeeze x1, local copies, waits for them, and re-layouts, on_device(): states[0]  3.14 us
    ppermute x2, starting transfers between devices, across(): return lax.ppermute(value, 'pair', [(0, 1), (1, 0)])  3.07 us
  transfers between devices with their start and end apart: 21, of which 4 were waited for; matrix products, arithmetic and copies ran while one was open for 0% of the time, Pallas kernels for 29%

profile of v1, /device:TPU:0, one launch (start us, length us, event | category | flops | bytes accessed | tf_op | source)
XLA Modules:
  0.0 149.3 jit_solution(4082014366658876660)
XLA Ops:
  0.0 3.1 %slice_bitcast_fusion = (f32[16,128,128]{2,1,0:T(8,128)}, f32[16,128,128]{2,1,0:T(8,128)}) fusion(f32[1,1,2,16,128,128]{5,4,3,2,1,0:T(8,128)} %param.3), kind=kLoop, calls=%fused_computation | loop fusion | bytes 4194304 | tf_op jit(solution)/shard_map/squeeze | solution.py:404
  3.2 0.6 pad_add_fusion.ids
  3.8 4.3 %prepare_now.1 = (f32[16,128,128]{2,1,0:T(8,128)}, f32[16,88,128]{2,1,0:T(8,128)}) custom-call(s32[3]{0:T(128)} %pad_add_fusion.ids, f32[16,128,128]{2,1,0:T(8,128)} %get-tuple-element.76.now), custom_call_target="tpu_custom_call" | custom-call | flops 1 | bytes 2818060 | tf_op jit(solution)/shard_map/prepare_now/pallas_call | solution.py:28
  8.1 0.6 pad.4.rec
  8.7 7.0 %prepare_rest.1 = (f32[16,128,128]{2,1,0:T(8,128)}, f32[16,128,128]{2,1,0:T(8,128)}, f32[13,128,128]{2,1,0:T(8,128)}, f32[13,128,128]{2,1,0:T(8,128)}) custom-call(s32[3]{0:T(128)} %pad_add_fusion.ids, f32[16,128,128]{2,1,0:T(8,128)} %get-tuple-element.75.old, f32[16,128,128]{2,1,0:T(8,128)} %coef.1, f32[16,16,128]{2,1,0:T(8,128)} %pad.4.rec, ...), custom_call_target="tpu_custom_call" | custom-call | flops 1 | bytes 7077900 | tf_op jit(solution)/shard_map/prepare_rest/pallas_call | solution.py:28
  15.8 0.5 collective-permute-start
  16.2 0.7 collective-permute-start.1
  17.0 1.5 %collective-permute-done.got_a = f32[13,128,128]{2,1,0:T(8,128)S(1)} collective-permute-done((f32[13,128,128]{2,1,0:T(8,128)}, f32[13,128,128]{2,1,0:T(8,128)S(1)}, u32[]{:S(2)}, u32[]{:S(2)}) %collective-permute-start) | collective-permute-done | bytes 852000 | tf_op jit(solution)/shard_map/ppermute | solution.py:384
  18.5 0.9 copy-done.2
  19.4 0.3 copy-done.3
  19.6 9.1 %first_block.1 = (f32[16,88,128]{2,1,0:T(8,128)}, f32[16,88,128]{2,1,0:T(8,128)}, f32[24,88,128]{2,1,0:T(8,128)}, f32[28,88,128]{2,1,0:T(8,128)}, f32[28,16,128]...) custom-call(s32[3]{0:T(128)} %pad_add_fusion.ids, f32[16,128,128]{2,1,0:T(8,128)} %get-tuple-element.40.nowt, ...), custom_call_target="tpu_custom_call" | custom-call | flops 1 | bytes 9715724 | tf_op jit(solution)/shard_map/first_block/pallas_call | solution.py:28
  28.7 3.0 %collective-permute-start.2 = (f32[16,88,128]{2,1,0:T(8,128)}, f32[16,88,128]{2,1,0:T(8,128)S(1)}, u32[]{:S(2)}, u32[]{:S(2)}) collective-permute-start(f32[16,88,128]{2,1,0:T(8,128)} %get-tuple-element.45), channel_id=1, source_target_pairs={{0,4},{4,0},{1,5},{5,1},{2,6},{6,2},{3,7},{7,3},{8,12},{12,8},{9,1... | collective-permute-start | bytes 2162696 | tf_op jit(solution)/shard_map/ppermute | solution.py:387
  31.8 11.6 %collective-permute-start.8 = (f32[8,88,128]{2,1,0:T(8,128)}, f32[8,88,128]{2,1,0:T(8,128)S(1)}, u32[]{:S(2)}, u32[]{:S(2)}) collective-permute-start(f32[8,88,128]{2,1,0:T(8,128)} %get-tuple-element.50), channel_id=1, source_target_pairs={{0,1},{1,0},{2,3},{3,2},{4,5},{5,4},{6,7},{7,6},{8,9},{9,8},{10,11... | collective-permute-start | bytes 1081352 | tf_op jit(solution)/shard_map/ppermute | solution.py:384
  43.4 0.7 collective-permute-start.9
  44.1 12.5 %collective-permute-start.3 = (f32[8,88,128]{2,1,0:T(8,128)S(1)}, f32[8,88,128]{2,1,0:T(8,128)S(1)}, u32[]{:S(2)}, u32[]{:S(2)}) collective-permute-start(f32[8,88,128]{2,1,0:T(8,128)S(1)} %get-tuple-element.80), channel_id=1, source_target_pairs={{0,1},{1,0},{2,3},{3,2},{4,5},{5,4},{6,7},{7,6},{8,9},{9,8},{10,11... | collective-permute-start | bytes 1081352 | tf_op jit(solution)/shard_map/ppermute | solution.py:384
  56.6 0.7 collective-permute-start.4
  57.3 7.0 %collective-permute-start.6 = (f32[4,88,128]{2,1,0:T(8,128)S(1)}, f32[4,88,128]{2,1,0:T(8,128)S(1)}, u32[]{:S(2)}, u32[]{:S(2)}) collective-permute-start(f32[4,88,128]{2,1,0:T(8,128)S(1)} %get-tuple-element.78), channel_id=1, source_target_pairs={{0,1},{1,0},{2,3},{3,2},{4,5},{5,4},{6,7},{7,6},{8,9},{9,8},{10,11... | collective-permute-start | bytes 540680 | tf_op jit(solution)/shard_map/ppermute | solution.py:384
  64.3 0.7 collective-permute-start.7
  65.0 0.7 copy-done.5
  65.7 9.3 %own_1.1 = (f32[24,88,128]{2,1,0:T(8,128)}, f32[16,88,128]{2,1,0:T(8,128)}, f32[8,80,128]{2,1,0:T(8,128)}, f32[8,80,128]{2,1,0:T(8,128)}) custom-call(s32[3]{0:T(128)} %pad_add_fusion.ids, f32[16,88,128]{2,1,0:T(8,128)} %get-tuple-element.49.refs_0_.refs_10_, f32[8,88,128]{2,1,0:T(8,128)} %copy-done.4, f32[8,88,128]{2,1,0:T(8,128)} %copy-done.5, ...), custom_call_target="tpu_custom_call" | custom-call | flops 1 | bytes 6471692 | tf_op jit(solution)/shard_map/own_1/pallas_call | solution.py:28
  75.0 2.7 %collective-permute-start.12 = (f32[8,80,128]{2,1,0:T(8,128)}, f32[8,80,128]{2,1,0:T(8,128)S(1)}, u32[]{:S(2)}, u32[]{:S(2)}) collective-permute-start(f32[8,80,128]{2,1,0:T(8,128)} %get-tuple-element.59), channel_id=1, source_target_pairs={{0,1},{1,0},{2,3},{3,2},{4,5},{5,4},{6,7},{7,6},{8,9},{9,8},{10,11... | collective-permute-start | bytes 983048 | tf_op jit(solution)/shard_map/ppermute | solution.py:384
  77.7 0.7 collective-permute-start.13
  78.5 0.6 copy-done.13
  79.2 0.2 copy-done.7
  79.4 10.5 %other_1.1 = (f32[24,88,128]{2,1,0:T(8,128)}, f32[16,88,128]{2,1,0:T(8,128)}, f32[8,80,128]{2,1,0:T(8,128)}, f32[8,80,128]{2,1,0:T(8,128)}, f32[8,128,128]{2,1,0:T(8,128)}) custom-call(s32[3]{0:T(128)} %pad_add_fusion.ids, f32[16,88,128]{2,1,0:T(8,128)} %copy-done, f32[8,88,128]{2,1,0:T(8,128)} %copy-done.6, f32[8,88,128]{2,1,0:T(8,128)} %copy-done.7, ...), custom_call_target="tpu_custom_call" | custom-call | flops 1 | bytes 9519116 | tf_op jit(solution)/shard_map/other_1/pallas_call | solution.py:28
  89.9 1.7 %collective-permute-start.10 = (f32[8,80,128]{2,1,0:T(8,128)}, f32[8,80,128]{2,1,0:T(8,128)S(1)}, u32[]{:S(2)}, u32[]{:S(2)}) collective-permute-start(f32[8,80,128]{2,1,0:T(8,128)} %get-tuple-element.56), channel_id=1, source_target_pairs={{0,1},{1,0},{2,3},{3,2},{4,5},{5,4},{6,7},{7,6},{8,9},{9,8},{10,11... | collective-permute-start | bytes 983048 | tf_op jit(solution)/shard_map/ppermute | solution.py:384
  91.6 0.7 collective-permute-start.11
  92.3 0.7 copy-done.8
  93.0 0.7 copy-done.9
  93.7 8.9 %own_5.1 = (f32[24,80,128]{2,1,0:T(8,128)}, f32[16,80,128]{2,1,0:T(8,128)}, f32[4,72,128]{2,1,0:T(8,128)}, f32[4,72,128]{2,1,0:T(8,128)}) custom-call(s32[3]{0:T(128)} %pad_add_fusion.ids, f32[16,88,128]{2,1,0:T(8,128)} %get-tuple-element.54.refs_9_.refs_0_, f32[8,80,128]{2,1,0:T(8,128)} %copy-done.8, f32[8,80,128]{2,1,0:T(8,128)} %copy-done.9, ...), custom_call_target="tpu_custom_call" | custom-call | flops 1 | bytes 5881868 | tf_op jit(solution)/shard_map/own_5/pallas_call | solution.py:28
  102.7 2.6 %collective-permute-start.16 = (f32[4,72,128]{2,1,0:T(8,128)}, f32[4,72,128]{2,1,0:T(8,128)S(1)}, u32[]{:S(2)}, u32[]{:S(2)}) collective-permute-start(f32[4,72,128]{2,1,0:T(8,128)} %get-tuple-element.68), channel_id=1, source_target_pairs={{0,1},{1,0},{2,3},{3,2},{4,5},{5,4},{6,7},{7,6},{8,9},{9,8},{10,11... | collective-permute-start | bytes 442376 | tf_op jit(solution)/shard_map/ppermute | solution.py:384
  105.2 0.7 collective-permute-start.17
  105.9 0.7 copy-done.10
  106.8 9.9 %other_5.1 = (f32[24,80,128]{2,1,0:T(8,128)}, f32[16,80,128]{2,1,0:T(8,128)}, f32[4,72,128]{2,1,0:T(8,128)}, f32[4,72,128]{2,1,0:T(8,128)}, f32[8,128,128]{2,1,0:T(8,128)}) custom-call(s32[3]{0:T(128)} %pad_add_fusion.ids, f32[16,88,128]{2,1,0:T(8,128)} %get-tuple-element.55.refs_0_, f32[8,80,128]{2,1,0:T(8,128)} %copy-done.10, f32[8,80,128]{2,1,0:T(8,128)} %copy-done.11, ...), custom_call_target="tpu_custom_call" | custom-call | flops 1 | bytes 8568844 | tf_op jit(solution)/shard_map/other_5/pallas_call | solution.py:28
  116.6 1.7 %collective-permute-start.14 = (f32[4,72,128]{2,1,0:T(8,128)}, f32[4,72,128]{2,1,0:T(8,128)S(1)}, u32[]{:S(2)}, u32[]{:S(2)}) collective-permute-start(f32[4,72,128]{2,1,0:T(8,128)} %get-tuple-element.65), channel_id=1, source_target_pairs={{0,1},{1,0},{2,3},{3,2},{4,5},{5,4},{6,7},{7,6},{8,9},{9,8},{10,11... | collective-permute-start | bytes 442376 | tf_op jit(solution)/shard_map/ppermute | solution.py:384
  118.3 0.7 collective-permute-start.15
  119.0 0.6 copy-done.14
  119.6 0.7 copy-done.15
  120.3 5.2 %own_9.1.refs_6_ = f32[16,72,128]{2,1,0:T(8,128)} custom-call(s32[3]{0:T(128)} %pad_add_fusion.ids, f32[16,80,128]{2,1,0:T(8,128)} %get-tuple-element.62.refs_7_.refs_0_, f32[4,72,128]{2,1,0:T(8,128)} %copy-done.14, f32[4,72,128]{2,1,0:T(8,128)} %copy-done.15, f32[24,80,128]{2,1,0:T(8,128)} %get-tuple-element.61.refs_6_.refs_3_, ...), custom_call_target="tpu_custom_call" | custom-call | flops 1 | bytes 4014092 | tf_op jit(solution)/shard_map/own_9/pallas_call | solution.py:28
  125.5 0.7 copy-done.16
  126.2 6.5 %other_9.1 = (f32[8,32,128]{2,1,0:T(8,128)}, f32[8,32,128]{2,1,0:T(8,128)}, f32[8,32,128]{2,1,0:T(8,128)}, f32[8,32,128]{2,1,0:T(8,128)}) custom-call(s32[3]{0:T(128)} %pad_add_fusion.ids, f32[16,80,128]{2,1,0:T(8,128)} %get-tuple-element.64.refs_0_, f32[4,72,128]{2,1,0:T(8,128)} %copy-done.16, f32[4,72,128]{2,1,0:T(8,128)} %copy-done.17, ...), custom_call_target="tpu_custom_call" | custom-call | flops 1 | bytes 5062668 | tf_op jit(solution)/shard_map/other_9/pallas_call | solution.py:28
  132.7 2.0 %collective-permute-start.18 = (f32[8,32,128]{2,1,0:T(8,128)}, f32[8,32,128]{2,1,0:T(8,128)S(1)}, u32[]{:S(2)}, u32[]{:S(2)}) collective-permute-start(f32[8,32,128]{2,1,0:T(8,128)} %get-tuple-element.72), channel_id=1, source_target_pairs={{0,8},{8,0},{16,24},{24,16},{1,9},{9,1},{17,25},{25,17},{2,10},{10... | collective-permute-start | bytes 393224 | tf_op jit(solution)/shard_map/ppermute | solution.py:453
  134.7 2.6 %collective-permute-start.19 = (f32[8,32,128]{2,1,0:T(8,128)}, f32[8,32,128]{2,1,0:T(8,128)S(1)}, u32[]{:S(2)}, u32[]{:S(2)}) collective-permute-start(f32[8,32,128]{2,1,0:T(8,128)} %get-tuple-element.73), channel_id=1, source_target_pairs={{0,16},{8,24},{16,0},{24,8},{1,17},{9,25},{17,1},{25,9},{2,18},{10... | collective-permute-start | bytes 393224 | tf_op jit(solution)/shard_map/ppermute | solution.py:453
  137.3 0.6 collective-permute-done.18.refs_1_
  137.9 4.1 %collective-permute-done.19.refs_2_ = f32[8,32,128]{2,1,0:T(8,128)S(1)} collective-permute-done((f32[8,32,128]{2,1,0:T(8,128)}, f32[8,32,128]{2,1,0:T(8,128)S(1)}, u32[]{:S(2)}, u32[]{:S(2)}) %collective-permute-start.19) | collective-permute-done | bytes 131104 | tf_op jit(solution)/shard_map/ppermute | solution.py:453
  142.0 4.2 %collective-permute-done.20.refs_3_ = f32[8,32,128]{2,1,0:T(8,128)S(1)} collective-permute-done((f32[8,32,128]{2,1,0:T(8,128)}, f32[8,32,128]{2,1,0:T(8,128)S(1)}, u32[]{:S(2)}, u32[]{:S(2)}) %collective-permute-start.20) | collective-permute-done | bytes 131104 | tf_op jit(solution)/shard_map/ppermute | solution.py:453
  146.2 0.6 copy-done.20
  146.9 2.4 %combine.1 = f32[16,32,64]{2,1,0:T(8,128)} custom-call(s32[3]{0:T(128)} %pad_add_fusion.ids, f32[8,32,128]{2,1,0:T(8,128)} %get-tuple-element.71.refs_0_, f32[8,32,128]{2,1,0:T(8,128)} %copy-done.18, f32[8,32,128]{2,1,0:T(8,128)} %copy-done.19, f32[8,32,128]{2,1,0:T(8,128)} %copy-done.20), custom_call_target="tpu_custom_call" | custom-call | flops 1 | bytes 655372 | tf_op jit(solution)/shard_map/combine/pallas_call | solution.py:28
  (56 shorter events, 0.7 us)
Async XLA Ops:
  0.0 3.1 %copy-start.21 = (f32[1,12,16,128]{3,2,1,0:T(8,128)S(1)}, f32[1,12,16,128]{3,2,1,0:T(8,128)}, u32[]{:S(2)}) copy-start(f32[1,12,16,128]{3,2,1,0:T(8,128)} %param.5) | copy-start | bytes 294916
  15.8 2.7 %collective-permute-start = (f32[13,128,128]{2,1,0:T(8,128)}, f32[13,128,128]{2,1,0:T(8,128)S(1)}, u32[]{:S(2)}, u32[]{:S(2)}) collective-permute-start(f32[13,128,128]{2,1,0:T(8,128)} %get-tuple-element.43), channel_id=1, source_target_pairs={{0,1},{1,0},{2,3},{3,2},{4,5},{5,4},{6,7},{7,6},{8,9},{9,8},{10,11... | collective-permute-start | bytes 2555912 | tf_op jit(solution)/shard_map/ppermute | solution.py:384
  16.2 2.2 %collective-permute-start.1 = (f32[13,128,128]{2,1,0:T(8,128)}, f32[13,128,128]{2,1,0:T(8,128)S(1)}, u32[]{:S(2)}, u32[]{:S(2)}) collective-permute-start(f32[13,128,128]{2,1,0:T(8,128)} %get-tuple-element.44), channel_id=1, source_target_pairs={{1,2},{2,1},{5,6},{6,5},{9,10},{10,9},{13,14},{14,13},{17,18},{18,... | collective-permute-start | bytes 2555912 | tf_op jit(solution)/shard_map/ppermute | solution.py:383
  18.5 0.9 copy-start.2
  18.5 1.2 copy-start.3
  19.6 12.1 %copy-start.22 = (f32[16,88,128]{2,1,0:T(8,128)S(1)}, f32[16,88,128]{2,1,0:T(8,128)}, u32[]{:S(2)}) copy-start(f32[16,88,128]{2,1,0:T(8,128)} %get-tuple-element.46) | copy-start | bytes 2162692
  28.7 15.3 %collective-permute-start.2 = (f32[16,88,128]{2,1,0:T(8,128)}, f32[16,88,128]{2,1,0:T(8,128)S(1)}, u32[]{:S(2)}, u32[]{:S(2)}) collective-permute-start(f32[16,88,128]{2,1,0:T(8,128)} %get-tuple-element.45), channel_id=1, source_target_pairs={{0,4},{4,0},{1,5},{5,1},{2,6},{6,2},{3,7},{7,3},{8,12},{12,8},{9,1... | collective-permute-start | bytes 2162696 | tf_op jit(solution)/shard_map/ppermute | solution.py:387
  31.7 25.5 %collective-permute-start.5 = (f32[16,88,128]{2,1,0:T(8,128)S(1)}, f32[16,88,128]{2,1,0:T(8,128)S(1)}, u32[]{:S(2)}, u32[]{:S(2)}) collective-permute-start(f32[16,88,128]{2,1,0:T(8,128)S(1)} %copy-done.22), channel_id=1, source_target_pairs={{0,4},{4,0},{1,5},{5,1},{2,6},{6,2},{3,7},{7,3},{8,12},{12,8},{9,1... | collective-permute-start | bytes 2162696 | tf_op jit(solution)/shard_map/ppermute | solution.py:387
  31.8 32.5 %collective-permute-start.8 = (f32[8,88,128]{2,1,0:T(8,128)}, f32[8,88,128]{2,1,0:T(8,128)S(1)}, u32[]{:S(2)}, u32[]{:S(2)}) collective-permute-start(f32[8,88,128]{2,1,0:T(8,128)} %get-tuple-element.50), channel_id=1, source_target_pairs={{0,1},{1,0},{2,3},{3,2},{4,5},{5,4},{6,7},{7,6},{8,9},{9,8},{10,11... | collective-permute-start | bytes 1081352 | tf_op jit(solution)/shard_map/ppermute | solution.py:384
  43.4 21.6 %collective-permute-start.9 = (f32[8,88,128]{2,1,0:T(8,128)}, f32[8,88,128]{2,1,0:T(8,128)S(1)}, u32[]{:S(2)}, u32[]{:S(2)}) collective-permute-start(f32[8,88,128]{2,1,0:T(8,128)} %get-tuple-element.51), channel_id=1, source_target_pairs={{1,2},{2,1},{5,6},{6,5},{9,10},{10,9},{13,14},{14,13},{17,18},{18,... | collective-permute-start | bytes 1081352 | tf_op jit(solution)/shard_map/ppermute | solution.py:383
  44.1 31.0 %copy-start = (f32[16,88,128]{2,1,0:T(8,128)}, f32[16,88,128]{2,1,0:T(8,128)S(1)}, u32[]{:S(2)}) copy-start(f32[16,88,128]{2,1,0:T(8,128)S(1)} %collective-permute-done.2.refs_0_) | copy-start | bytes 2162692
  44.1 34.3 %collective-permute-start.3 = (f32[8,88,128]{2,1,0:T(8,128)S(1)}, f32[8,88,128]{2,1,0:T(8,128)S(1)}, u32[]{:S(2)}, u32[]{:S(2)}) collective-permute-start(f32[8,88,128]{2,1,0:T(8,128)S(1)} %get-tuple-element.80), channel_id=1, source_target_pairs={{0,1},{1,0},{2,3},{3,2},{4,5},{5,4},{6,7},{7,6},{8,9},{9,8},{10,11... | collective-permute-start | bytes 1081352 | tf_op jit(solution)/shard_map/ppermute | solution.py:384
  56.6 21.8 %collective-permute-start.4 = (f32[8,88,128]{2,1,0:T(8,128)S(1)}, f32[8,88,128]{2,1,0:T(8,128)S(1)}, u32[]{:S(2)}, u32[]{:S(2)}) collective-permute-start(f32[8,88,128]{2,1,0:T(8,128)S(1)} %get-tuple-element.79), channel_id=1, source_target_pairs={{1,2},{2,1},{5,6},{6,5},{9,10},{10,9},{13,14},{14,13},{17,18},{18,... | collective-permute-start | bytes 1081352 | tf_op jit(solution)/shard_map/ppermute | solution.py:383
  57.3 17.8 %copy-start.1 = (f32[16,88,128]{2,1,0:T(8,128)}, f32[16,88,128]{2,1,0:T(8,128)S(1)}, u32[]{:S(2)}) copy-start(f32[16,88,128]{2,1,0:T(8,128)S(1)} %collective-permute-done.5.refs_3_) | copy-start | bytes 2162692
  57.3 20.4 %collective-permute-start.6 = (f32[4,88,128]{2,1,0:T(8,128)S(1)}, f32[4,88,128]{2,1,0:T(8,128)S(1)}, u32[]{:S(2)}, u32[]{:S(2)}) collective-permute-start(f32[4,88,128]{2,1,0:T(8,128)S(1)} %get-tuple-element.78), channel_id=1, source_target_pairs={{0,1},{1,0},{2,3},{3,2},{4,5},{5,4},{6,7},{7,6},{8,9},{9,8},{10,11... | collective-permute-start | bytes 540680 | tf_op jit(solution)/shard_map/ppermute | solution.py:384
  64.3 0.7 copy-start.4
  64.3 14.1 %collective-permute-start.7 = (f32[4,88,128]{2,1,0:T(8,128)S(1)}, f32[4,88,128]{2,1,0:T(8,128)S(1)}, u32[]{:S(2)}, u32[]{:S(2)}) collective-permute-start(f32[4,88,128]{2,1,0:T(8,128)S(1)} %get-tuple-element.77), channel_id=1, source_target_pairs={{1,2},{2,1},{5,6},{6,5},{9,10},{10,9},{13,14},{14,13},{17,18},{18,... | collective-permute-start | bytes 540680 | tf_op jit(solution)/shard_map/ppermute | solution.py:383
  65.0 0.7 copy-start.5
  75.0 17.2 %collective-permute-start.12 = (f32[8,80,128]{2,1,0:T(8,128)}, f32[8,80,128]{2,1,0:T(8,128)S(1)}, u32[]{:S(2)}, u32[]{:S(2)}) collective-permute-start(f32[8,80,128]{2,1,0:T(8,128)} %get-tuple-element.59), channel_id=1, source_target_pairs={{0,1},{1,0},{2,3},{3,2},{4,5},{5,4},{6,7},{7,6},{8,9},{9,8},{10,11... | collective-permute-start | bytes 983048 | tf_op jit(solution)/shard_map/ppermute | solution.py:384
  77.7 0.7 copy-start.12
  77.7 14.6 %collective-permute-start.13 = (f32[8,80,128]{2,1,0:T(8,128)}, f32[8,80,128]{2,1,0:T(8,128)S(1)}, u32[]{:S(2)}, u32[]{:S(2)}) collective-permute-start(f32[8,80,128]{2,1,0:T(8,128)} %get-tuple-element.60), channel_id=1, source_target_pairs={{1,2},{2,1},{5,6},{6,5},{9,10},{10,9},{13,14},{14,13},{17,18},{18,... | collective-permute-start | bytes 983048 | tf_op jit(solution)/shard_map/ppermute | solution.py:383
  78.4 0.7 copy-start.13
  78.4 0.8 copy-start.6
  78.4 0.9 copy-start.7
  89.9 16.0 %collective-permute-start.10 = (f32[8,80,128]{2,1,0:T(8,128)}, f32[8,80,128]{2,1,0:T(8,128)S(1)}, u32[]{:S(2)}, u32[]{:S(2)}) collective-permute-start(f32[8,80,128]{2,1,0:T(8,128)} %get-tuple-element.56), channel_id=1, source_target_pairs={{0,1},{1,0},{2,3},{3,2},{4,5},{5,4},{6,7},{7,6},{8,9},{9,8},{10,11... | collective-permute-start | bytes 983048 | tf_op jit(solution)/shard_map/ppermute | solution.py:384
  91.6 14.3 %collective-permute-start.11 = (f32[8,80,128]{2,1,0:T(8,128)}, f32[8,80,128]{2,1,0:T(8,128)S(1)}, u32[]{:S(2)}, u32[]{:S(2)}) collective-permute-start(f32[8,80,128]{2,1,0:T(8,128)} %get-tuple-element.57), channel_id=1, source_target_pairs={{1,2},{2,1},{5,6},{6,5},{9,10},{10,9},{13,14},{14,13},{17,18},{18,... | collective-permute-start | bytes 983048 | tf_op jit(solution)/shard_map/ppermute | solution.py:383
  92.3 0.7 copy-start.8
  93.0 0.7 copy-start.9
  102.7 16.3 %collective-permute-start.16 = (f32[4,72,128]{2,1,0:T(8,128)}, f32[4,72,128]{2,1,0:T(8,128)S(1)}, u32[]{:S(2)}, u32[]{:S(2)}) collective-permute-start(f32[4,72,128]{2,1,0:T(8,128)} %get-tuple-element.68), channel_id=1, source_target_pairs={{0,1},{1,0},{2,3},{3,2},{4,5},{5,4},{6,7},{7,6},{8,9},{9,8},{10,11... | collective-permute-start | bytes 442376 | tf_op jit(solution)/shard_map/ppermute | solution.py:384
  105.2 13.8 %collective-permute-start.17 = (f32[4,72,128]{2,1,0:T(8,128)}, f32[4,72,128]{2,1,0:T(8,128)S(1)}, u32[]{:S(2)}, u32[]{:S(2)}) collective-permute-start(f32[4,72,128]{2,1,0:T(8,128)} %get-tuple-element.69), channel_id=1, source_target_pairs={{1,2},{2,1},{5,6},{6,5},{9,10},{10,9},{13,14},{14,13},{17,18},{18,... | collective-permute-start | bytes 442376 | tf_op jit(solution)/shard_map/ppermute | solution.py:383
  105.9 0.8 copy-start.10
  105.9 0.9 copy-start.11
  116.6 8.8 %collective-permute-start.14 = (f32[4,72,128]{2,1,0:T(8,128)}, f32[4,72,128]{2,1,0:T(8,128)S(1)}, u32[]{:S(2)}, u32[]{:S(2)}) collective-permute-start(f32[4,72,128]{2,1,0:T(8,128)} %get-tuple-element.65), channel_id=1, source_target_pairs={{0,1},{1,0},{2,3},{3,2},{4,5},{5,4},{6,7},{7,6},{8,9},{9,8},{10,11... | collective-permute-start | bytes 442376 | tf_op jit(solution)/shard_map/ppermute | solution.py:384
  118.3 7.2 %collective-permute-start.15 = (f32[4,72,128]{2,1,0:T(8,128)}, f32[4,72,128]{2,1,0:T(8,128)S(1)}, u32[]{:S(2)}, u32[]{:S(2)}) collective-permute-start(f32[4,72,128]{2,1,0:T(8,128)} %get-tuple-element.66), channel_id=1, source_target_pairs={{1,2},{2,1},{5,6},{6,5},{9,10},{10,9},{13,14},{14,13},{17,18},{18,... | collective-permute-start | bytes 442376 | tf_op jit(solution)/shard_map/ppermute | solution.py:383
  119.0 0.7 copy-start.14
  119.6 0.7 copy-start.15
  125.5 0.7 copy-start.16
  125.5 0.7 copy-start.17
  132.7 5.2 %collective-permute-start.18 = (f32[8,32,128]{2,1,0:T(8,128)}, f32[8,32,128]{2,1,0:T(8,128)S(1)}, u32[]{:S(2)}, u32[]{:S(2)}) collective-permute-start(f32[8,32,128]{2,1,0:T(8,128)} %get-tuple-element.72), channel_id=1, source_target_pairs={{0,8},{8,0},{16,24},{24,16},{1,9},{9,1},{17,25},{25,17},{2,10},{10... | collective-permute-start | bytes 393224 | tf_op jit(solution)/shard_map/ppermute | solution.py:453
  134.7 7.3 %collective-permute-start.19 = (f32[8,32,128]{2,1,0:T(8,128)}, f32[8,32,128]{2,1,0:T(8,128)S(1)}, u32[]{:S(2)}, u32[]{:S(2)}) collective-permute-start(f32[8,32,128]{2,1,0:T(8,128)} %get-tuple-element.73), channel_id=1, source_target_pairs={{0,16},{8,24},{16,0},{24,8},{1,17},{9,25},{17,1},{25,9},{2,18},{10... | collective-permute-start | bytes 393224 | tf_op jit(solution)/shard_map/ppermute | solution.py:453
  137.3 8.9 %collective-permute-start.20 = (f32[8,32,128]{2,1,0:T(8,128)}, f32[8,32,128]{2,1,0:T(8,128)S(1)}, u32[]{:S(2)}, u32[]{:S(2)}) collective-permute-start(f32[8,32,128]{2,1,0:T(8,128)} %get-tuple-element.74), channel_id=1, source_target_pairs={{0,24},{8,16},{16,8},{24,0},{1,25},{9,17},{17,9},{25,1},{2,26},{10... | collective-permute-start | bytes 393224 | tf_op jit(solution)/shard_map/ppermute | solution.py:453
  137.9 8.3 %copy-start.18 = (f32[8,32,128]{2,1,0:T(8,128)}, f32[8,32,128]{2,1,0:T(8,128)S(1)}, u32[]{:S(2)}) copy-start(f32[8,32,128]{2,1,0:T(8,128)S(1)} %collective-permute-done.18.refs_1_) | copy-start | bytes 393220
  142.0 4.2 %copy-start.19 = (f32[8,32,128]{2,1,0:T(8,128)}, f32[8,32,128]{2,1,0:T(8,128)S(1)}, u32[]{:S(2)}) copy-start(f32[8,32,128]{2,1,0:T(8,128)S(1)} %collective-permute-done.19.refs_2_) | copy-start | bytes 393220
  146.2 0.7 copy-start.20

commit v2 on v1

--- a/solution.py
+++ b/solution.py
@@ -7,23 +7,23 @@
 from jax.experimental.pallas import tpu as pltpu
 from jax.sharding import PartitionSpec as P
 
+
 STEPS = 12
 IMAGE_EVERY = 2
 GROUP = 4
 F32 = jnp.float32
 VM = pl.BlockSpec(memory_space=pltpu.VMEM)
 SM = pl.BlockSpec(memory_space=pltpu.SMEM)
-LIMIT = 56 << 20
 HC = 6
 DEPTH = 8
-TPAD = 16
+HR = 8
 
 
 def sds(*shape):
     return jax.ShapeDtypeStruct(shape, F32)
 
 
-def call(kernel, outs, scratch, *args, flops=1, name=None):
+def call(kernel, outs, scratch, *args, limit=8, flops=1):
     moved = sum(4 * a.size for a in args) + sum(4 * o.size for o in outs)
     return pl.pallas_call(
         kernel,
@@ -31,9 +31,8 @@
         in_specs=[SM] + [VM] * (len(args) - 1),
         out_specs=[VM] * len(outs),
         scratch_shapes=scratch,
-        compiler_params=pltpu.CompilerParams(vmem_limit_bytes=LIMIT),
+        compiler_params=pltpu.CompilerParams(vmem_limit_bytes=limit << 20),
         cost_estimate=pl.CostEstimate(flops=flops, bytes_accessed=moved, transcendentals=0),
-        name=name,
     )(*args)
 
 
@@ -97,48 +96,42 @@
 
 def pulse(rec, x, tick, flag):
     sub = lax.broadcasted_iota(jnp.int32, (8, 128), 0)
-    row = rec[x, pl.ds(tick, 1), :] * flag
+    row = rec[tick, pl.ds(x, 1), :] * flag
     return jnp.where(sub < 1, jnp.broadcast_to(row, (8, 128)), 0.0)
 
 
-def turn(dst, src, planes, scale=None):
-    @pl.loop(0, planes)
-    def _(x):
-        value = src[x].T
-        dst[x] = value if scale is None else value * scale
+def pack(ids, states, courant, rec, send_a, send_b, sems):
+    n = courant.shape[0]
+    copies = []
+    for index, (send, high) in enumerate(((send_a, ids[0] == 0), (send_b, ids[0] == 1))):
+        at = lambda h: jnp.where(high, n - h, 0)
+        moves = [
+            (states.at[0, 0, 1, pl.ds(at(4), 4)], send.at[pl.ds(0, 4)]),
+            (states.at[0, 0, 0, pl.ds(at(2), 2)], send.at[pl.ds(4, 2)]),
+            (courant.at[pl.ds(at(HC), HC)], send.at[pl.ds(6, HC)]),
+        ]
+        first = pl.multiple_of(at(HR), HR)
+        for k in range(STEPS):
+            send[6 + HC, HR * k : HR * (k + 1), :] = rec[0, k, pl.ds(first, HR), :]
+        for k, (source, target) in enumerate(moves):
+            copy = pltpu.make_async_copy(source, target, sems.at[index, k])
+            copy.start()
+            copies.append(copy)
+    for copy in copies:
+        copy.wait()
 
 
 def prepare_now(ids, now, nowt, give):
-    n = now.shape[0]
-    turn(nowt, now, n)
     start = pl.multiple_of((1 - ids[1]) * (128 - give.shape[1]), 8)
-
-    @pl.loop(0, n)
-    def _(x):
-        give[x] = nowt[x, pl.ds(start, give.shape[1]), :]
-
-
-def prepare_rest(ids, old, coef, rec, nowt, oldt, coeft, send_a, send_b):
-    n = old.shape[0]
-    turn(oldt, old, n)
-    turn(coeft, coef, n, 1.0 / 12.0)
-    odd = ids[0]
-
-    def pack(send, high):
-        def tail(h):
-            return jnp.where(high, n - h, 0)
-
-        for k in range(4):
-            send[k] = nowt[tail(4) + k]
-        for k in range(2):
-            send[4 + k] = oldt[tail(2) + k]
-        for k in range(HC):
-            send[6 + k] = coeft[tail(HC) + k]
-        for k in range(HC):
-            send[6 + HC, TPAD * k : TPAD * (k + 1), :] = rec[tail(HC) + k]
-
-    pack(send_a, odd == 0)
-    pack(send_b, odd == 1)
+    for k in range(GROUP):
+        nowt[k] = now[0, 0, 0, k].T
+        give[k] = nowt[k, pl.ds(start, give.shape[1]), :]
+
+
+def prepare_rest(ids, old, coef, oldt, coeft):
+    for k in range(GROUP):
+        oldt[k] = old[0, 0, 0, k].T
+        coeft[k] = coef[k].T * (1.0 / 12.0)
 
 
 def place(odd, n, halo, depth):
@@ -147,8 +140,8 @@
 
 
 def first_block(ids, nowt, oldt, coeft, rec, got_a, got_b,
-                give, one, was, cfull, rfull, send_a, send_b,
-                cur, old, mid, new, cx, band):
+                give, one, was_a, was_b, cfull, rfull, send_a, send_b,
+                cur, old, mid, new, cx, band, raw_a, raw_b, plain):
     n = nowt.shape[0]
     odd, role = ids[0], ids[1]
     flag = role.astype(F32)
@@ -162,29 +155,38 @@
         load(cur, x + 4, nowt, x, 0, 16)
         load(old, x + 2, oldt, x, 0, 16)
         load(cx, x + 2, coeft, x, 0, 16)
-        was[x + 4] = nowt[x, pl.ds(base, rows), :]
         cfull[x + HC] = coeft[x, pl.ds(base, rows), :]
-        rfull[x + HC] = rec[x]
+
+    a_rec, b_rec = place(odd, n, HR, HR)
+    for k in range(STEPS):
+        rfull[k, HR : HR + n, :] = rec[0, k]
+        for got, at in ((got_a, a_rec), (got_b, b_rec)):
+            rfull[k, pl.ds(pl.multiple_of(at, HR), HR), :] = got[6 + HC, HR * k : HR * (k + 1), :]
 
     a4, b4 = place(odd, n, 4, 4)
     a2, b2 = place(odd, n, 2, 2)
     ac, bc = place(odd, n, HC, HC)
-    for got, at4, at2, atc, before in ((got_a, a4, a2, ac, odd == 1), (got_b, b4, b2, bc, odd == 0)):
+    for raw, turned, was in ((got_a, raw_a, was_a), (got_b, raw_b, was_b)):
+        for k in range(6 + HC):
+            value = raw[k].T
+            if k < 4:
+                was[k] = value
+            turned[k] = value if k < 6 else value * (1.0 / 12.0)
+
+    for got, at4, at2, atc, before in ((raw_a, a4, a2, ac, odd == 1), (raw_b, b4, b2, bc, odd == 0)):
         near_c = 6 + jnp.where(before, HC - 2, 0)
         for k in range(4):
             load(cur, at4 + k, got, k, 0, 16)
-            was[at4 + k] = got[k, pl.ds(base, rows), :]
         for k in range(2):
             load(old, at2 + k, got, 4 + k, 0, 16)
             load(cx, at2 + k, got, near_c + k, 0, 16)
         for k in range(HC):
             cfull[atc + k] = got[6 + k, pl.ds(base, rows), :]
-            rfull[atc + k] = got[6 + HC, TPAD * k : TPAD * (k + 1), :]
 
     def put0(x, j, value):
         value = value - old[x, j]
         if j == 0:
-            value = value + pulse(rfull, x + HC - 2, 0, flag)
+            value = value + pulse(rfull, x + HR - 2, 0, flag)
         mid[x, j] = value
 
     sweep(cur, cx, band, 2, n + 4, 0, put0)
@@ -192,16 +194,16 @@
     def put1(x, j, value):
         value = value - cur[x + 4, j]
         if j == 0:
-            value = value + pulse(rfull, x + HC, 1, flag)
+            value = value + pulse(rfull, x + HR, 1, flag)
         new[x, j] = value
 
     sweep(mid, cx, band, 2, n, 2, put1)
 
     @pl.loop(0, n)
     def _(x):
-        store(nowt, x, new, x, 16)
-        one[x] = nowt[x, pl.ds(base, rows), :]
-        give[x] = nowt[x, pl.ds(other, rows), :]
+        store(plain, x, new, x, 16)
+        one[x] = plain[x, pl.ds(base, rows), :]
+        give[x] = plain[x, pl.ds(other, rows), :]
 
     pack_ends(one, send_a, send_b, odd, role)
 
@@ -288,7 +290,7 @@
 
         def put_mid(x, j, value):
             if lit and j == 0:
-                value = value + pulse(rfull, x + HC - (reach - 2), time + 1, flag)
+                value = value + pulse(rfull, x + HR - (reach - 2), time + 1, flag)
             mid[x, j] = value
 
         sweep(now, cx, band, 2, n + 2 * (reach - 2), halo - reach, put_mid)
@@ -297,7 +299,7 @@
             keep = now[x + 4, j]
             value = value - (keep + keep) - before[x, j]
             if lit and j == 0:
-                at = x + HC - (reach - 4)
+                at = x + HR - (reach - 4)
                 value = value + (pulse(rfull, at, time, flag) + pulse(rfull, at, time + 2, flag))
             before[x, j] = value
 
@@ -367,13 +369,11 @@
 
 
 def on_device(states, courant, records):
-    states, records = states[0, 0], records[0]
     n = courant.shape[0]
     shots, spaces = lax.axis_size("shot"), lax.axis_size("space")
     role, place_x = lax.axis_index("pair"), lax.axis_index("space")
     odd = place_x % 2
     ids = jnp.stack([odd, role, lax.axis_index("shot")]).astype(jnp.int32)
-    rec = jnp.pad(jnp.swapaxes(records, 0, 1), ((0, 0), (0, TPAD - STEPS), (0, 0)))
 
     pairs_a = [(i, i ^ 1) for i in range(spaces)]
     pairs_b = [(i, i + 1) for i in range(1, spaces - 1, 2)]
@@ -393,23 +393,51 @@
 
     wide, mid_rows, thin = 88, 80, 72
     band = pltpu.VMEM((256, 128), jnp.bfloat16)
-
-    nowt, give_now = call(
-        prepare_now, (sds(n, 128, 128), sds(n, wide, 128)), [], ids, states[1], name="prepare_now"
-    )
+    hbm = pl.BlockSpec(memory_space=pltpu.HBM)
+
+    send_a, send_b = pl.pallas_call(
+        pack,
+        out_shape=(sds(7 + HC, 128, 128),) * 2,
+        in_specs=[SM, hbm, hbm, VM],
+        out_specs=[VM, VM],
+        scratch_shapes=[pltpu.SemaphoreType.DMA((2, 3))],
+        compiler_params=pltpu.CompilerParams(vmem_limit_bytes=58 << 20),
+        name="pack",
+    )(ids, states, courant, records)
+    got_a, got_b = swap(send_a, send_b)
+
+    def state_block(index):
+        return pl.BlockSpec((1, 1, 1, GROUP, 128, 128), lambda i: (0, 0, index, i, 0, 0))
+
+    def planes(rows):
+        return pl.BlockSpec((GROUP, rows, 128), lambda i: (i, 0, 0))
+
+    nowt, give_now = pl.pallas_call(
+        prepare_now,
+        grid=(n // GROUP,),
+        out_shape=(sds(n, 128, 128), sds(n, wide, 128)),
+        in_specs=[SM, state_block(1)],
+        out_specs=[planes(128), planes(wide)],
+        compiler_params=pltpu.CompilerParams(vmem_limit_bytes=6 << 20),
+        name="prepare_now",
+    )(ids, states)
     other_was = across(give_now)
-    oldt, coeft, send_a, send_b = call(
+    oldt, coeft = pl.pallas_call(
         prepare_rest,
-        (sds(n, 128, 128), sds(n, 128, 128), sds(7 + HC, 128, 128), sds(7 + HC, 128, 128)),
-        [], ids, states[0], courant, rec, nowt, name="prepare_rest",
-    )
-    got_a, got_b = swap(send_a, send_b)
-    give_one, one, was, cfull, rfull, send_a, send_b = call(
+        grid=(n // GROUP,),
+        out_shape=(sds(n, 128, 128), sds(n, 128, 128)),
+        in_specs=[SM, state_block(0), planes(128)],
+        out_specs=[planes(128), planes(128)],
+        compiler_params=pltpu.CompilerParams(vmem_limit_bytes=6 << 20),
+        name="prepare_rest",
+    )(ids, states, courant)
+    give_one, one, was_a, was_b, cfull, rfull, send_a, send_b = call(
         first_block,
-        (sds(n, wide, 128), sds(n, wide, 128), sds(n + 8, wide, 128), sds(n + 2 * HC, wide, 128),
-         sds(n + 2 * HC, TPAD, 128), sds(DEPTH, wide, 128), sds(DEPTH, wide, 128)),
-        [ext_ref(n + 8, 128), ext_ref(n + 4, 128), ext_ref(n + 4, 128), ext_ref(n, 128), ext_ref(n + 4, 128), band],
-        ids, nowt, oldt, coeft, rec, got_a, got_b, name="first_block",
+        (sds(n, wide, 128), sds(n, wide, 128), sds(4, 128, 128), sds(4, 128, 128), sds(n + 2 * HC, wide, 128),
+         sds(STEPS, n + 2 * HR, 128), sds(DEPTH, wide, 128), sds(DEPTH, wide, 128)),
+        [ext_ref(n + 8, 128), ext_ref(n + 4, 128), ext_ref(n + 4, 128), ext_ref(n, 128), ext_ref(n + 4, 128), band]
+        + [pltpu.VMEM((6 + HC, 128, 128), F32)] * 2 + [pltpu.VMEM((n, 128, 128), F32)],
+        ids, nowt, oldt, coeft, records, got_a, got_b, limit=12,
     )
     other_one = across(give_one)
 
@@ -429,10 +457,10 @@
         if lit and last:
             scratch += [pltpu.VMEM((n, rows, 128), F32), pltpu.VMEM((n // 2, 128, 128), F32)]
         kernel = functools.partial(block, rows, steps, tick, lit, fresh, last, shots)
-        return call(kernel, tuple(outs), scratch, ids, *args, name=f"{'other' if lit else 'own'}_{tick}")
+        return call(kernel, tuple(outs), scratch, ids, *args)
 
     got = swap(send_a, send_b)
-    three, five, send_a, send_b = run(wide, 2, 1, False, False, False, 8, one, *got, was, cfull, rfull)
+    three, five, send_a, send_b = run(wide, 2, 1, False, True, False, 8, one, *got, nowt, was_a, was_b, cfull, rfull)
     got = swap(send_a, send_b)
     seven, nine, send_a, send_b = run(mid_rows, 2, 5, False, False, False, 4, five, *got, three, cfull, rfull)
     got = swap(send_a, send_b)
@@ -451,9 +479,7 @@
     arrived = [pieces[0]]
     for index in range(1, shots):
         arrived.append(lax.ppermute(pieces[index], "shot", [(i, i ^ index) for i in range(shots)]))
-    (result,) = call(
-        functools.partial(combine, shots), (sds(n, 128 // shots, 64),), [], ids, *arrived, name="combine"
-    )
+    (result,) = call(functools.partial(combine, shots), (sds(n, 128 // shots, 64),), [], ids, *arrived)
     return result
 
 
@@ -463,6 +489,4 @@
         P("space", None, None),
         P("shot", None, "space", None),
     )
-    return jax.shard_map(
-        on_device, mesh=mesh, in_specs=placed, out_specs=P("space", "shot", "pair"), check_vma=False
-    )
+    return jax.shard_map(on_device, mesh=mesh, in_specs=placed, out_specs=P("space", "shot", "pair"), check_vma=False)

time: 152 us -> 119 us (0.78)
  the two profiles are of different devices: /device:TPU:0 before, /device:TPU:1 now
where the time goes in v2:
time: 119 us
  Pallas kernels  50 us (42%)
  starting transfers between devices  33.6 us (28%)
  waiting for transfers between devices  29.8 us (25%)
  other arithmetic  2.82 us (2%)
  local copies, waits for them, and re-layouts  2.2 us (2%)
    pallas_call x8, Pallas kernels, call(): pl.pallas_call(kernel, out_shape=outs, in_specs=[SM] + [VM] * (len(args)...  42.5 us
    ppermute x8, starting transfers between devices, swap(): got_b = lax.ppermute(send_b, 'space', pairs_b)  26.8 us
    ppermute x2, waiting for transfers between devices, across(): return lax.ppermute(value, 'pair', [(0, 1), (1, 0)])  14.1 us
    ppermute x3, waiting for transfers between devices, on_device(): lax.ppermute(pieces[index], 'shot', [(i, i ^ index) for i in range(shots)])  8.97 us
    ppermute x8, waiting for transfers between devices, swap(): got_b = lax.ppermute(send_b, 'space', pairs_b)  6.72 us
    ppermute x3, starting transfers between devices, on_device(): lax.ppermute(pieces[index], 'shot', [(i, i ^ index) for i in range(shots)])  4 us
    pallas_call x1, Pallas kernels, on_device(): pl.pallas_call(pack, out_shape=(sds(7 + HC, 128, 128),) * 2, in_specs=[SM...  3.67 us
    pallas_call x1, Pallas kernels, on_device(): pl.pallas_call(prepare_now, grid=(n // GROUP,), out_shape=(sds(n, 128, 12...  2.41 us
  transfers between devices with their start and end apart: 21, of which 5 were waited for; matrix products, arithmetic and copies ran while one was open for 2% of the time, Pallas kernels for 29%

profile of v2, /device:TPU:1, one launch (start us, length us, event | category | flops | bytes accessed | tf_op | source)
XLA Modules:
  0.0 118.7 jit_solution(11357651488038469610)
XLA Ops:
  0.0 0.6 pad_add_fusion.ids
  0.6 3.7 %pack.1 = (f32[13,128,128]{2,1,0:T(8,128)}, f32[13,128,128]{2,1,0:T(8,128)}) custom-call(s32[3]{0:T(128)} %pad_add_fusion.ids, f32[1,1,2,16,128,128]{5,4,3,2,1,0:T(8,128)} %states.1, f32[16,128,128]{2,1,0:T(8,128)} %courant.1, f32[1,12,16,128]{3,2,1,0:T(8,128)} %rec.3), custom_call_target="tpu_custom_call" | custom-call | tf_op jit(solution)/shard_map/pack/pallas_call | solution.py:398
  4.3 0.0 copy-start.1
  4.3 0.1 collective-permute-start
  4.4 4.6 %collective-permute-start.1 = (f32[13,128,128]{2,1,0:T(8,128)}, f32[13,128,128]{2,1,0:T(8,128)S(1)}, u32[]{:S(2)}, u32[]{:S(2)}) collective-permute-start(f32[13,128,128]{2,1,0:T(8,128)} %get-tuple-element.45), channel_id=1, source_target_pairs={{1,2},{2,1},{5,6},{6,5},{9,10},{10,9},{13,14},{14,13},{17,18},{18,... | collective-permute-start | bytes 2555912 | tf_op jit(solution)/shard_map/ppermute | solution.py:383
  9.1 2.4 %prepare_now.1 = (f32[16,128,128]{2,1,0:T(8,128)S(1)}, f32[16,88,128]{2,1,0:T(8,128)}) custom-call(s32[3]{0:T(128)S(1)} %copy-done.5, f32[1,1,2,16,128,128]{5,4,3,2,1,0:T(8,128)S(1)} %copy-done), custom_call_target="tpu_custom_call" | custom-call | tf_op jit(solution)/shard_map/prepare_now/pallas_call | solution.py:415
  11.5 1.4 %prepare_rest.1 = (f32[16,128,128]{2,1,0:T(8,128)S(1)}, f32[16,128,128]{2,1,0:T(8,128)S(1)}) custom-call(s32[3]{0:T(128)S(1)} %copy-done.5, f32[1,1,2,16,128,128]{5,4,3,2,1,0:T(8,128)S(1)} %copy-done, f32[16,128,128]{2,1,0:T(8,128)S(1)} %copy-done.1), custom_call_target="tpu_custom_call" | custom-call | tf_op jit(solution)/shard_map/prepare_rest/pallas_call | solution.py:425
  12.9 6.7 %collective-permute-done.1.got_b = f32[13,128,128]{2,1,0:T(8,128)S(1)} collective-permute-done((f32[13,128,128]{2,1,0:T(8,128)}, f32[13,128,128]{2,1,0:T(8,128)S(1)}, u32[]{:S(2)}, u32[]{:S(2)}) %collective-permute-start.1) | collective-permute-done | bytes 852000 | tf_op jit(solution)/shard_map/ppermute | solution.py:383
  19.6 6.4 %shard_map.37 = (f32[16,88,128]{2,1,0:T(8,128)}, f32[16,88,128]{2,1,0:T(8,128)S(1)}, f32[4,128,128]{2,1,0:T(8,128)S(1)}, f32[4,128,128]{2,1,0:T(8,128)S(1)}, f32...) custom-call(s32[3]{0:T(128)S(1)} %copy-done.5, ...), custom_call_target="tpu_custom_call" | custom-call | flops 1 | bytes 9093132 | tf_op jit(solution)/shard_map/pallas_call | solution.py:28
  26.1 0.7 copy-done.3
  26.8 0.7 copy-done.6
  27.5 0.7 copy-done.7
  28.2 1.8 %collective-permute-start.2 = (f32[16,88,128]{2,1,0:T(8,128)}, f32[16,88,128]{2,1,0:T(8,128)}, u32[]{:S(2)}, u32[]{:S(2)}) collective-permute-start(f32[16,88,128]{2,1,0:T(8,128)} %get-tuple-element.46), channel_id=1, source_target_pairs={{0,4},{4,0},{1,5},{5,1},{2,6},{6,2},{3,7},{7,3},{8,12},{12,8},{9,1... | collective-permute-start | bytes 2162696 | tf_op jit(solution)/shard_map/ppermute | solution.py:387
  30.0 0.0 collective-permute-start.5
  30.0 0.0 collective-permute-start.8
  30.0 4.0 %collective-permute-start.9 = (f32[8,88,128]{2,1,0:T(8,128)}, f32[8,88,128]{2,1,0:T(8,128)S(1)}, u32[]{:S(2)}, u32[]{:S(2)}) collective-permute-start(f32[8,88,128]{2,1,0:T(8,128)} %copy-done.6), channel_id=1, source_target_pairs={{1,2},{2,1},{5,6},{6,5},{9,10},{10,9},{13,14},{14,13},{17,18},{18,... | collective-permute-start | bytes 1081352 | tf_op jit(solution)/shard_map/ppermute | solution.py:383
  34.0 11.1 %collective-permute-done.2.refs_0_ = f32[16,88,128]{2,1,0:T(8,128)} collective-permute-done((f32[16,88,128]{2,1,0:T(8,128)}, f32[16,88,128]{2,1,0:T(8,128)}, u32[]{:S(2)}, u32[]{:S(2)}) %collective-permute-start.2) | collective-permute-done | bytes 720928 | tf_op jit(solution)/shard_map/ppermute | solution.py:387
  45.2 1.1 slice_select_fusion
  46.3 3.6 %collective-permute-start.4 = (f32[8,88,128]{2,1,0:T(8,128)S(1)}, f32[8,88,128]{2,1,0:T(8,128)S(1)}, u32[]{:S(2)}, u32[]{:S(2)}) collective-permute-start(f32[8,88,128]{2,1,0:T(8,128)S(1)} %get-tuple-element.79), channel_id=1, source_target_pairs={{1,2},{2,1},{5,6},{6,5},{9,10},{10,9},{13,14},{14,13},{17,18},{18,... | collective-permute-start | bytes 1081352 | tf_op jit(solution)/shard_map/ppermute | solution.py:383
  49.9 0.1 collective-permute-start.3
  49.9 2.9 %collective-permute-done.5.refs_3_ = f32[16,88,128]{2,1,0:T(8,128)} collective-permute-done((f32[16,88,128]{2,1,0:T(8,128)}, f32[16,88,128]{2,1,0:T(8,128)}, u32[]{:S(2)}, u32[]{:S(2)}) %collective-permute-start.5) | collective-permute-done | bytes 720928 | tf_op jit(solution)/shard_map/ppermute | solution.py:387
  52.9 1.0 slice_select_fusion.2
  53.9 3.6 %collective-permute-start.7 = (f32[4,88,128]{2,1,0:T(8,128)S(1)}, f32[4,88,128]{2,1,0:T(8,128)S(1)}, u32[]{:S(2)}, u32[]{:S(2)}) collective-permute-start(f32[4,88,128]{2,1,0:T(8,128)S(1)} %get-tuple-element.77), channel_id=1, source_target_pairs={{1,2},{2,1},{5,6},{6,5},{9,10},{10,9},{13,14},{14,13},{17,18},{18,... | collective-permute-start | bytes 540680 | tf_op jit(solution)/shard_map/ppermute | solution.py:383
  57.5 0.1 collective-permute-start.6
  57.6 0.0 collective-permute-done.9.refs_2_
  57.6 6.6 %shard_map.38 = (f32[24,88,128]{2,1,0:T(8,128)S(1)}, f32[16,88,128]{2,1,0:T(8,128)S(1)}, f32[8,80,128]{2,1,0:T(8,128)S(1)}, f32[8,80,128]{2,1,0:T(8,128)S(1)}) custom-call(s32[3]{0:T(128)S(1)} %copy-done.5, f32[16,88,128]{2,1,0:T(8,128)S(1)} %get-tuple-element.50.refs_0_.refs_10_, f32[8,88,128]{2,1,0:T(8,128)S(1)} %collective-permute-done.8.refs_1_, ...), custom_call_target="tpu_custom_call" | custom-call | flops 1 | bytes 6930444 | tf_op jit(solution)/shard_map/pallas_call | solution.py:28
  64.2 0.5 collective-permute-start.12
  64.8 2.0 %collective-permute-start.13 = (f32[8,80,128]{2,1,0:T(8,128)S(1)}, f32[8,80,128]{2,1,0:T(8,128)S(1)}, u32[]{:S(2)}, u32[]{:S(2)}) collective-permute-start(f32[8,80,128]{2,1,0:T(8,128)S(1)} %get-tuple-element.62), channel_id=1, source_target_pairs={{1,2},{2,1},{5,6},{6,5},{9,10},{10,9},{13,14},{14,13},{17,18},{18,... | collective-permute-start | bytes 983048 | tf_op jit(solution)/shard_map/ppermute | solution.py:383
  66.8 0.0 collective-permute-done.6.refs_4_
  66.8 0.0 collective-permute-done.4.refs_2_
  66.8 7.6 %shard_map.39 = (f32[24,88,128]{2,1,0:T(8,128)S(1)}, f32[16,88,128]{2,1,0:T(8,128)S(1)}, f32[8,80,128]{2,1,0:T(8,128)S(1)}, f32[8,80,128]{2,1,0:T(8,128)S(1)}, f32[8,128,128]{2,1,0:T(8,128)S(1)}) custom-call(s32[3]{0:T(128)S(1)} %copy-done.5, f32[16,88,128]{2,1,0:T(8,128)} %collective-permute-done.2.refs_0_, ...), custom_call_target="tpu_custom_call" | custom-call | flops 1 | bytes 9486348 | tf_op jit(solution)/shard_map/pallas_call | solution.py:28
  74.5 0.1 collective-permute-start.10
  74.5 3.5 %collective-permute-start.11 = (f32[8,80,128]{2,1,0:T(8,128)S(1)}, f32[8,80,128]{2,1,0:T(8,128)S(1)}, u32[]{:S(2)}, u32[]{:S(2)}) collective-permute-start(f32[8,80,128]{2,1,0:T(8,128)S(1)} %get-tuple-element.59), channel_id=1, source_target_pairs={{1,2},{2,1},{5,6},{6,5},{9,10},{10,9},{13,14},{14,13},{17,18},{18,... | collective-permute-start | bytes 983048 | tf_op jit(solution)/shard_map/ppermute | solution.py:383
  78.1 0.0 collective-permute-done.12.refs_1_
  78.1 6.3 %shard_map.40 = (f32[24,80,128]{2,1,0:T(8,128)S(1)}, f32[16,80,128]{2,1,0:T(8,128)S(1)}, f32[4,72,128]{2,1,0:T(8,128)S(1)}, f32[4,72,128]{2,1,0:T(8,128)S(1)}) custom-call(s32[3]{0:T(128)S(1)} %copy-done.5, f32[16,88,128]{2,1,0:T(8,128)S(1)} %get-tuple-element.56.refs_9_.refs_0_, f32[8,80,128]{2,1,0:T(8,128)S(1)} %collective-permute-done.12.refs_1_, ...), custom_call_target="tpu_custom_call" | custom-call | flops 1 | bytes 5849100 | tf_op jit(solution)/shard_map/pallas_call | solution.py:28
  84.4 0.1 collective-permute-start.16
  84.5 2.0 %collective-permute-start.17 = (f32[4,72,128]{2,1,0:T(8,128)S(1)}, f32[4,72,128]{2,1,0:T(8,128)S(1)}, u32[]{:S(2)}, u32[]{:S(2)}) collective-permute-start(f32[4,72,128]{2,1,0:T(8,128)S(1)} %get-tuple-element.71), channel_id=1, source_target_pairs={{1,2},{2,1},{5,6},{6,5},{9,10},{10,9},{13,14},{14,13},{17,18},{18,... | collective-permute-start | bytes 442376 | tf_op jit(solution)/shard_map/ppermute | solution.py:383
  86.5 0.0 collective-permute-done.10.refs_1_
  86.6 6.6 %shard_map.41 = (f32[24,80,128]{2,1,0:T(8,128)S(1)}, f32[16,80,128]{2,1,0:T(8,128)S(1)}, f32[4,72,128]{2,1,0:T(8,128)S(1)}, f32[4,72,128]{2,1,0:T(8,128)S(1)}, f32[8,128,128]{2,1,0:T(8,128)S(1)}) custom-call(s32[3]{0:T(128)S(1)} %copy-done.5, f32[16,88,128]{2,1,0:T(8,128)S(1)} %get-tuple-element.57.refs_0_, ...), custom_call_target="tpu_custom_call" | custom-call | flops 1 | bytes 8536076 | tf_op jit(solution)/shard_map/pallas_call | solution.py:28
  93.1 0.1 collective-permute-start.14
  93.2 3.5 %collective-permute-start.15 = (f32[4,72,128]{2,1,0:T(8,128)S(1)}, f32[4,72,128]{2,1,0:T(8,128)S(1)}, u32[]{:S(2)}, u32[]{:S(2)}) collective-permute-start(f32[4,72,128]{2,1,0:T(8,128)S(1)} %get-tuple-element.68), channel_id=1, source_target_pairs={{1,2},{2,1},{5,6},{6,5},{9,10},{10,9},{13,14},{14,13},{17,18},{18,... | collective-permute-start | bytes 442376 | tf_op jit(solution)/shard_map/ppermute | solution.py:383
  96.8 3.0 %shard_map.42.refs_6_ = f32[16,72,128]{2,1,0:T(8,128)S(1)} custom-call(s32[3]{0:T(128)S(1)} %copy-done.5, f32[16,80,128]{2,1,0:T(8,128)S(1)} %get-tuple-element.64.refs_7_.refs_0_, f32[4,72,128]{2,1,0:T(8,128)S(1)} %collective-permute-done.16.refs_1_, f32[4,72,128]{2,1,0:T(8,128)S(1)} %collective-permute-done.17.refs_2_, ...), custom_call_target="tpu_custom_call" | custom-call | flops 1 | bytes 3981324 | tf_op jit(solution)/shard_map/pallas_call | solution.py:28
  99.8 4.0 %shard_map.43 = (f32[8,32,128]{2,1,0:T(8,128)S(1)}, f32[8,32,128]{2,1,0:T(8,128)S(1)}, f32[8,32,128]{2,1,0:T(8,128)S(1)}, f32[8,32,128]{2,1,0:T(8,128)S(1)}) custom-call(s32[3]{0:T(128)S(1)} %copy-done.5, f32[16,80,128]{2,1,0:T(8,128)S(1)} %get-tuple-element.66.refs_0_, f32[4,72,128]{2,1,0:T(8,128)S(1)} %collective-permute-done.14.refs_1_, ...), custom_call_target="tpu_custom_call" | custom-call | flops 1 | bytes 5029900 | tf_op jit(solution)/shard_map/pallas_call | solution.py:28
  103.9 1.7 %collective-permute-start.18 = (f32[8,32,128]{2,1,0:T(8,128)S(1)}, f32[8,32,128]{2,1,0:T(8,128)S(1)}, u32[]{:S(2)}, u32[]{:S(2)}) collective-permute-start(f32[8,32,128]{2,1,0:T(8,128)S(1)} %get-tuple-element.74), channel_id=1, source_target_pairs={{0,8},{8,0},{16,24},{24,16},{1,9},{9,1},{17,25},{25,17},{2,10},{10... | collective-permute-start | bytes 393224 | tf_op jit(solution)/shard_map/ppermute | solution.py:481
  105.5 2.3 %collective-permute-start.19 = (f32[8,32,128]{2,1,0:T(8,128)S(1)}, f32[8,32,128]{2,1,0:T(8,128)S(1)}, u32[]{:S(2)}, u32[]{:S(2)}) collective-permute-start(f32[8,32,128]{2,1,0:T(8,128)S(1)} %get-tuple-element.75), channel_id=1, source_target_pairs={{0,16},{8,24},{16,0},{24,8},{1,17},{9,25},{17,1},{25,9},{2,18},{10... | collective-permute-start | bytes 393224 | tf_op jit(solution)/shard_map/ppermute | solution.py:481
  107.9 1.4 %collective-permute-done.18.refs_1_ = f32[8,32,128]{2,1,0:T(8,128)S(1)} collective-permute-done((f32[8,32,128]{2,1,0:T(8,128)S(1)}, f32[8,32,128]{2,1,0:T(8,128)S(1)}, u32[]{:S(2)}, u32[]{:S(2)}) %collective-permute-start.18) | collective-permute-done | bytes 131104 | tf_op jit(solution)/shard_map/ppermute | solution.py:481
  109.3 7.5 %collective-permute-done.19.refs_2_ = f32[8,32,128]{2,1,0:T(8,128)S(1)} collective-permute-done((f32[8,32,128]{2,1,0:T(8,128)S(1)}, f32[8,32,128]{2,1,0:T(8,128)S(1)}, u32[]{:S(2)}, u32[]{:S(2)}) %collective-permute-start.19) | collective-permute-done | bytes 131104 | tf_op jit(solution)/shard_map/ppermute | solution.py:481
  116.8 1.8 %shard_map.44 = f32[16,32,64]{2,1,0:T(8,128)} custom-call(s32[3]{0:T(128)S(1)} %copy-done.5, f32[8,32,128]{2,1,0:T(8,128)S(1)} %get-tuple-element.73.refs_0_, f32[8,32,128]{2,1,0:T(8,128)S(1)} %collective-permute-done.18.refs_1_, f32[8,32,128]{2,1,0:T(8,128)S(1)} %collective-permute-done.19.refs_2_, f32[8,32,128]{2,1,0:T(8,128)S(1)} %collective-permute-done.20.refs_3_), custom_call_target="tpu_custom_call" | custom-call | flops 1 | bytes 655372 | tf_op jit(solution)/shard_map/pallas_call | solution.py:28
  (24 shorter events, 0.1 us)
Async XLA Ops:
  0.6 8.4 %copy-start = (f32[1,1,2,16,128,128]{5,4,3,2,1,0:T(8,128)S(1)}, f32[1,1,2,16,128,128]{5,4,3,2,1,0:T(8,128)}, u32[]{:S(2)}) copy-start(f32[1,1,2,16,128,128]{5,4,3,2,1,0:T(8,128)} %states.1) | copy-start | bytes 6291460
  0.6 8.4 %copy-start.5 = (s32[3]{0:T(128)S(1)}, s32[3]{0:T(128)}, u32[]{:S(2)}) copy-start(s32[3]{0:T(128)} %pad_add_fusion.ids) | copy-start | bytes 40
  4.3 7.2 %copy-start.1 = (f32[16,128,128]{2,1,0:T(8,128)S(1)}, f32[16,128,128]{2,1,0:T(8,128)}, u32[]{:S(2)}) copy-start(f32[16,128,128]{2,1,0:T(8,128)} %courant.1) | copy-start | bytes 3145732
  4.3 8.6 %collective-permute-start = (f32[13,128,128]{2,1,0:T(8,128)}, f32[13,128,128]{2,1,0:T(8,128)S(1)}, u32[]{:S(2)}, u32[]{:S(2)}) collective-permute-start(f32[13,128,128]{2,1,0:T(8,128)} %get-tuple-element.44), channel_id=1, source_target_pairs={{0,1},{1,0},{2,3},{3,2},{4,5},{5,4},{6,7},{7,6},{8,9},{9,8},{10,11... | collective-permute-start | bytes 2555912 | tf_op jit(solution)/shard_map/ppermute | solution.py:384
  4.4 15.2 %collective-permute-start.1 = (f32[13,128,128]{2,1,0:T(8,128)}, f32[13,128,128]{2,1,0:T(8,128)S(1)}, u32[]{:S(2)}, u32[]{:S(2)}) collective-permute-start(f32[13,128,128]{2,1,0:T(8,128)} %get-tuple-element.45), channel_id=1, source_target_pairs={{1,2},{2,1},{5,6},{6,5},{9,10},{10,9},{13,14},{14,13},{17,18},{18,... | collective-permute-start | bytes 2555912 | tf_op jit(solution)/shard_map/ppermute | solution.py:383
  11.5 8.1 %copy-start.2 = (f32[1,12,16,128]{3,2,1,0:T(8,128)S(1)}, f32[1,12,16,128]{3,2,1,0:T(8,128)}, u32[]{:S(2)}) copy-start(f32[1,12,16,128]{3,2,1,0:T(8,128)} %rec.3) | copy-start | bytes 294916
  26.1 0.7 copy-start.3
  26.8 0.7 copy-start.6
  27.5 0.7 copy-start.7
  28.2 16.9 %collective-permute-start.2 = (f32[16,88,128]{2,1,0:T(8,128)}, f32[16,88,128]{2,1,0:T(8,128)}, u32[]{:S(2)}, u32[]{:S(2)}) collective-permute-start(f32[16,88,128]{2,1,0:T(8,128)} %get-tuple-element.46), channel_id=1, source_target_pairs={{0,4},{4,0},{1,5},{5,1},{2,6},{6,2},{3,7},{7,3},{8,12},{12,8},{9,1... | collective-permute-start | bytes 2162696 | tf_op jit(solution)/shard_map/ppermute | solution.py:387
  30.0 22.9 %collective-permute-start.5 = (f32[16,88,128]{2,1,0:T(8,128)}, f32[16,88,128]{2,1,0:T(8,128)}, u32[]{:S(2)}, u32[]{:S(2)}) collective-permute-start(f32[16,88,128]{2,1,0:T(8,128)} %get-tuple-element.47), channel_id=1, source_target_pairs={{0,4},{4,0},{1,5},{5,1},{2,6},{6,2},{3,7},{7,3},{8,12},{12,8},{9,1... | collective-permute-start | bytes 2162696 | tf_op jit(solution)/shard_map/ppermute | solution.py:387
  30.0 27.6 %copy-start.4 = (f32[4,128,128]{2,1,0:T(8,128)S(1)}, f32[4,128,128]{2,1,0:T(8,128)}, u32[]{:S(2)}) copy-start(f32[4,128,128]{2,1,0:T(8,128)} %copy-done.3) | copy-start | bytes 786436
  30.0 27.5 %collective-permute-start.8 = (f32[8,88,128]{2,1,0:T(8,128)}, f32[8,88,128]{2,1,0:T(8,128)S(1)}, u32[]{:S(2)}, u32[]{:S(2)}) collective-permute-start(f32[8,88,128]{2,1,0:T(8,128)} %copy-done.7), channel_id=1, source_target_pairs={{0,1},{1,0},{2,3},{3,2},{4,5},{5,4},{6,7},{7,6},{8,9},{9,8},{10,11... | collective-permute-start | bytes 1081352 | tf_op jit(solution)/shard_map/ppermute | solution.py:384
  30.0 27.5 %collective-permute-start.9 = (f32[8,88,128]{2,1,0:T(8,128)}, f32[8,88,128]{2,1,0:T(8,128)S(1)}, u32[]{:S(2)}, u32[]{:S(2)}) collective-permute-start(f32[8,88,128]{2,1,0:T(8,128)} %copy-done.6), channel_id=1, source_target_pairs={{1,2},{2,1},{5,6},{6,5},{9,10},{10,9},{13,14},{14,13},{17,18},{18,... | collective-permute-start | bytes 1081352 | tf_op jit(solution)/shard_map/ppermute | solution.py:383
  46.3 20.5 %collective-permute-start.4 = (f32[8,88,128]{2,1,0:T(8,128)S(1)}, f32[8,88,128]{2,1,0:T(8,128)S(1)}, u32[]{:S(2)}, u32[]{:S(2)}) collective-permute-start(f32[8,88,128]{2,1,0:T(8,128)S(1)} %get-tuple-element.79), channel_id=1, source_target_pairs={{1,2},{2,1},{5,6},{6,5},{9,10},{10,9},{13,14},{14,13},{17,18},{18,... | collective-permute-start | bytes 1081352 | tf_op jit(solution)/shard_map/ppermute | solution.py:383
  49.9 16.9 %collective-permute-start.3 = (f32[8,88,128]{2,1,0:T(8,128)S(1)}, f32[8,88,128]{2,1,0:T(8,128)S(1)}, u32[]{:S(2)}, u32[]{:S(2)}) collective-permute-start(f32[8,88,128]{2,1,0:T(8,128)S(1)} %get-tuple-element.80), channel_id=1, source_target_pairs={{0,1},{1,0},{2,3},{3,2},{4,5},{5,4},{6,7},{7,6},{8,9},{9,8},{10,11... | collective-permute-start | bytes 1081352 | tf_op jit(solution)/shard_map/ppermute | solution.py:384
  53.9 10.8 %collective-permute-start.7 = (f32[4,88,128]{2,1,0:T(8,128)S(1)}, f32[4,88,128]{2,1,0:T(8,128)S(1)}, u32[]{:S(2)}, u32[]{:S(2)}) collective-permute-start(f32[4,88,128]{2,1,0:T(8,128)S(1)} %get-tuple-element.77), channel_id=1, source_target_pairs={{1,2},{2,1},{5,6},{6,5},{9,10},{10,9},{13,14},{14,13},{17,18},{18,... | collective-permute-start | bytes 540680 | tf_op jit(solution)/shard_map/ppermute | solution.py:383
  57.5 9.3 %collective-permute-start.6 = (f32[4,88,128]{2,1,0:T(8,128)S(1)}, f32[4,88,128]{2,1,0:T(8,128)S(1)}, u32[]{:S(2)}, u32[]{:S(2)}) collective-permute-start(f32[4,88,128]{2,1,0:T(8,128)S(1)} %get-tuple-element.78), channel_id=1, source_target_pairs={{0,1},{1,0},{2,3},{3,2},{4,5},{5,4},{6,7},{7,6},{8,9},{9,8},{10,11... | collective-permute-start | bytes 540680 | tf_op jit(solution)/shard_map/ppermute | solution.py:384
  64.2 13.9 %collective-permute-start.12 = (f32[8,80,128]{2,1,0:T(8,128)S(1)}, f32[8,80,128]{2,1,0:T(8,128)S(1)}, u32[]{:S(2)}, u32[]{:S(2)}) collective-permute-start(f32[8,80,128]{2,1,0:T(8,128)S(1)} %get-tuple-element.61), channel_id=1, source_target_pairs={{0,1},{1,0},{2,3},{3,2},{4,5},{5,4},{6,7},{7,6},{8,9},{9,8},{10,11... | collective-permute-start | bytes 983048 | tf_op jit(solution)/shard_map/ppermute | solution.py:384
  64.8 13.3 %collective-permute-start.13 = (f32[8,80,128]{2,1,0:T(8,128)S(1)}, f32[8,80,128]{2,1,0:T(8,128)S(1)}, u32[]{:S(2)}, u32[]{:S(2)}) collective-permute-start(f32[8,80,128]{2,1,0:T(8,128)S(1)} %get-tuple-element.62), channel_id=1, source_target_pairs={{1,2},{2,1},{5,6},{6,5},{9,10},{10,9},{13,14},{14,13},{17,18},{18,... | collective-permute-start | bytes 983048 | tf_op jit(solution)/shard_map/ppermute | solution.py:383
  74.5 12.1 %collective-permute-start.10 = (f32[8,80,128]{2,1,0:T(8,128)S(1)}, f32[8,80,128]{2,1,0:T(8,128)S(1)}, u32[]{:S(2)}, u32[]{:S(2)}) collective-permute-start(f32[8,80,128]{2,1,0:T(8,128)S(1)} %get-tuple-element.58), channel_id=1, source_target_pairs={{0,1},{1,0},{2,3},{3,2},{4,5},{5,4},{6,7},{7,6},{8,9},{9,8},{10,11... | collective-permute-start | bytes 983048 | tf_op jit(solution)/shard_map/ppermute | solution.py:384
  74.5 12.0 %collective-permute-start.11 = (f32[8,80,128]{2,1,0:T(8,128)S(1)}, f32[8,80,128]{2,1,0:T(8,128)S(1)}, u32[]{:S(2)}, u32[]{:S(2)}) collective-permute-start(f32[8,80,128]{2,1,0:T(8,128)S(1)} %get-tuple-element.59), channel_id=1, source_target_pairs={{1,2},{2,1},{5,6},{6,5},{9,10},{10,9},{13,14},{14,13},{17,18},{18,... | collective-permute-start | bytes 983048 | tf_op jit(solution)/shard_map/ppermute | solution.py:383
  84.4 12.3 %collective-permute-start.16 = (f32[4,72,128]{2,1,0:T(8,128)S(1)}, f32[4,72,128]{2,1,0:T(8,128)S(1)}, u32[]{:S(2)}, u32[]{:S(2)}) collective-permute-start(f32[4,72,128]{2,1,0:T(8,128)S(1)} %get-tuple-element.70), channel_id=1, source_target_pairs={{0,1},{1,0},{2,3},{3,2},{4,5},{5,4},{6,7},{7,6},{8,9},{9,8},{10,11... | collective-permute-start | bytes 442376 | tf_op jit(solution)/shard_map/ppermute | solution.py:384
  84.5 12.3 %collective-permute-start.17 = (f32[4,72,128]{2,1,0:T(8,128)S(1)}, f32[4,72,128]{2,1,0:T(8,128)S(1)}, u32[]{:S(2)}, u32[]{:S(2)}) collective-permute-start(f32[4,72,128]{2,1,0:T(8,128)S(1)} %get-tuple-element.71), channel_id=1, source_target_pairs={{1,2},{2,1},{5,6},{6,5},{9,10},{10,9},{13,14},{14,13},{17,18},{18,... | collective-permute-start | bytes 442376 | tf_op jit(solution)/shard_map/ppermute | solution.py:383
  93.1 6.7 %collective-permute-start.14 = (f32[4,72,128]{2,1,0:T(8,128)S(1)}, f32[4,72,128]{2,1,0:T(8,128)S(1)}, u32[]{:S(2)}, u32[]{:S(2)}) collective-permute-start(f32[4,72,128]{2,1,0:T(8,128)S(1)} %get-tuple-element.67), channel_id=1, source_target_pairs={{0,1},{1,0},{2,3},{3,2},{4,5},{5,4},{6,7},{7,6},{8,9},{9,8},{10,11... | collective-permute-start | bytes 442376 | tf_op jit(solution)/shard_map/ppermute | solution.py:384
  93.2 6.6 %collective-permute-start.15 = (f32[4,72,128]{2,1,0:T(8,128)S(1)}, f32[4,72,128]{2,1,0:T(8,128)S(1)}, u32[]{:S(2)}, u32[]{:S(2)}) collective-permute-start(f32[4,72,128]{2,1,0:T(8,128)S(1)} %get-tuple-element.68), channel_id=1, source_target_pairs={{1,2},{2,1},{5,6},{6,5},{9,10},{10,9},{13,14},{14,13},{17,18},{18,... | collective-permute-start | bytes 442376 | tf_op jit(solution)/shard_map/ppermute | solution.py:383
  103.9 5.5 %collective-permute-start.18 = (f32[8,32,128]{2,1,0:T(8,128)S(1)}, f32[8,32,128]{2,1,0:T(8,128)S(1)}, u32[]{:S(2)}, u32[]{:S(2)}) collective-permute-start(f32[8,32,128]{2,1,0:T(8,128)S(1)} %get-tuple-element.74), channel_id=1, source_target_pairs={{0,8},{8,0},{16,24},{24,16},{1,9},{9,1},{17,25},{25,17},{2,10},{10... | collective-permute-start | bytes 393224 | tf_op jit(solution)/shard_map/ppermute | solution.py:481
  105.5 11.3 %collective-permute-start.19 = (f32[8,32,128]{2,1,0:T(8,128)S(1)}, f32[8,32,128]{2,1,0:T(8,128)S(1)}, u32[]{:S(2)}, u32[]{:S(2)}) collective-permute-start(f32[8,32,128]{2,1,0:T(8,128)S(1)} %get-tuple-element.75), channel_id=1, source_target_pairs={{0,16},{8,24},{16,0},{24,8},{1,17},{9,25},{17,1},{25,9},{2,18},{10... | collective-permute-start | bytes 393224 | tf_op jit(solution)/shard_map/ppermute | solution.py:481
  107.9 9.0 %collective-permute-start.20 = (f32[8,32,128]{2,1,0:T(8,128)S(1)}, f32[8,32,128]{2,1,0:T(8,128)S(1)}, u32[]{:S(2)}, u32[]{:S(2)}) collective-permute-start(f32[8,32,128]{2,1,0:T(8,128)S(1)} %get-tuple-element.76), channel_id=1, source_target_pairs={{0,24},{8,16},{16,8},{24,0},{1,25},{9,17},{17,9},{25,1},{2,26},{10... | collective-permute-start | bytes 393224 | tf_op jit(solution)/shard_map/ppermute | solution.py:481

commit v3 on v2

v3 whole, which is shorter than its diff:
```python
import functools

import jax
import jax.numpy as jnp
from jax import lax
from jax.experimental import pallas as pl
from jax.experimental.pallas import tpu as pltpu
from jax.sharding import PartitionSpec as P


STEPS = 12
IMAGE_EVERY = 2
GROUP = 4
F32 = jnp.float32
VM = pl.BlockSpec(memory_space=pltpu.VMEM)
HC = 6
DEPTH = 8
MORE = 4
HR = 16
REC = 8
PER = 128 // HR
FIRST = REC + -(-STEPS // PER)


def sds(*shape):
    return jax.ShapeDtypeStruct(shape, F32)


def call(kernel, outs, scratch, *args, limit=8, flops=1):
    moved = sum(4 * a.size for a in args) + sum(4 * o.size for o in outs)
    return pl.pallas_call(
        kernel,
        out_shape=outs,
        in_specs=[VM] * len(args),
        out_specs=[VM] * len(outs),
        scratch_shapes=scratch,
        compiler_params=pltpu.CompilerParams(vmem_limit_bytes=limit << 20),
        cost_estimate=pl.CostEstimate(flops=flops, bytes_accessed=moved, transcendentals=0),
    )(*args)


def ext_ref(planes, rows):
    return pltpu.VMEM((planes, rows // 8, 8, 128), F32)


def parity():
    return lax.rem(lax.axis_index("space"), 2)


def fill_band(band):
    row = lax.broadcasted_iota(jnp.int32, (128, 128), 0)
    col = lax.broadcasted_iota(jnp.int32, (128, 128), 1)
    away = jnp.abs(row - col)
    taps = jnp.where(away == 0, -90.0, jnp.where(away == 1, 16.0, jnp.where(away == 2, -1.0, 0.0)))
    band[0:128] = taps.astype(jnp.bfloat16)
    band[128:256] = taps.astype(jnp.bfloat16)


def load(dst, at, src, x, base, width):
    for j in range(width):
        dst[at, j] = src[x, pl.ds(base + j, 8, stride=width), :]


def store(dst, at, src, x, width):
    for j in range(width):
        dst[at, pl.ds(j, 8, stride=width), :] = src[x, j]


def sweep(field, coef, band, first, count, c_first, put):
    width = field.shape[1]
    sub = lax.broadcasted_iota(jnp.int32, (8, 128), 0)
    top, bottom = sub < 1, sub >= 7
    zero = jnp.zeros((8, 128), F32)

    @pl.loop(0, count, step=GROUP)
    def _(k):
        x = first + k
        flat = field[pl.ds(x, GROUP)].reshape(GROUP * width * 8, 128)
        high = flat.astype(jnp.bfloat16)
        rest = flat - high.astype(F32)
        middle = rest.astype(jnp.bfloat16)
        low = (rest - middle.astype(F32)).astype(jnp.bfloat16)
        lanes = jnp.dot(
            jnp.concatenate([high, middle], 1), band[...], preferred_element_type=F32
        ) + jnp.dot(low, band[0:128], preferred_element_type=F32)
        for p in range(GROUP):
            own = [field[x + p, j] for j in range(width)]
            rows = (
                [jnp.where(top, zero, pltpu.roll(own[width - 2], 1, 0)),
                 jnp.where(top, zero, pltpu.roll(own[width - 1], 1, 0))]
                + own
                + [jnp.where(bottom, zero, pltpu.roll(own[0], 7, 0)),
                   jnp.where(bottom, zero, pltpu.roll(own[1], 7, 0))]
            )
            for j in range(width):
                near = (field[x + p - 1, j] + field[x + p + 1, j]) + (rows[j + 1] + rows[j + 3])
                far = (field[x + p - 2, j] + field[x + p + 2, j]) + (rows[j] + rows[j + 4])
                at = (p * width + j) * 8
                total = 16.0 * near - far + lanes[at : at + 8]
                v = own[j]
                put(k + p, j, v, coef[c_first + k + p, j] * total)


def pulse(rec, x, tick, flag):
    sub = lax.broadcasted_iota(jnp.int32, (8, 128), 0)
    row = rec[tick, pl.ds(x, 1), :] * flag
    return jnp.where(sub < 1, jnp.broadcast_to(row, (8, 128)), 0.0)


def pack(states, courant, rec, send_a, send_b, sems):
    n = courant.shape[0]
    odd = parity()
    copies = []
    for index, (send, high) in enumerate(((send_a, odd == 0), (send_b, odd == 1))):
        at = lambda h: jnp.where(high, n - h, 0)
        moves = [
            (states.at[0, 0, 1, pl.ds(at(4), 4)], send.at[pl.ds(0, 4)]),
            (states.at[0, 0, 0, pl.ds(at(2), 2)], send.at[pl.ds(4, 2)]),
            (courant.at[pl.ds(at(2), 2)], send.at[pl.ds(6, 2)]),
        ]
        first = pl.multiple_of(at(HR), HR)
        for k in range(STEPS):
            send[REC + k // PER, HR * (k % PER) : HR * (k % PER + 1), :] = rec[0, k, pl.ds(first, HR), :]
        for k, (source, target) in enumerate(moves):
            copy = pltpu.make_async_copy(source, target, sems.at[index, k])
            copy.start()
            copies.append(copy)
    for copy in copies:
        copy.wait()


def prepare_now(now, nowt, give):
    start = pl.multiple_of((1 - lax.axis_index("pair")) * (128 - give.shape[1]), 8)
    for k in range(GROUP):
        nowt[k] = now[0, 0, 0, k].T
        give[k] = nowt[k, pl.ds(start, give.shape[1]), :]


def prepare_rest(old, coef, oldt, coeft):
    for k in range(GROUP):
        oldt[k] = old[0, 0, 0, k].T
        coeft[k] = coef[k].T * (1.0 / 12.0)


def place(odd, n, halo, depth):
    after, before = halo + n, halo - depth
    return jnp.where(odd == 0, after, before), jnp.where(odd == 0, before, after)


def first_block(nowt, oldt, coeft, rec, got_a, got_b,
                give, one, near, rfull, send_a, send_b,
                cur, old, mid, new, cx, band, raw_a, raw_b, plain):
    n = nowt.shape[0]
    odd, role = parity(), lax.axis_index("pair")
    flag = role.astype(F32)
    rows = one.shape[1]
    base = pl.multiple_of(role * (128 - rows), 8)
    other = pl.multiple_of((1 - role) * (128 - rows), 8)
    fill_band(band)

    @pl.loop(0, n)
    def _(x):
        load(cur, x + 4, nowt, x, 0, 16)
        load(old, x + 2, oldt, x, 0, 16)
        load(cx, x + 2, coeft, x, 0, 16)
        near[x + 2] = coeft[x, pl.ds(base, rows), :]

    for raw, turned in ((got_a, raw_a), (got_b, raw_b)):
        for k in range(REC):
            value = raw[k].T
            turned[k] = value if k < 6 else value * (1.0 / 12.0)

    a_rec, b_rec = place(odd, n, HR, HR)
    for k in range(STEPS):
        rfull[k, HR : HR + n, :] = rec[0, k]
        for got, at in ((got_a, a_rec), (got_b, b_rec)):
            piece = got[REC + k // PER, HR * (k % PER) : HR * (k % PER + 1), :]
            rfull[k, pl.ds(pl.multiple_of(at, 8), HR), :] = piece

    a4, b4 = place(odd, n, 4, 4)
    a2, b2 = place(odd, n, 2, 2)
    for got, at4, at2, spot in ((raw_a, a4, a2, n + 4), (raw_b, b4, b2, n + 8)):
        for k in range(4):
            load(cur, at4 + k, got, k, 0, 16)
            near[spot + k] = got[k, pl.ds(base, rows), :]
        for k in range(2):
            load(old, at2 + k, got, 4 + k, 0, 16)
            load(cx, at2 + k, got, 6 + k, 0, 16)
            near[at2 + k] = got[6 + k, pl.ds(base, rows), :]

    def put0(x, j, v, change):
        value = (v + v) - old[x, j] + change
        if j == 0:
            value = value + pulse(rfull, x + HR - 2, 0, flag)
        mid[x, j] = value

    sweep(cur, cx, band, 2, n + 4, 0, put0)

    def put1(x, j, v, change):
        value = (v + v) - cur[x + 4, j] + change
        if j == 0:
            value = value + pulse(rfull, x + HR, 1, flag)
        new[x, j] = value

    sweep(mid, cx, band, 2, n, 2, put1)

    @pl.loop(0, n)
    def _(x):
        store(plain, x, new, x, 16)
        one[x] = plain[x, pl.ds(base, rows), :]
        give[x] = plain[x, pl.ds(other, rows), :]

    pack_ends(one, send_a, send_b, odd, role, DEPTH)
    for send, high in ((send_a, odd == 0), (send_b, odd == 1)):
        start = jnp.where(high, n - HC, 2) + 2
        for k in range(HC - 2):
            send[DEPTH + k] = near[start + k]


def pack_ends(field, send_a, send_b, odd, role, depth):
    n, rows = field.shape[0], send_a.shape[1]
    base = pl.multiple_of(role * (field.shape[1] - rows), 8)
    high = n - depth
    for send, start in ((send_a, jnp.where(odd == 0, high, 0)), (send_b, jnp.where(odd == 0, 0, high))):

        @pl.loop(0, depth)
        def _(k):
            send[k] = field[start + k, pl.ds(base, rows), :]


def block(rows, steps, tick, lit, fresh, last, shots, *refs):
    it = iter(refs)
    take = lambda count: [next(it) for _ in range(count)]
    u, got_a, got_b, was, coef, rfull = take(6)
    was_a, was_b = take(2) if fresh and lit else (None, None)
    mates = take(steps) if lit else []
    first_mate = take(1)[0] if lit and fresh else None
    image_in = take(1)[0] if lit and not fresh else None
    inner = take(1)[0] if steps > 1 else None
    out = take(1)[0] if not (lit and last) else None
    send_a, send_b = take(2) if not last else (None, None)
    whole = take(1)[0] if fresh and not lit else coef
    image = take(1)[0] if lit and not last else None
    pieces = take(shots) if lit and last else []
    cur, old, mid, cx, band = take(5)
    third = take(1)[0] if steps == 3 else None
    if lit and last:
        out, image = take(2)

    odd, role = parity(), lax.axis_index("pair")
    n = u.shape[0]
    width = rows // 8
    halo = 4 * steps
    flag = (1 - role).astype(F32)
    fill_band(band)

    def window(ref):
        return pl.multiple_of(role * (ref.shape[1] - rows), 8)

    if fresh and not lit:
        was_a, was_b = coef.at[pl.ds(n + 4, 4)], coef.at[pl.ds(n + 8, 4)]

        @pl.loop(0, n + 4)
        def _(x):
            whole[x + HC - 2] = coef[x]

        at_a, at_b = place(odd, n + 4, HC - 2, HC - 2)
        for k in range(HC - 2):
            whole[at_a + k] = got_a[DEPTH + k]
            whole[at_b + k] = got_b[DEPTH + k]

    reach_old = halo - 4
    if fresh:
        @pl.loop(0, n)
        def _(x):
            load(old, x + reach_old, was, x, window(was), width)

        old_a, old_b = place(odd, n, reach_old, reach_old)

        @pl.loop(0, reach_old)
        def _(k):
            load(old, old_a + k, was_a, k, window(was_a), width)
            load(old, old_b + k, was_b, k, window(was_b), width)
    else:
        shift = (was.shape[0] - n) // 2 - reach_old

        @pl.loop(0, n + 2 * reach_old)
        def _(x):
            load(old, x, was, x + shift, window(was), width)

    beyond = max(halo - 2 - HC, 0)

    @pl.loop(0, n + 2 * min(halo - 2, HC))
    def _(x):
        load(cx, x + beyond, whole, x + max(HC - (halo - 2), 0), window(whole), width)

    if beyond:
        at_a, at_b = place(odd, n + 2 * HC, beyond, beyond)

        @pl.loop(0, beyond)
        def _(k):
            load(cx, at_a + k, was_a, reach_old + k, window(was_a), width)
            load(cx, at_b + k, was_b, reach_old + k, window(was_b), width)

    @pl.loop(0, n)
    def _(x):
        load(cur, x + halo, u, x, window(u), width)

    at_a, at_b = place(odd, n, halo, halo)

    @pl.loop(0, halo)
    def _(k):
        load(cur, at_a + k, got_a, k, 0, width)
        load(cur, at_b + k, got_b, k, 0, width)

    now, before = cur, old
    for s in range(steps):
        reach = halo - 4 * s
        time = tick + 2 * s

        def put_mid(x, j, v, change):
            value = (v + v) + change
            if lit and j == 0:
                value = value + pulse(rfull, x + HR - (reach - 2), time + 1, flag)
            mid[x, j] = value

        sweep(now, cx, band, 2, n + 2 * (reach - 2), halo - reach, put_mid)

        def put_new(x, j, v, change):
            gain = v - now[x + 4, j]
            value = (gain + gain) - before[x, j] + change
            if lit and j == 0:
                at = x + HR - (reach - 4)
                value = value + (pulse(rfull, at, time, flag) + pulse(rfull, at, time + 2, flag))
            before[x, j] = value

        sweep(mid, cx, band, 2, n + 2 * (reach - 4), halo - reach + 2, put_new)
        target = (third, inner, out)[3 - steps + s]
        skip = (reach - 4) - (target.shape[0] - n) // 2

        @pl.loop(0, target.shape[0])
        def _(x):
            store(target, x, before, x + skip, width)

        if s < steps - 1:
            now, before = before, now.at[pl.ds(8, n + 2 * (reach - 8))]

    if not last:
        pack_ends(out, send_a, send_b, odd, role, send_a.shape[0])

    if lit:
        half, pairs = 64, n // 2
        mine = [third, inner, out][3 - steps :]

        @pl.loop(0, pairs)
        def _(k):
            for side in range(2):
                x = k + side * pairs

                def part(ref, extra):
                    start = pl.multiple_of(role * (ref.shape[1] - half), 8)
                    return ref[x + extra, pl.ds(start, half), :]

                total = None
                for field, mate in zip(mine, mates):
                    product = part(field, (field.shape[0] - n) // 2) * part(mate, (mate.shape[0] - n) // 2)
                    total = product if total is None else total + product
                if fresh:
                    total = total + part(u, 0) * part(first_mate, 0)
                else:
                    total = total + image_in[k, side * half : (side + 1) * half, :]
                image[k, side * half : (side + 1) * half, :] = total

        if last:
            piece = 128 // shots
            weight = IMAGE_EVERY / STEPS

            @pl.loop(0, pairs)
            def _(k):
                image[k] = image[k].T * weight
                for index in range(shots):
                    target = jnp.bitwise_xor(lax.axis_index("shot"), index)
                    pieces[index][k] = image[k, pl.ds(pl.multiple_of(target * piece, 8), piece), :]


def combine(count, *refs):
    out = refs[count]
    pairs = refs[0].shape[0]

    @pl.loop(0, pairs)
    def _(k):
        total = refs[0][k]
        for index in range(1, count):
            total = total + refs[index][k]
        out[k] = total[:, :64]
        out[k + pairs] = pltpu.roll(total, 64, 1)[:, :64]


def on_device(states, courant, records):
    n = courant.shape[0]
    shots, spaces = lax.axis_size("shot"), lax.axis_size("space")
    odd = parity()

    pairs_a = [(i, i ^ 1) for i in range(spaces)]
    pairs_b = [(i, i + 1) for i in range(1, spaces - 1, 2)]
    pairs_b = pairs_b + [(j, i) for i, j in pairs_b]

    def swap(send_a, send_b):
        got_b = lax.ppermute(send_b, "space", pairs_b)
        return lax.ppermute(send_a, "space", pairs_a), got_b

    def across(value):
        return lax.ppermute(value, "pair", [(0, 1), (1, 0)])

    def ends(value, depth, skip=0):
        low, high = value[skip : skip + depth], value[n - skip - depth : n - skip]
        high_first = odd == 0
        return jnp.where(high_first, high, low), jnp.where(high_first, low, high)

    wide, mid_rows, thin = 88, 80, 72
    band = pltpu.VMEM((256, 128), jnp.bfloat16)
    hbm = pl.BlockSpec(memory_space=pltpu.HBM)

    send_a, send_b = pl.pallas_call(
        pack,
        out_shape=(sds(FIRST, 128, 128),) * 2,
        in_specs=[hbm, hbm, VM],
        out_specs=[VM, VM],
        scratch_shapes=[pltpu.SemaphoreType.DMA((2, 3))],
        compiler_params=pltpu.CompilerParams(vmem_limit_bytes=58 << 20),
        name="pack",
    )(states, courant, records)
    got_a, got_b = swap(send_a, send_b)

    def state_block(index):
        return pl.BlockSpec((1, 1, 1, GROUP, 128, 128), lambda i: (0, 0, index, i, 0, 0))

    def planes(rows):
        return pl.BlockSpec((GROUP, rows, 128), lambda i: (i, 0, 0))

    nowt, give_now = pl.pallas_call(
        prepare_now,
        grid=(n // GROUP,),
        out_shape=(sds(n, 128, 128), sds(n, wide, 128)),
        in_specs=[state_block(1)],
        out_specs=[planes(128), planes(wide)],
        compiler_params=pltpu.CompilerParams(vmem_limit_bytes=6 << 20),
        name="prepare_now",
    )(states)
    other_was = across(give_now)
    oldt, coeft = pl.pallas_call(
        prepare_rest,
        grid=(n // GROUP,),
        out_shape=(sds(n, 128, 128), sds(n, 128, 128)),
        in_specs=[state_block(0), planes(128)],
        out_specs=[planes(128), planes(128)],
        compiler_params=pltpu.CompilerParams(vmem_limit_bytes=6 << 20),
        name="prepare_rest",
    )(states, courant)
    give_one, one, near, rfull, send_a, send_b = call(
        first_block,
        (sds(n, wide, 128), sds(n, wide, 128), sds(n + 12, wide, 128), sds(STEPS, n + 2 * HR, 128),
         sds(DEPTH + HC - 2, wide, 128), sds(DEPTH + HC - 2, wide, 128)),
        [ext_ref(n + 8, 128), ext_ref(n + 4, 128), ext_ref(n + 4, 128), ext_ref(n, 128), ext_ref(n + 4, 128), band]
        + [pltpu.VMEM((REC, 128, 128), F32)] * 2 + [pltpu.VMEM((n, 128, 128), F32)],
        nowt, oldt, coeft, records, got_a, got_b, limit=12,
    )
    other_one = across(give_one)

    def run(rows, steps, tick, lit, fresh, last, depth, after, *args):
        outs = []
        if steps > 1:
            outs.append(sds(n + 8, rows, 128))
        if not (lit and last):
            outs.append(sds(n, rows, 128))
        if not last:
            outs += [sds(depth, after, 128)] * 2
        if fresh and not lit:
            outs.append(sds(n + 2 * HC, rows, 128))
        if lit:
            outs += [sds(n // 2, 128 // shots, 128)] * shots if last else [sds(n // 2, 128, 128)]
        halo = 4 * steps
        scratch = [ext_ref(n + 2 * halo, rows), ext_ref(n + 2 * (halo - 4), rows), ext_ref(n + 2 * (halo - 2), rows),
                   ext_ref(n + 2 * (halo - 2), rows), band]
        if steps == 3:
            scratch.append(pltpu.VMEM((n, rows, 128), F32))
        if lit and last:
            scratch += [pltpu.VMEM((n, rows, 128), F32), pltpu.VMEM((n // 2, 128, 128), F32)]
        kernel = functools.partial(block, rows, steps, tick, lit, fresh, last, shots)
        return call(kernel, tuple(outs), scratch, *args, limit=10)

    got = swap(send_a, send_b)
    three, five, send_a, send_b, cfull = run(
        wide, 2, 1, False, True, False, 8, mid_rows, one, *got, nowt, near, rfull)
    got = swap(send_a, send_b)
    seven, nine, send_a, send_b = run(
        mid_rows, 2, 5, False, False, False, 4, thin, five, *got, three, cfull, rfull)
    got = swap(send_a, send_b)
    (eleven,) = run(thin, 1, 9, False, False, True, 0, 0, nine, *got, seven, cfull, rfull)

    was_ends, coef_ends = ends(other_was, 8), ends(near[2 : 2 + n], MORE, HC)
    got_was = swap(*(jnp.concatenate(pair) for pair in zip(was_ends, coef_ends)))
    got = swap(*ends(other_one, 12))
    o_five, o_seven, send_a, send_b, image = run(
        wide, 3, 1, True, True, False, 8, thin,
        other_one, *got, other_was, cfull, rfull, *got_was, three, five, seven, one)
    got = swap(send_a, send_b)
    _, *pieces = run(
        thin, 2, 7, True, False, True, 0, 0, o_seven, *got, o_five, cfull, rfull, nine, eleven, image)

    arrived = [pieces[0]]
    for index in range(1, shots):
        arrived.append(lax.ppermute(pieces[index], "shot", [(i, i ^ index) for i in range(shots)]))
    (result,) = call(functools.partial(combine, shots), (sds(n, 128 // shots, 64),), [], *arrived)
    return result


def solution(mesh):
    placed = (
        P("shot", "pair", None, "space", None, None),
        P("space", None, None),
        P("shot", None, "space", None),
    )
    return jax.shard_map(on_device, mesh=mesh, in_specs=placed, out_specs=P("space", "shot", "pair"), check_vma=False)
```

time: 119 us -> 105 us (0.88)
  starting transfers between devices: 33.6 us -> 28.5 us
  Pallas kernels: 50 us -> 45.7 us
  other arithmetic: 2.82 us -> 0.2 us
  waiting for transfers between devices: 29.8 us -> 28.1 us
    ppermute x8 -> x7, waiting for transfers between devices: 6.72 us -> 21.6 us  [swap(): got_b = lax.ppermute(send_b, 'space', pairs_b)]
    ppermute x2, waiting for transfers between devices: 14.1 us -> 0.01 us  [across(): return lax.ppermute(value, 'pair', [(0, 1), (1, 0)])]
    ppermute x8 -> x7, starting transfers between devices: 26.8 us -> 21.4 us  [swap(): got_b = lax.ppermute(send_b, 'space', pairs_b)]
    pallas_call x9 -> x8, Pallas kernels: 46.1 us -> 43 us  [the longest x7 39.6 us: call(): pl.pallas_call(kernel, out_shape=outs, in_specs=[VM] * len(args), out_spe...]
    ppermute x3, waiting for transfers between devices: 8.97 us -> 6.49 us  [on_device(): lax.ppermute(pieces[index], 'shot', [(i, i ^ index) for i in range(shots)])]
    select_n x2, other arithmetic: 2.18 us -> 0.13 us  [ends(): return (jnp.where(high_first, high, low), jnp.where(high_first, low, high))]
    ppermute x2, starting transfers between devices: 1.78 us -> 2.99 us  [across(): return lax.ppermute(value, 'pair', [(0, 1), (1, 0)])]
  transfers between devices with their start and end apart: 21 -> 19, of which waited for: 5 -> 6; matrix products, arithmetic and copies ran while one was open for 2% -> 1% of each run, Pallas kernels for 29% -> 22%
where the time goes in v3:
time: 105 us
  Pallas kernels  45.7 us (44%)
  starting transfers between devices  28.5 us (27%)
  waiting for transfers between devices  28.1 us (27%)
  local copies, waits for them, and re-layouts  2.02 us (2%)
    pallas_call x7, Pallas kernels, call(): pl.pallas_call(kernel, out_shape=outs, in_specs=[VM] * len(args), out_spe...  39.6 us
    ppermute x7, waiting for transfers between devices, swap(): got_b = lax.ppermute(send_b, 'space', pairs_b)  21.6 us
    ppermute x7, starting transfers between devices, swap(): got_b = lax.ppermute(send_b, 'space', pairs_b)  21.4 us
    ppermute x3, waiting for transfers between devices, on_device(): lax.ppermute(pieces[index], 'shot', [(i, i ^ index) for i in range(shots)])  6.49 us
    ppermute x3, starting transfers between devices, on_device(): lax.ppermute(pieces[index], 'shot', [(i, i ^ index) for i in range(shots)])  3.62 us
    pallas_call x1, Pallas kernels, on_device(): pl.pallas_call(pack, out_shape=(sds(FIRST, 128, 128),) * 2, in_specs=[hbm...  3.41 us
    ppermute x2, starting transfers between devices, across(): return lax.ppermute(value, 'pair', [(0, 1), (1, 0)])  2.99 us
  transfers between devices with their start and end apart: 19, of which 6 were waited for; matrix products, arithmetic and copies ran while one was open for 1% of the time, Pallas kernels for 22%

profile of v3, /device:TPU:1, one launch (start us, length us, event | category | flops | bytes accessed | tf_op | source)
XLA Modules:
  0.0 104.8 jit_solution(1387789866567445529)
XLA Ops:
  0.0 3.4 %pack.1 = (f32[10,128,128]{2,1,0:T(8,128)}, f32[10,128,128]{2,1,0:T(8,128)}) custom-call(f32[1,1,2,16,128,128]{5,4,3,2,1,0:T(8,128)} %states.1, f32[16,128,128]{2,1,0:T(8,128)} %courant.1, f32[1,12,16,128]{3,2,1,0:T(8,128)} %rec.3), custom_call_target="tpu_custom_call" | custom-call | tf_op jit(solution)/shard_map/pack/pallas_call | solution.py:424
  3.4 0.0 copy-start.1
  3.4 0.1 collective-permute-start
  3.5 4.6 %collective-permute-start.1 = (f32[10,128,128]{2,1,0:T(8,128)}, f32[10,128,128]{2,1,0:T(8,128)S(1)}, u32[]{:S(2)}, u32[]{:S(2)}) collective-permute-start(f32[10,128,128]{2,1,0:T(8,128)} %get-tuple-element.39), channel_id=1, source_target_pairs={{1,2},{2,1},{5,6},{6,5},{9,10},{10,9},{13,14},{14,13},{17,18},{18,... | collective-permute-start | bytes 1966088 | tf_op jit(solution)/shard_map/ppermute | solution.py:409
  8.2 1.9 %prepare_now.1 = (f32[16,128,128]{2,1,0:T(8,128)S(1)}, f32[16,88,128]{2,1,0:T(8,128)}) custom-call(f32[1,1,2,16,128,128]{5,4,3,2,1,0:T(8,128)S(1)} %copy-done), custom_call_target="tpu_custom_call" | custom-call | tf_op jit(solution)/shard_map/prepare_now/pallas_call | solution.py:441
  10.0 1.2 %collective-permute-start.5 = (f32[16,88,128]{2,1,0:T(8,128)}, f32[16,88,128]{2,1,0:T(8,128)S(1)}, u32[]{:S(2)}, u32[]{:S(2)}) collective-permute-start(f32[16,88,128]{2,1,0:T(8,128)} %get-tuple-element.41), channel_id=1, source_target_pairs={{0,4},{4,0},{1,5},{5,1},{2,6},{6,2},{3,7},{7,3},{8,12},{12,8},{9,1... | collective-permute-start | bytes 2162696 | tf_op jit(solution)/shard_map/ppermute | solution.py:413
  11.2 0.8 prepare_rest.1
  12.1 0.0 collective-permute-done.got_a
  12.1 4.8 %collective-permute-done.1.got_b = f32[10,128,128]{2,1,0:T(8,128)S(1)} collective-permute-done((f32[10,128,128]{2,1,0:T(8,128)}, f32[10,128,128]{2,1,0:T(8,128)S(1)}, u32[]{:S(2)}, u32[]{:S(2)}) %collective-permute-start.1) | collective-permute-done | bytes 655392 | tf_op jit(solution)/shard_map/ppermute | solution.py:409
  16.9 5.8 %shard_map.37 = (f32[16,88,128]{2,1,0:T(8,128)}, f32[16,88,128]{2,1,0:T(8,128)S(1)}, f32[28,88,128]{2,1,0:T(8,128)S(1)}, f32[12,48,128]{2,1,0:T(8,128)S(1)}, f32...) custom-call(f32[16,128,128]{2,1,0:T(8,128)S(1)} %get-tuple-element.35.nowt.refs_3_, ...), custom_call_target="tpu_custom_call" | custom-call | flops 1 | bytes 8634368 | tf_op jit(solution)/shard_map/pallas_call | solution.py:31
  22.7 1.1 %copy-done.2 = f32[28,88,128]{2,1,0:T(8,128)} copy-done((f32[28,88,128]{2,1,0:T(8,128)}, f32[28,88,128]{2,1,0:T(8,128)S(1)}, u32[]{:S(2)}) %copy-start.2) | copy-done | bytes 1261592
  23.7 1.8 %collective-permute-start.2 = (f32[16,88,128]{2,1,0:T(8,128)}, f32[16,88,128]{2,1,0:T(8,128)S(1)}, u32[]{:S(2)}, u32[]{:S(2)}) collective-permute-start(f32[16,88,128]{2,1,0:T(8,128)} %get-tuple-element.40), channel_id=1, source_target_pairs={{0,4},{4,0},{1,5},{5,1},{2,6},{6,2},{3,7},{7,3},{8,12},{12,8},{9,1... | collective-permute-start | bytes 2162696 | tf_op jit(solution)/shard_map/ppermute | solution.py:413
  25.5 0.0 collective-permute-start.6
  25.5 3.1 %collective-permute-start.7 = (f32[12,88,128]{2,1,0:T(8,128)}, f32[12,88,128]{2,1,0:T(8,128)}, u32[]{:S(2)}, u32[]{:S(2)}) collective-permute-start(f32[12,88,128]{2,1,0:T(8,128)} %get-tuple-element.44), channel_id=1, source_target_pairs={{1,2},{2,1},{5,6},{6,5},{9,10},{10,9},{13,14},{14,13},{17,18},{18,... | collective-permute-start | bytes 1622024 | tf_op jit(solution)/shard_map/ppermute | solution.py:409
  28.7 0.9 slice.22
  29.6 0.0 collective-permute-done.5.refs_3_
  29.6 0.1 slice_select_fusion.2
  29.7 0.1 pad_maximum_fusion
  29.8 2.5 %collective-permute-start.9 = (f32[12,88,128]{2,1,0:T(8,128)S(1)}, f32[12,88,128]{2,1,0:T(8,128)S(1)}, u32[]{:S(2)}, u32[]{:S(2)}) collective-permute-start(f32[12,88,128]{2,1,0:T(8,128)S(1)} %get-tuple-element.69), channel_id=1, source_target_pairs={{1,2},{2,1},{5,6},{6,5},{9,10},{10,9},{13,14},{14,13},{17,18},{18,... | collective-permute-start | bytes 1622024 | tf_op jit(solution)/shard_map/ppermute | solution.py:409
  32.3 0.1 collective-permute-start.8
  32.4 0.0 collective-permute-done.6.refs_1_
  32.4 4.3 %collective-permute-done.7.refs_2_ = f32[12,88,128]{2,1,0:T(8,128)} collective-permute-done((f32[12,88,128]{2,1,0:T(8,128)}, f32[12,88,128]{2,1,0:T(8,128)}, u32[]{:S(2)}, u32[]{:S(2)}) %collective-permute-start.7) | collective-permute-done | bytes 540704 | tf_op jit(solution)/shard_map/ppermute | solution.py:409
  36.7 7.1 %shard_map.38 = (f32[24,88,128]{2,1,0:T(8,128)S(1)}, f32[16,88,128]{2,1,0:T(8,128)S(1)}, f32[8,80,128]{2,1,0:T(8,128)S(1)}, f32[8,80,128]{2,1,0:T(8,128)S(1)}, f32[28,88,128]{2,1,0:T(8,128)S(1)}) custom-call(f32[16,88,128]{2,1,0:T(8,128)S(1)} %get-tuple-element.42.refs_0_.refs_11_, f32[12,88,128]{2,1,0:T(8,128)} %collective-permute-done.6.refs_1_, ...), custom_call_target="tpu_custom_call" | custom-call | flops 1 | bytes 8126464 | tf_op jit(solution)/shard_map/pallas_call | solution.py:31
  43.8 0.1 collective-permute-start.10
  43.9 0.1 slice_select_fusion
  44.0 3.0 %collective-permute-start.4 = (f32[12,88,128]{2,1,0:T(8,128)S(1)}, f32[12,88,128]{2,1,0:T(8,128)S(1)}, u32[]{:S(2)}, u32[]{:S(2)}) collective-permute-start(f32[12,88,128]{2,1,0:T(8,128)S(1)} %get-tuple-element.67), channel_id=1, source_target_pairs={{1,2},{2,1},{5,6},{6,5},{9,10},{10,9},{13,14},{14,13},{17,18},{18,... | collective-permute-start | bytes 1622024 | tf_op jit(solution)/shard_map/ppermute | solution.py:409
  47.0 0.1 collective-permute-start.3
  47.1 2.6 %collective-permute-start.11 = (f32[8,80,128]{2,1,0:T(8,128)S(1)}, f32[8,80,128]{2,1,0:T(8,128)S(1)}, u32[]{:S(2)}, u32[]{:S(2)}) collective-permute-start(f32[8,80,128]{2,1,0:T(8,128)S(1)} %get-tuple-element.51), channel_id=1, source_target_pairs={{1,2},{2,1},{5,6},{6,5},{9,10},{10,9},{13,14},{14,13},{17,18},{18,... | collective-permute-start | bytes 983048 | tf_op jit(solution)/shard_map/ppermute | solution.py:409
  49.7 8.5 %collective-permute-done.11.refs_2_ = f32[8,80,128]{2,1,0:T(8,128)S(1)} collective-permute-done((f32[8,80,128]{2,1,0:T(8,128)S(1)}, f32[8,80,128]{2,1,0:T(8,128)S(1)}, u32[]{:S(2)}, u32[]{:S(2)}) %collective-permute-start.11) | collective-permute-done | bytes 327712 | tf_op jit(solution)/shard_map/ppermute | solution.py:409
  58.2 5.5 %shard_map.39 = (f32[24,80,128]{2,1,0:T(8,128)S(1)}, f32[16,80,128]{2,1,0:T(8,128)S(1)}, f32[4,72,128]{2,1,0:T(8,128)S(1)}, f32[4,72,128]{2,1,0:T(8,128)S(1)}) custom-call(f32[16,88,128]{2,1,0:T(8,128)S(1)} %get-tuple-element.49.refs_0_.refs_9_, f32[8,80,128]{2,1,0:T(8,128)S(1)} %collective-permute-done.10.refs_1_, ...), custom_call_target="tpu_custom_call" | custom-call | flops 1 | bytes 5947392 | tf_op jit(solution)/shard_map/pallas_call | solution.py:31
  63.8 0.0 collective-permute-done.4.refs_2_
  63.8 0.0 collective-permute-done.3.refs_1_
  63.8 10.2 %shard_map.40 = (f32[24,88,128]{2,1,0:T(8,128)S(1)}, f32[16,88,128]{2,1,0:T(8,128)S(1)}, f32[8,72,128]{2,1,0:T(8,128)S(1)}, f32[8,72,128]{2,1,0:T(8,128)S(1)}, f32[8,128,128]{2,1,0:T(8,128)S(1)}) custom-call(f32[16,88,128]{2,1,0:T(8,128)S(1)} %collective-permute-done.2.refs_0_, f32[12,88,128]{2,1,0:T(8,128)S(1)} %collective-permute-done.3.refs_1_, ...), custom_call_target="tpu_custom_call" | custom-call | flops 1 | bytes 11583488 | tf_op jit(solution)/shard_map/pallas_call | solution.py:31
  74.0 0.1 collective-permute-start.12
  74.0 2.9 %collective-permute-start.13 = (f32[8,72,128]{2,1,0:T(8,128)S(1)}, f32[8,72,128]{2,1,0:T(8,128)S(1)}, u32[]{:S(2)}, u32[]{:S(2)}) collective-permute-start(f32[8,72,128]{2,1,0:T(8,128)S(1)} %get-tuple-element.55), channel_id=1, source_target_pairs={{1,2},{2,1},{5,6},{6,5},{9,10},{10,9},{13,14},{14,13},{17,18},{18,... | collective-permute-start | bytes 884744 | tf_op jit(solution)/shard_map/ppermute | solution.py:409
  77.0 0.1 collective-permute-start.14
  77.1 2.6 %collective-permute-start.15 = (f32[4,72,128]{2,1,0:T(8,128)S(1)}, f32[4,72,128]{2,1,0:T(8,128)S(1)}, u32[]{:S(2)}, u32[]{:S(2)}) collective-permute-start(f32[4,72,128]{2,1,0:T(8,128)S(1)} %get-tuple-element.59), channel_id=1, source_target_pairs={{1,2},{2,1},{5,6},{6,5},{9,10},{10,9},{13,14},{14,13},{17,18},{18,... | collective-permute-start | bytes 442376 | tf_op jit(solution)/shard_map/ppermute | solution.py:409
  79.7 0.0 collective-permute-done.14.refs_1_
  79.7 4.0 %collective-permute-done.15.refs_2_ = f32[4,72,128]{2,1,0:T(8,128)S(1)} collective-permute-done((f32[4,72,128]{2,1,0:T(8,128)S(1)}, f32[4,72,128]{2,1,0:T(8,128)S(1)}, u32[]{:S(2)}, u32[]{:S(2)}) %collective-permute-start.15) | collective-permute-done | bytes 147488 | tf_op jit(solution)/shard_map/ppermute | solution.py:409
  83.7 2.4 %shard_map.41.refs_7_ = f32[16,72,128]{2,1,0:T(8,128)S(1)} custom-call(f32[16,80,128]{2,1,0:T(8,128)S(1)} %get-tuple-element.57.refs_0_.refs_6_, f32[4,72,128]{2,1,0:T(8,128)S(1)} %collective-permute-done.14.refs_1_, f32[4,72,128]{2,1,0:T(8,128)S(1)} %collective-permute-done.15.refs_2_, f32[24,80,128]{2,1,0:T(8,128)S(1)} %get-tuple-element.52.refs_10_.refs_3_, ...), custom_call_target="tpu_custom_call" | custom-call | flops 1 | bytes 4079616 | tf_op jit(solution)/shard_map/pallas_call | solution.py:31
  86.1 0.0 collective-permute-done.12.refs_1_
  86.1 7.3 %shard_map.42 = (f32[24,72,128]{2,1,0:T(8,128)}, f32[8,32,128]{2,1,0:T(8,128)S(1)}, f32[8,32,128]{2,1,0:T(8,128)S(1)}, f32[8,32,128]{2,1,0:T(8,128)S(1)}, f32[8,32,128]{2,1,0:T(8,128)S(1)}) custom-call(f32[16,88,128]{2,1,0:T(8,128)S(1)} %get-tuple-element.53.refs_0_, f32[8,72,128]{2,1,0:T(8,128)S(1)} %collective-permute-done.12.refs_1_, ...), custom_call_target="tpu_custom_call" | custom-call | flops 1 | bytes 7127040 | tf_op jit(solution)/shard_map/pallas_call | solution.py:31
  93.4 1.3 %collective-permute-start.16 = (f32[8,32,128]{2,1,0:T(8,128)S(1)}, f32[8,32,128]{2,1,0:T(8,128)S(1)}, u32[]{:S(2)}, u32[]{:S(2)}) collective-permute-start(f32[8,32,128]{2,1,0:T(8,128)S(1)} %get-tuple-element.62), channel_id=1, source_target_pairs={{0,8},{8,0},{16,24},{24,16},{1,9},{9,1},{17,25},{25,17},{2,10},{10... | collective-permute-start | bytes 393224 | tf_op jit(solution)/shard_map/ppermute | solution.py:513
  94.7 2.3 %collective-permute-start.17 = (f32[8,32,128]{2,1,0:T(8,128)S(1)}, f32[8,32,128]{2,1,0:T(8,128)S(1)}, u32[]{:S(2)}, u32[]{:S(2)}) collective-permute-start(f32[8,32,128]{2,1,0:T(8,128)S(1)} %get-tuple-element.63), channel_id=1, source_target_pairs={{0,16},{8,24},{16,0},{24,8},{1,17},{9,25},{17,1},{25,9},{2,18},{10... | collective-permute-start | bytes 393224 | tf_op jit(solution)/shard_map/ppermute | solution.py:513
  97.0 0.0 collective-permute-start.18
  97.0 2.4 %collective-permute-done.16.refs_1_ = f32[8,32,128]{2,1,0:T(8,128)S(1)} collective-permute-done((f32[8,32,128]{2,1,0:T(8,128)S(1)}, f32[8,32,128]{2,1,0:T(8,128)S(1)}, u32[]{:S(2)}, u32[]{:S(2)}) %collective-permute-start.16) | collective-permute-done | bytes 131104 | tf_op jit(solution)/shard_map/ppermute | solution.py:513
  99.4 4.1 %collective-permute-done.17.refs_2_ = f32[8,32,128]{2,1,0:T(8,128)S(1)} collective-permute-done((f32[8,32,128]{2,1,0:T(8,128)S(1)}, f32[8,32,128]{2,1,0:T(8,128)S(1)}, u32[]{:S(2)}, u32[]{:S(2)}) %collective-permute-start.17) | collective-permute-done | bytes 131104 | tf_op jit(solution)/shard_map/ppermute | solution.py:513
  103.5 1.3 %shard_map.43 = f32[16,32,64]{2,1,0:T(8,128)} custom-call(f32[8,32,128]{2,1,0:T(8,128)S(1)} %get-tuple-element.61.refs_0_, f32[8,32,128]{2,1,0:T(8,128)S(1)} %collective-permute-done.16.refs_1_, f32[8,32,128]{2,1,0:T(8,128)S(1)} %collective-permute-done.17.refs_2_, f32[8,32,128]{2,1,0:T(8,128)S(1)} %collective-permute-done.18.refs_3_), custom_call_target="tpu_custom_call" | custom-call | flops 1 | bytes 655360 | tf_op jit(solution)/shard_map/pallas_call | solution.py:31
  (14 shorter events, 0.0 us)
Async XLA Ops:
  0.0 8.1 %copy-start = (f32[1,1,2,16,128,128]{5,4,3,2,1,0:T(8,128)S(1)}, f32[1,1,2,16,128,128]{5,4,3,2,1,0:T(8,128)}, u32[]{:S(2)}) copy-start(f32[1,1,2,16,128,128]{5,4,3,2,1,0:T(8,128)} %states.1) | copy-start | bytes 6291460
  3.4 7.8 %copy-start.1 = (f32[16,128,128]{2,1,0:T(8,128)S(1)}, f32[16,128,128]{2,1,0:T(8,128)}, u32[]{:S(2)}) copy-start(f32[16,128,128]{2,1,0:T(8,128)} %courant.1) | copy-start | bytes 3145732
  3.4 8.7 %collective-permute-start = (f32[10,128,128]{2,1,0:T(8,128)}, f32[10,128,128]{2,1,0:T(8,128)S(1)}, u32[]{:S(2)}, u32[]{:S(2)}) collective-permute-start(f32[10,128,128]{2,1,0:T(8,128)} %get-tuple-element.38), channel_id=1, source_target_pairs={{0,1},{1,0},{2,3},{3,2},{4,5},{5,4},{6,7},{7,6},{8,9},{9,8},{10,11... | collective-permute-start | bytes 1966088 | tf_op jit(solution)/shard_map/ppermute | solution.py:410
  3.5 13.4 %collective-permute-start.1 = (f32[10,128,128]{2,1,0:T(8,128)}, f32[10,128,128]{2,1,0:T(8,128)S(1)}, u32[]{:S(2)}, u32[]{:S(2)}) collective-permute-start(f32[10,128,128]{2,1,0:T(8,128)} %get-tuple-element.39), channel_id=1, source_target_pairs={{1,2},{2,1},{5,6},{6,5},{9,10},{10,9},{13,14},{14,13},{17,18},{18,... | collective-permute-start | bytes 1966088 | tf_op jit(solution)/shard_map/ppermute | solution.py:409
  10.0 6.9 %copy-start.4 = (f32[1,12,16,128]{3,2,1,0:T(8,128)S(1)}, f32[1,12,16,128]{3,2,1,0:T(8,128)}, u32[]{:S(2)}) copy-start(f32[1,12,16,128]{3,2,1,0:T(8,128)} %rec.3) | copy-start | bytes 294916
  10.0 19.6 %collective-permute-start.5 = (f32[16,88,128]{2,1,0:T(8,128)}, f32[16,88,128]{2,1,0:T(8,128)S(1)}, u32[]{:S(2)}, u32[]{:S(2)}) collective-permute-start(f32[16,88,128]{2,1,0:T(8,128)} %get-tuple-element.41), channel_id=1, source_target_pairs={{0,4},{4,0},{1,5},{5,1},{2,6},{6,2},{3,7},{7,3},{8,12},{12,8},{9,1... | collective-permute-start | bytes 2162696 | tf_op jit(solution)/shard_map/ppermute | solution.py:413
  22.7 1.1 %copy-start.2 = (f32[28,88,128]{2,1,0:T(8,128)}, f32[28,88,128]{2,1,0:T(8,128)S(1)}, u32[]{:S(2)}) copy-start(f32[28,88,128]{2,1,0:T(8,128)S(1)} %get-tuple-element.45.refs_4_) | copy-start | bytes 3784708
  23.7 20.2 %collective-permute-start.2 = (f32[16,88,128]{2,1,0:T(8,128)}, f32[16,88,128]{2,1,0:T(8,128)S(1)}, u32[]{:S(2)}, u32[]{:S(2)}) collective-permute-start(f32[16,88,128]{2,1,0:T(8,128)} %get-tuple-element.40), channel_id=1, source_target_pairs={{0,4},{4,0},{1,5},{5,1},{2,6},{6,2},{3,7},{7,3},{8,12},{12,8},{9,1... | collective-permute-start | bytes 2162696 | tf_op jit(solution)/shard_map/ppermute | solution.py:413
  25.5 6.9 %collective-permute-start.6 = (f32[12,88,128]{2,1,0:T(8,128)}, f32[12,88,128]{2,1,0:T(8,128)}, u32[]{:S(2)}, u32[]{:S(2)}) collective-permute-start(f32[12,88,128]{2,1,0:T(8,128)} %get-tuple-element.43), channel_id=1, source_target_pairs={{0,1},{1,0},{2,3},{3,2},{4,5},{5,4},{6,7},{7,6},{8,9},{9,8},{10,11... | collective-permute-start | bytes 1622024 | tf_op jit(solution)/shard_map/ppermute | solution.py:410
  25.5 11.2 %collective-permute-start.7 = (f32[12,88,128]{2,1,0:T(8,128)}, f32[12,88,128]{2,1,0:T(8,128)}, u32[]{:S(2)}, u32[]{:S(2)}) collective-permute-start(f32[12,88,128]{2,1,0:T(8,128)} %get-tuple-element.44), channel_id=1, source_target_pairs={{1,2},{2,1},{5,6},{6,5},{9,10},{10,9},{13,14},{14,13},{17,18},{18,... | collective-permute-start | bytes 1622024 | tf_op jit(solution)/shard_map/ppermute | solution.py:409
  29.7 7.0 %copy-start.3 = (f32[28,88,128]{2,1,0:T(8,128)S(1)}, f32[28,88,128]{2,1,0:T(8,128)}, u32[]{:S(2)}) copy-start(f32[28,88,128]{2,1,0:T(8,128)} %copy-done.2) | copy-start | bytes 3784708
  29.8 34.0 %collective-permute-start.9 = (f32[12,88,128]{2,1,0:T(8,128)S(1)}, f32[12,88,128]{2,1,0:T(8,128)S(1)}, u32[]{:S(2)}, u32[]{:S(2)}) collective-permute-start(f32[12,88,128]{2,1,0:T(8,128)S(1)} %get-tuple-element.69), channel_id=1, source_target_pairs={{1,2},{2,1},{5,6},{6,5},{9,10},{10,9},{13,14},{14,13},{17,18},{18,... | collective-permute-start | bytes 1622024 | tf_op jit(solution)/shard_map/ppermute | solution.py:409
  32.3 31.4 %collective-permute-start.8 = (f32[12,88,128]{2,1,0:T(8,128)S(1)}, f32[12,88,128]{2,1,0:T(8,128)S(1)}, u32[]{:S(2)}, u32[]{:S(2)}) collective-permute-start(f32[12,88,128]{2,1,0:T(8,128)S(1)} %get-tuple-element.70), channel_id=1, source_target_pairs={{0,1},{1,0},{2,3},{3,2},{4,5},{5,4},{6,7},{7,6},{8,9},{9,8},{10,11... | collective-permute-start | bytes 1622024 | tf_op jit(solution)/shard_map/ppermute | solution.py:410
  43.8 3.2 %collective-permute-start.10 = (f32[8,80,128]{2,1,0:T(8,128)S(1)}, f32[8,80,128]{2,1,0:T(8,128)S(1)}, u32[]{:S(2)}, u32[]{:S(2)}) collective-permute-start(f32[8,80,128]{2,1,0:T(8,128)S(1)} %get-tuple-element.50), channel_id=1, source_target_pairs={{0,1},{1,0},{2,3},{3,2},{4,5},{5,4},{6,7},{7,6},{8,9},{9,8},{10,11... | collective-permute-start | bytes 983048 | tf_op jit(solution)/shard_map/ppermute | solution.py:410
  44.0 19.8 %collective-permute-start.4 = (f32[12,88,128]{2,1,0:T(8,128)S(1)}, f32[12,88,128]{2,1,0:T(8,128)S(1)}, u32[]{:S(2)}, u32[]{:S(2)}) collective-permute-start(f32[12,88,128]{2,1,0:T(8,128)S(1)} %get-tuple-element.67), channel_id=1, source_target_pairs={{1,2},{2,1},{5,6},{6,5},{9,10},{10,9},{13,14},{14,13},{17,18},{18,... | collective-permute-start | bytes 1622024 | tf_op jit(solution)/shard_map/ppermute | solution.py:409
  47.0 16.8 %collective-permute-start.3 = (f32[12,88,128]{2,1,0:T(8,128)S(1)}, f32[12,88,128]{2,1,0:T(8,128)S(1)}, u32[]{:S(2)}, u32[]{:S(2)}) collective-permute-start(f32[12,88,128]{2,1,0:T(8,128)S(1)} %get-tuple-element.68), channel_id=1, source_target_pairs={{0,1},{1,0},{2,3},{3,2},{4,5},{5,4},{6,7},{7,6},{8,9},{9,8},{10,11... | collective-permute-start | bytes 1622024 | tf_op jit(solution)/shard_map/ppermute | solution.py:410
  47.1 11.1 %collective-permute-start.11 = (f32[8,80,128]{2,1,0:T(8,128)S(1)}, f32[8,80,128]{2,1,0:T(8,128)S(1)}, u32[]{:S(2)}, u32[]{:S(2)}) collective-permute-start(f32[8,80,128]{2,1,0:T(8,128)S(1)} %get-tuple-element.51), channel_id=1, source_target_pairs={{1,2},{2,1},{5,6},{6,5},{9,10},{10,9},{13,14},{14,13},{17,18},{18,... | collective-permute-start | bytes 983048 | tf_op jit(solution)/shard_map/ppermute | solution.py:409
  74.0 12.1 %collective-permute-start.12 = (f32[8,72,128]{2,1,0:T(8,128)S(1)}, f32[8,72,128]{2,1,0:T(8,128)S(1)}, u32[]{:S(2)}, u32[]{:S(2)}) collective-permute-start(f32[8,72,128]{2,1,0:T(8,128)S(1)} %get-tuple-element.54), channel_id=1, source_target_pairs={{0,1},{1,0},{2,3},{3,2},{4,5},{5,4},{6,7},{7,6},{8,9},{9,8},{10,11... | collective-permute-start | bytes 884744 | tf_op jit(solution)/shard_map/ppermute | solution.py:410
  74.0 12.0 %collective-permute-start.13 = (f32[8,72,128]{2,1,0:T(8,128)S(1)}, f32[8,72,128]{2,1,0:T(8,128)S(1)}, u32[]{:S(2)}, u32[]{:S(2)}) collective-permute-start(f32[8,72,128]{2,1,0:T(8,128)S(1)} %get-tuple-element.55), channel_id=1, source_target_pairs={{1,2},{2,1},{5,6},{6,5},{9,10},{10,9},{13,14},{14,13},{17,18},{18,... | collective-permute-start | bytes 884744 | tf_op jit(solution)/shard_map/ppermute | solution.py:409
  77.0 2.7 %collective-permute-start.14 = (f32[4,72,128]{2,1,0:T(8,128)S(1)}, f32[4,72,128]{2,1,0:T(8,128)S(1)}, u32[]{:S(2)}, u32[]{:S(2)}) collective-permute-start(f32[4,72,128]{2,1,0:T(8,128)S(1)} %get-tuple-element.58), channel_id=1, source_target_pairs={{0,1},{1,0},{2,3},{3,2},{4,5},{5,4},{6,7},{7,6},{8,9},{9,8},{10,11... | collective-permute-start | bytes 442376 | tf_op jit(solution)/shard_map/ppermute | solution.py:410
  77.1 6.6 %collective-permute-start.15 = (f32[4,72,128]{2,1,0:T(8,128)S(1)}, f32[4,72,128]{2,1,0:T(8,128)S(1)}, u32[]{:S(2)}, u32[]{:S(2)}) collective-permute-start(f32[4,72,128]{2,1,0:T(8,128)S(1)} %get-tuple-element.59), channel_id=1, source_target_pairs={{1,2},{2,1},{5,6},{6,5},{9,10},{10,9},{13,14},{14,13},{17,18},{18,... | collective-permute-start | bytes 442376 | tf_op jit(solution)/shard_map/ppermute | solution.py:409
  93.4 6.0 %collective-permute-start.16 = (f32[8,32,128]{2,1,0:T(8,128)S(1)}, f32[8,32,128]{2,1,0:T(8,128)S(1)}, u32[]{:S(2)}, u32[]{:S(2)}) collective-permute-start(f32[8,32,128]{2,1,0:T(8,128)S(1)} %get-tuple-element.62), channel_id=1, source_target_pairs={{0,8},{8,0},{16,24},{24,16},{1,9},{9,1},{17,25},{25,17},{2,10},{10... | collective-permute-start | bytes 393224 | tf_op jit(solution)/shard_map/ppermute | solution.py:513
  94.7 8.8 %collective-permute-start.17 = (f32[8,32,128]{2,1,0:T(8,128)S(1)}, f32[8,32,128]{2,1,0:T(8,128)S(1)}, u32[]{:S(2)}, u32[]{:S(2)}) collective-permute-start(f32[8,32,128]{2,1,0:T(8,128)S(1)} %get-tuple-element.63), channel_id=1, source_target_pairs={{0,16},{8,24},{16,0},{24,8},{1,17},{9,25},{17,1},{25,9},{2,18},{10... | collective-permute-start | bytes 393224 | tf_op jit(solution)/shard_map/ppermute | solution.py:513
  97.0 6.5 %collective-permute-start.18 = (f32[8,32,128]{2,1,0:T(8,128)S(1)}, f32[8,32,128]{2,1,0:T(8,128)S(1)}, u32[]{:S(2)}, u32[]{:S(2)}) collective-permute-start(f32[8,32,128]{2,1,0:T(8,128)S(1)} %get-tuple-element.64), channel_id=1, source_target_pairs={{0,24},{8,16},{16,8},{24,0},{1,25},{9,17},{17,9},{25,1},{2,26},{10... | collective-permute-start | bytes 393224 | tf_op jit(solution)/shard_map/ppermute | solution.py:513

commit v4 on v3

--- a/solution.py
+++ b/solution.py
@@ -72,7 +72,7 @@
     top, bottom = sub < 1, sub >= 7
     zero = jnp.zeros((8, 128), F32)
 
-    @pl.loop(0, count, step=GROUP)
+    @pl.loop(0, count, step=GROUP, unroll=True)
     def _(k):
         x = first + k
         flat = field[pl.ds(x, GROUP)].reshape(GROUP * width * 8, 128)
@@ -107,26 +107,34 @@
     return jnp.where(sub < 1, jnp.broadcast_to(row, (8, 128)), 0.0)
 
 
-def pack(states, courant, rec, send_a, send_b, sems):
+def pack(states, courant, rec, send_a, send_b, held_a, held_b, sems):
     n = courant.shape[0]
     odd = parity()
     copies = []
-    for index, (send, high) in enumerate(((send_a, odd == 0), (send_b, odd == 1))):
+    for index, (send, held, high) in enumerate(((send_a, held_a, odd == 0), (send_b, held_b, odd == 1))):
         at = lambda h: jnp.where(high, n - h, 0)
-        moves = [
-            (states.at[0, 0, 1, pl.ds(at(4), 4)], send.at[pl.ds(0, 4)]),
-            (states.at[0, 0, 0, pl.ds(at(2), 2)], send.at[pl.ds(4, 2)]),
-            (courant.at[pl.ds(at(2), 2)], send.at[pl.ds(6, 2)]),
-        ]
+        moves = (
+            (states.at[0, 0, 1, pl.ds(at(4), 4)], 0, 4),
+            (states.at[0, 0, 0, pl.ds(at(2), 2)], 4, 2),
+            (courant.at[pl.ds(at(2), 2)], 6, 2),
+        )
+        for k, (source, start, count) in enumerate(moves):
+            part = held.at[pl.ds(start, count)]
+            come = pltpu.make_async_copy(source, part, sems.at[index, 0, k])
+            come.start()
+            leave = pltpu.make_async_copy(part, send.at[pl.ds(start, count)], sems.at[index, 1, k])
+            copies.append((come, leave))
         first = pl.multiple_of(at(HR), HR)
         for k in range(STEPS):
-            send[REC + k // PER, HR * (k % PER) : HR * (k % PER + 1), :] = rec[0, k, pl.ds(first, HR), :]
-        for k, (source, target) in enumerate(moves):
-            copy = pltpu.make_async_copy(source, target, sems.at[index, k])
-            copy.start()
-            copies.append(copy)
-    for copy in copies:
-        copy.wait()
+            held[REC + k // PER, HR * (k % PER) : HR * (k % PER + 1), :] = rec[0, k, pl.ds(first, HR), :]
+        tail = pl.ds(REC, FIRST - REC)
+        copies.append((None, pltpu.make_async_copy(held.at[tail], send.at[tail], sems.at[index, 1, 3])))
+    for come, leave in copies:
+        if come is not None:
+            come.wait()
+        leave.start()
+    for _, leave in copies:
+        leave.wait()
 
 
 def prepare_now(now, nowt, give):
@@ -148,7 +156,7 @@
 
 
 def first_block(nowt, oldt, coeft, rec, got_a, got_b,
-                give, one, near, rfull, send_a, send_b,
+                give, one, rfull, send_a, send_b,
                 cur, old, mid, new, cx, band, raw_a, raw_b, plain):
     n = nowt.shape[0]
     odd, role = parity(), lax.axis_index("pair")
@@ -158,12 +166,11 @@
     other = pl.multiple_of((1 - role) * (128 - rows), 8)
     fill_band(band)
 
-    @pl.loop(0, n)
+    @pl.loop(0, n, unroll=4)
     def _(x):
         load(cur, x + 4, nowt, x, 0, 16)
         load(old, x + 2, oldt, x, 0, 16)
         load(cx, x + 2, coeft, x, 0, 16)
-        near[x + 2] = coeft[x, pl.ds(base, rows), :]
 
     for raw, turned in ((got_a, raw_a), (got_b, raw_b)):
         for k in range(REC):
@@ -179,14 +186,12 @@
 
     a4, b4 = place(odd, n, 4, 4)
     a2, b2 = place(odd, n, 2, 2)
-    for got, at4, at2, spot in ((raw_a, a4, a2, n + 4), (raw_b, b4, b2, n + 8)):
+    for got, at4, at2 in ((raw_a, a4, a2), (raw_b, b4, b2)):
         for k in range(4):
             load(cur, at4 + k, got, k, 0, 16)
-            near[spot + k] = got[k, pl.ds(base, rows), :]
         for k in range(2):
             load(old, at2 + k, got, 4 + k, 0, 16)
             load(cx, at2 + k, got, 6 + k, 0, 16)
-            near[at2 + k] = got[6 + k, pl.ds(base, rows), :]
 
     def put0(x, j, v, change):
         value = (v + v) - old[x, j] + change
@@ -204,7 +209,7 @@
 
     sweep(mid, cx, band, 2, n, 2, put1)
 
-    @pl.loop(0, n)
+    @pl.loop(0, n, unroll=4)
     def _(x):
         store(plain, x, new, x, 16)
         one[x] = plain[x, pl.ds(base, rows), :]
@@ -212,9 +217,9 @@
 
     pack_ends(one, send_a, send_b, odd, role, DEPTH)
     for send, high in ((send_a, odd == 0), (send_b, odd == 1)):
-        start = jnp.where(high, n - HC, 2) + 2
+        start = jnp.where(high, n - HC, 2)
         for k in range(HC - 2):
-            send[DEPTH + k] = near[start + k]
+            send[DEPTH + k] = coeft[start + k, pl.ds(base, rows), :]
 
 
 def pack_ends(field, send_a, send_b, odd, role, depth):
@@ -223,7 +228,7 @@
     high = n - depth
     for send, start in ((send_a, jnp.where(odd == 0, high, 0)), (send_b, jnp.where(odd == 0, 0, high))):
 
-        @pl.loop(0, depth)
+        @pl.loop(0, depth, unroll=4)
         def _(k):
             send[k] = field[start + k, pl.ds(base, rows), :]
 
@@ -232,7 +237,7 @@
     it = iter(refs)
     take = lambda count: [next(it) for _ in range(count)]
     u, got_a, got_b, was, coef, rfull = take(6)
-    was_a, was_b = take(2) if fresh and lit else (None, None)
+    was_a, was_b = take(2) if fresh else (None, None)
     mates = take(steps) if lit else []
     first_mate = take(1)[0] if lit and fresh else None
     image_in = take(1)[0] if lit and not fresh else None
@@ -244,6 +249,7 @@
     pieces = take(shots) if lit and last else []
     cur, old, mid, cx, band = take(5)
     third = take(1)[0] if steps == 3 else None
+    turned = take(2) if fresh and not lit else []
     if lit and last:
         out, image = take(2)
 
@@ -258,57 +264,66 @@
         return pl.multiple_of(role * (ref.shape[1] - rows), 8)
 
     if fresh and not lit:
-        was_a, was_b = coef.at[pl.ds(n + 4, 4)], coef.at[pl.ds(n + 8, 4)]
-
-        @pl.loop(0, n + 4)
+        base = window(coef)
+        at_a, at_b = place(odd, n, HC, 2)
+        far_a, far_b = place(odd, n + 4, HC - 2, HC - 2)
+
+        @pl.loop(0, n, unroll=4)
         def _(x):
-            whole[x + HC - 2] = coef[x]
-
-        at_a, at_b = place(odd, n + 4, HC - 2, HC - 2)
-        for k in range(HC - 2):
-            whole[at_a + k] = got_a[DEPTH + k]
-            whole[at_b + k] = got_b[DEPTH + k]
+            whole[x + HC] = coef[x, pl.ds(base, rows), :]
+
+        for raw, plain, got, at, far in (
+            (was_a, turned[0], got_a, at_a, far_a), (was_b, turned[1], got_b, at_b, far_b)
+        ):
+            for k in range(4):
+                plain[k] = raw[k].T
+            for k in range(2):
+                plain[4 + k] = raw[6 + k].T * (1.0 / 12.0)
+                whole[at + k] = plain[4 + k, pl.ds(base, rows), :]
+            for k in range(HC - 2):
+                whole[far + k] = got[DEPTH + k]
+        was_a, was_b = turned
 
     reach_old = halo - 4
     if fresh:
-        @pl.loop(0, n)
+        @pl.loop(0, n, unroll=4)
         def _(x):
             load(old, x + reach_old, was, x, window(was), width)
 
         old_a, old_b = place(odd, n, reach_old, reach_old)
 
-        @pl.loop(0, reach_old)
+        @pl.loop(0, reach_old, unroll=4)
         def _(k):
             load(old, old_a + k, was_a, k, window(was_a), width)
             load(old, old_b + k, was_b, k, window(was_b), width)
     else:
         shift = (was.shape[0] - n) // 2 - reach_old
 
-        @pl.loop(0, n + 2 * reach_old)
+        @pl.loop(0, n + 2 * reach_old, unroll=4)
         def _(x):
             load(old, x, was, x + shift, window(was), width)
 
     beyond = max(halo - 2 - HC, 0)
 
-    @pl.loop(0, n + 2 * min(halo - 2, HC))
+    @pl.loop(0, n + 2 * min(halo - 2, HC), unroll=4)
     def _(x):
         load(cx, x + beyond, whole, x + max(HC - (halo - 2), 0), window(whole), width)
 
     if beyond:
         at_a, at_b = place(odd, n + 2 * HC, beyond, beyond)
 
-        @pl.loop(0, beyond)
+        @pl.loop(0, beyond, unroll=4)
         def _(k):
             load(cx, at_a + k, was_a, reach_old + k, window(was_a), width)
             load(cx, at_b + k, was_b, reach_old + k, window(was_b), width)
 
-    @pl.loop(0, n)
+    @pl.loop(0, n, unroll=4)
     def _(x):
         load(cur, x + halo, u, x, window(u), width)
 
     at_a, at_b = place(odd, n, halo, halo)
 
-    @pl.loop(0, halo)
+    @pl.loop(0, halo, unroll=4)
     def _(k):
         load(cur, at_a + k, got_a, k, 0, width)
         load(cur, at_b + k, got_b, k, 0, width)
@@ -338,7 +353,7 @@
         target = (third, inner, out)[3 - steps + s]
         skip = (reach - 4) - (target.shape[0] - n) // 2
 
-        @pl.loop(0, target.shape[0])
+        @pl.loop(0, target.shape[0], unroll=4)
         def _(x):
             store(target, x, before, x + skip, width)
 
@@ -352,7 +367,7 @@
         half, pairs = 64, n // 2
         mine = [third, inner, out][3 - steps :]
 
-        @pl.loop(0, pairs)
+        @pl.loop(0, pairs, unroll=4)
         def _(k):
             for side in range(2):
                 x = k + side * pairs
@@ -375,7 +390,7 @@
             piece = 128 // shots
             weight = IMAGE_EVERY / STEPS
 
-            @pl.loop(0, pairs)
+            @pl.loop(0, pairs, unroll=4)
             def _(k):
                 image[k] = image[k].T * weight
                 for index in range(shots):
@@ -383,11 +398,25 @@
                     pieces[index][k] = image[k, pl.ds(pl.multiple_of(target * piece, 8), piece), :]
 
 
+def ends(field, *refs):
+    *coef, send_a, send_b = refs
+    odd, role = parity(), lax.axis_index("pair")
+    n, rows = field.shape[0], field.shape[1]
+    depth = send_a.shape[0] - MORE * len(coef)
+    pack_ends(field, send_a, send_b, odd, role, depth)
+    if coef:
+        base = pl.multiple_of(role * (128 - rows), 8)
+        for send, high in ((send_a, odd == 0), (send_b, odd == 1)):
+            start = jnp.where(high, n - HC - MORE, HC)
+            for k in range(MORE):
+                send[depth + k] = coef[0][start + k, pl.ds(base, rows), :]
+
+
 def combine(count, *refs):
     out = refs[count]
     pairs = refs[0].shape[0]
 
-    @pl.loop(0, pairs)
+    @pl.loop(0, pairs, unroll=4)
     def _(k):
         total = refs[0][k]
         for index in range(1, count):
@@ -412,11 +441,6 @@
     def across(value):
         return lax.ppermute(value, "pair", [(0, 1), (1, 0)])
 
-    def ends(value, depth, skip=0):
-        low, high = value[skip : skip + depth], value[n - skip - depth : n - skip]
-        high_first = odd == 0
-        return jnp.where(high_first, high, low), jnp.where(high_first, low, high)
-
     wide, mid_rows, thin = 88, 80, 72
     band = pltpu.VMEM((256, 128), jnp.bfloat16)
     hbm = pl.BlockSpec(memory_space=pltpu.HBM)
@@ -425,12 +449,12 @@
         pack,
         out_shape=(sds(FIRST, 128, 128),) * 2,
         in_specs=[hbm, hbm, VM],
-        out_specs=[VM, VM],
-        scratch_shapes=[pltpu.SemaphoreType.DMA((2, 3))],
+        out_specs=[hbm, hbm],
+        scratch_shapes=[pltpu.VMEM((FIRST, 128, 128), F32)] * 2 + [pltpu.SemaphoreType.DMA((2, 2, 4))],
         compiler_params=pltpu.CompilerParams(vmem_limit_bytes=58 << 20),
         name="pack",
     )(states, courant, records)
-    got_a, got_b = swap(send_a, send_b)
+    first_a, first_b = swap(send_a, send_b)
 
     def state_block(index):
         return pl.BlockSpec((1, 1, 1, GROUP, 128, 128), lambda i: (0, 0, index, i, 0, 0))
@@ -457,13 +481,13 @@
         compiler_params=pltpu.CompilerParams(vmem_limit_bytes=6 << 20),
         name="prepare_rest",
     )(states, courant)
-    give_one, one, near, rfull, send_a, send_b = call(
+    give_one, one, rfull, send_a, send_b = call(
         first_block,
-        (sds(n, wide, 128), sds(n, wide, 128), sds(n + 12, wide, 128), sds(STEPS, n + 2 * HR, 128),
+        (sds(n, wide, 128), sds(n, wide, 128), sds(STEPS, n + 2 * HR, 128),
          sds(DEPTH + HC - 2, wide, 128), sds(DEPTH + HC - 2, wide, 128)),
         [ext_ref(n + 8, 128), ext_ref(n + 4, 128), ext_ref(n + 4, 128), ext_ref(n, 128), ext_ref(n + 4, 128), band]
         + [pltpu.VMEM((REC, 128, 128), F32)] * 2 + [pltpu.VMEM((n, 128, 128), F32)],
-        nowt, oldt, coeft, records, got_a, got_b, limit=12,
+        nowt, oldt, coeft, records, first_a, first_b, limit=12,
     )
     other_one = across(give_one)
 
@@ -484,6 +508,8 @@
                    ext_ref(n + 2 * (halo - 2), rows), band]
         if steps == 3:
             scratch.append(pltpu.VMEM((n, rows, 128), F32))
+        if fresh and not lit:
+            scratch += [pltpu.VMEM((6, 128, 128), F32)] * 2
         if lit and last:
             scratch += [pltpu.VMEM((n, rows, 128), F32), pltpu.VMEM((n // 2, 128, 128), F32)]
         kernel = functools.partial(block, rows, steps, tick, lit, fresh, last, shots)
@@ -491,16 +517,17 @@
 
     got = swap(send_a, send_b)
     three, five, send_a, send_b, cfull = run(
-        wide, 2, 1, False, True, False, 8, mid_rows, one, *got, nowt, near, rfull)
+        wide, 2, 1, False, True, False, 8, mid_rows, one, *got, nowt, coeft, rfull, first_a, first_b)
     got = swap(send_a, send_b)
     seven, nine, send_a, send_b = run(
         mid_rows, 2, 5, False, False, False, 4, thin, five, *got, three, cfull, rfull)
     got = swap(send_a, send_b)
     (eleven,) = run(thin, 1, 9, False, False, True, 0, 0, nine, *got, seven, cfull, rfull)
 
-    was_ends, coef_ends = ends(other_was, 8), ends(near[2 : 2 + n], MORE, HC)
-    got_was = swap(*(jnp.concatenate(pair) for pair in zip(was_ends, coef_ends)))
-    got = swap(*ends(other_one, 12))
+    send_a, send_b = call(ends, (sds(DEPTH + MORE, wide, 128),) * 2, [], other_was, coeft, limit=5)
+    got_was = swap(send_a, send_b)
+    send_a, send_b = call(ends, (sds(12, wide, 128),) * 2, [], other_one, limit=5)
+    got = swap(send_a, send_b)
     o_five, o_seven, send_a, send_b, image = run(
         wide, 3, 1, True, True, False, 8, thin,
         other_one, *got, other_was, cfull, rfull, *got_was, three, five, seven, one)

time: 105 us -> 94.4 us (0.90)
  Pallas kernels: 45.7 us -> 29 us
  waiting for transfers between devices: 28.1 us -> 35 us
  local copies, waits for them, and re-layouts: 2.02 us -> 0.02 us
  starting transfers between devices: 28.5 us -> 29.7 us
    pallas_call x7 -> x9, Pallas kernels: 39.6 us -> 24.3 us  [call(): pl.pallas_call(kernel, out_shape=outs, in_specs=[VM] * len(args), out_spe...]
    ppermute x7, waiting for transfers between devices: 21.6 us -> 28.6 us  [swap(): got_b = lax.ppermute(send_b, 'space', pairs_b)]
    pallas_call x1, Pallas kernels: 1.86 us -> 0.66 us  [on_device(): pl.pallas_call(prepare_now, grid=(n // GROUP,), out_shape=(sds(n, 128, 12...]
    unnamed x10 -> x6, local copies, waits for them, and re-layouts: 1.09 us -> 0.02 us
  transfers between devices with their start and end apart: 19 -> 19, of which waited for: 6 -> 6; matrix products, arithmetic and copies ran while one was open for 1% -> 0% of each run, Pallas kernels for 22% -> 15%
where the time goes in v4:
time: 94.4 us; the launch traced here: 94.1 us
  waiting for transfers between devices  35 us (37%)
  starting transfers between devices  29.7 us (31%)
  Pallas kernels  29 us (31%)
    ppermute x7, waiting for transfers between devices, swap(): got_b = lax.ppermute(send_b, 'space', pairs_b)  28.6 us
    pallas_call x9, Pallas kernels, call(): pl.pallas_call(kernel, out_shape=outs, in_specs=[VM] * len(args), out_spe...  24.3 us
    ppermute x7, starting transfers between devices, swap(): got_b = lax.ppermute(send_b, 'space', pairs_b)  22.1 us
    ppermute x3, waiting for transfers between devices, on_device(): lax.ppermute(pieces[index], 'shot', [(i, i ^ index) for i in range(shots)])  6.38 us
    ppermute x3, starting transfers between devices, on_device(): lax.ppermute(pieces[index], 'shot', [(i, i ^ index) for i in range(shots)])  3.62 us
    pallas_call x1, Pallas kernels, on_device(): pl.pallas_call(pack, out_shape=(sds(FIRST, 128, 128),) * 2, in_specs=[hbm...  3.23 us
    ppermute x2, starting transfers between devices, across(): return lax.ppermute(value, 'pair', [(0, 1), (1, 0)])  3.09 us
  transfers between devices with their start and end apart: 19, of which 6 were waited for; matrix products, arithmetic and copies ran while one was open for 0% of the time, Pallas kernels for 15%

profile of v4, /device:TPU:1, one launch (start us, length us, event | category | flops | bytes accessed | tf_op | source)
XLA Modules:
  0.0 94.1 jit_solution(6116574759763915268)
XLA Ops:
  0.0 3.2 %pack.1 = (f32[10,128,128]{2,1,0:T(8,128)}, f32[10,128,128]{2,1,0:T(8,128)}) custom-call(f32[1,1,2,16,128,128]{5,4,3,2,1,0:T(8,128)} %states.1, f32[16,128,128]{2,1,0:T(8,128)} %courant.1, f32[1,12,16,128]{3,2,1,0:T(8,128)} %rec.3), custom_call_target="tpu_custom_call" | custom-call | tf_op jit(solution)/shard_map/pack/pallas_call | solution.py:448
  3.2 0.0 copy-start.1
  3.2 0.1 collective-permute-start
  3.3 4.6 %collective-permute-start.1 = (f32[10,128,128]{2,1,0:T(8,128)}, f32[10,128,128]{2,1,0:T(8,128)S(1)}, u32[]{:S(2)}, u32[]{:S(2)}) collective-permute-start(f32[10,128,128]{2,1,0:T(8,128)} %get-tuple-element.42), channel_id=1, source_target_pairs={{1,2},{2,1},{5,6},{6,5},{9,10},{10,9},{13,14},{14,13},{17,18},{18,... | collective-permute-start | bytes 1966088 | tf_op jit(solution)/shard_map/ppermute | solution.py:438
  8.0 0.7 prepare_now.1
  8.6 0.0 copy-start.2
  8.6 1.3 %collective-permute-start.5 = (f32[16,88,128]{2,1,0:T(8,128)S(1)}, f32[16,88,128]{2,1,0:T(8,128)S(1)}, u32[]{:S(2)}, u32[]{:S(2)}) collective-permute-start(f32[16,88,128]{2,1,0:T(8,128)S(1)} %get-tuple-element.46), channel_id=1, source_target_pairs={{0,4},{4,0},{1,5},{5,1},{2,6},{6,2},{3,7},{7,3},{8,12},{12,8},{9,1... | collective-permute-start | bytes 2162696 | tf_op jit(solution)/shard_map/ppermute | solution.py:442
  9.9 0.8 prepare_rest.1
  10.8 0.0 collective-permute-done.got_a.refs_6_
  10.8 5.9 %collective-permute-done.1.got_b.refs_7_ = f32[10,128,128]{2,1,0:T(8,128)S(1)} collective-permute-done((f32[10,128,128]{2,1,0:T(8,128)}, f32[10,128,128]{2,1,0:T(8,128)S(1)}, u32[]{:S(2)}, u32[]{:S(2)}) %collective-permute-start.1) | collective-permute-done | bytes 655392 | tf_op jit(solution)/shard_map/ppermute | solution.py:438
  16.7 3.7 %shard_map.37 = (f32[16,88,128]{2,1,0:T(8,128)S(1)}, f32[16,88,128]{2,1,0:T(8,128)S(1)}, f32[12,48,128]{2,1,0:T(8,128)S(1)}, f32[12,88,128]{2,1,0:T(8,128)S(1)}, f32[12,88,128]{2,1,0:T(8,128)S(1)}) custom-call(f32[16,128,128]{2,1,0:T(8,128)S(1)} %get-tuple-element.38.nowt.refs_3_, f32[16,128,128]{2,1,0:T(8,128)S(1)} %get-tuple-element.39.oldt, ...), custom_call_target="tpu_custom_call" | custom-call | flops 1 | bytes 7372800 | tf_op jit(solution)/shard_map/pallas_call | solution.py:31
  20.5 1.8 %collective-permute-start.2 = (f32[16,88,128]{2,1,0:T(8,128)S(1)}, f32[16,88,128]{2,1,0:T(8,128)S(1)}, u32[]{:S(2)}, u32[]{:S(2)}) collective-permute-start(f32[16,88,128]{2,1,0:T(8,128)S(1)} %get-tuple-element.43), channel_id=1, source_target_pairs={{0,4},{4,0},{1,5},{5,1},{2,6},{6,2},{3,7},{7,3},{8,12},{12,8},{9,1... | collective-permute-start | bytes 2162696 | tf_op jit(solution)/shard_map/ppermute | solution.py:442
  22.3 0.0 collective-permute-start.6
  22.3 3.1 %collective-permute-start.7 = (f32[12,88,128]{2,1,0:T(8,128)S(1)}, f32[12,88,128]{2,1,0:T(8,128)S(1)}, u32[]{:S(2)}, u32[]{:S(2)}) collective-permute-start(f32[12,88,128]{2,1,0:T(8,128)S(1)} %get-tuple-element.49), channel_id=1, source_target_pairs={{1,2},{2,1},{5,6},{6,5},{9,10},{10,9},{13,14},{14,13},{17,18},{18,... | collective-permute-start | bytes 1622024 | tf_op jit(solution)/shard_map/ppermute | solution.py:438
  25.4 0.0 collective-permute-done.6.refs_1_
  25.4 7.8 %collective-permute-done.7.refs_2_ = f32[12,88,128]{2,1,0:T(8,128)S(1)} collective-permute-done((f32[12,88,128]{2,1,0:T(8,128)S(1)}, f32[12,88,128]{2,1,0:T(8,128)S(1)}, u32[]{:S(2)}, u32[]{:S(2)}) %collective-permute-start.7) | collective-permute-done | bytes 540704 | tf_op jit(solution)/shard_map/ppermute | solution.py:438
  33.2 3.9 %shard_map.39 = (f32[24,88,128]{2,1,0:T(8,128)S(1)}, f32[16,88,128]{2,1,0:T(8,128)S(1)}, f32[8,80,128]{2,1,0:T(8,128)S(1)}, f32[8,80,128]{2,1,0:T(8,128)S(1)}, f32[28,88,128]{2,1,0:T(8,128)S(1)}) custom-call(f32[16,88,128]{2,1,0:T(8,128)S(1)} %get-tuple-element.47.refs_0_.refs_11_, f32[12,88,128]{2,1,0:T(8,128)S(1)} %collective-permute-done.6.refs_1_, ...), custom_call_target="tpu_custom_call" | custom-call | flops 1 | bytes 9224192 | tf_op jit(solution)/shard_map/pallas_call | solution.py:31
  37.2 0.1 collective-permute-start.10
  37.3 0.0 collective-permute-done.5.field.refs_3_
  37.3 0.1 shard_map.40
  37.4 0.5 collective-permute-start.8
  37.9 2.8 %collective-permute-start.9 = (f32[12,88,128]{2,1,0:T(8,128)S(1)}, f32[12,88,128]{2,1,0:T(8,128)S(1)}, u32[]{:S(2)}, u32[]{:S(2)}) collective-permute-start(f32[12,88,128]{2,1,0:T(8,128)S(1)} %get-tuple-element.53), channel_id=1, source_target_pairs={{1,2},{2,1},{5,6},{6,5},{9,10},{10,9},{13,14},{14,13},{17,18},{18,... | collective-permute-start | bytes 1622024 | tf_op jit(solution)/shard_map/ppermute | solution.py:438
  40.8 0.0 collective-permute-done.2.field.refs_0_
  40.8 0.1 shard_map.38
  40.9 0.1 collective-permute-start.3
  40.9 2.7 %collective-permute-start.4 = (f32[12,88,128]{2,1,0:T(8,128)S(1)}, f32[12,88,128]{2,1,0:T(8,128)S(1)}, u32[]{:S(2)}, u32[]{:S(2)}) collective-permute-start(f32[12,88,128]{2,1,0:T(8,128)S(1)} %get-tuple-element.45), channel_id=1, source_target_pairs={{1,2},{2,1},{5,6},{6,5},{9,10},{10,9},{13,14},{14,13},{17,18},{18,... | collective-permute-start | bytes 1622024 | tf_op jit(solution)/shard_map/ppermute | solution.py:438
  43.7 3.0 %collective-permute-start.11 = (f32[8,80,128]{2,1,0:T(8,128)S(1)}, f32[8,80,128]{2,1,0:T(8,128)S(1)}, u32[]{:S(2)}, u32[]{:S(2)}) collective-permute-start(f32[8,80,128]{2,1,0:T(8,128)S(1)} %get-tuple-element.57), channel_id=1, source_target_pairs={{1,2},{2,1},{5,6},{6,5},{9,10},{10,9},{13,14},{14,13},{17,18},{18,... | collective-permute-start | bytes 983048 | tf_op jit(solution)/shard_map/ppermute | solution.py:438
  46.7 11.2 %collective-permute-done.11.refs_2_ = f32[8,80,128]{2,1,0:T(8,128)S(1)} collective-permute-done((f32[8,80,128]{2,1,0:T(8,128)S(1)}, f32[8,80,128]{2,1,0:T(8,128)S(1)}, u32[]{:S(2)}, u32[]{:S(2)}) %collective-permute-start.11) | collective-permute-done | bytes 327712 | tf_op jit(solution)/shard_map/ppermute | solution.py:438
  57.9 3.4 %shard_map.41 = (f32[24,80,128]{2,1,0:T(8,128)S(1)}, f32[16,80,128]{2,1,0:T(8,128)S(1)}, f32[4,72,128]{2,1,0:T(8,128)S(1)}, f32[4,72,128]{2,1,0:T(8,128)S(1)}) custom-call(f32[16,88,128]{2,1,0:T(8,128)S(1)} %get-tuple-element.55.refs_0_.refs_9_, f32[8,80,128]{2,1,0:T(8,128)S(1)} %collective-permute-done.10.refs_1_, ...), custom_call_target="tpu_custom_call" | custom-call | flops 1 | bytes 5947392 | tf_op jit(solution)/shard_map/pallas_call | solution.py:31
  61.2 0.0 collective-permute-done.8.refs_6_
  61.3 0.0 collective-permute-done.4.refs_2_
  61.3 6.4 %shard_map.42 = (f32[24,88,128]{2,1,0:T(8,128)S(1)}, f32[16,88,128]{2,1,0:T(8,128)S(1)}, f32[8,72,128]{2,1,0:T(8,128)S(1)}, f32[8,72,128]{2,1,0:T(8,128)S(1)}, f32[8,128,128]{2,1,0:T(8,128)S(1)}) custom-call(f32[16,88,128]{2,1,0:T(8,128)S(1)} %collective-permute-done.2.field.refs_0_, f32[12,88,128]{2,1,0:T(8,128)S(1)} %collective-permute-done.3.refs_1_, ...), custom_call_target="tpu_custom_call" | custom-call | flops 1 | bytes 11583488 | tf_op jit(solution)/shard_map/pallas_call | solution.py:31
  67.7 0.1 collective-permute-start.12
  67.8 2.9 %collective-permute-start.13 = (f32[8,72,128]{2,1,0:T(8,128)S(1)}, f32[8,72,128]{2,1,0:T(8,128)S(1)}, u32[]{:S(2)}, u32[]{:S(2)}) collective-permute-start(f32[8,72,128]{2,1,0:T(8,128)S(1)} %get-tuple-element.61), channel_id=1, source_target_pairs={{1,2},{2,1},{5,6},{6,5},{9,10},{10,9},{13,14},{14,13},{17,18},{18,... | collective-permute-start | bytes 884744 | tf_op jit(solution)/shard_map/ppermute | solution.py:438
  70.6 0.1 collective-permute-start.14
  70.7 2.9 %collective-permute-start.15 = (f32[4,72,128]{2,1,0:T(8,128)S(1)}, f32[4,72,128]{2,1,0:T(8,128)S(1)}, u32[]{:S(2)}, u32[]{:S(2)}) collective-permute-start(f32[4,72,128]{2,1,0:T(8,128)S(1)} %get-tuple-element.65), channel_id=1, source_target_pairs={{1,2},{2,1},{5,6},{6,5},{9,10},{10,9},{13,14},{14,13},{17,18},{18,... | collective-permute-start | bytes 442376 | tf_op jit(solution)/shard_map/ppermute | solution.py:438
  73.7 0.0 collective-permute-done.14.refs_1_
  73.7 3.7 %collective-permute-done.15.refs_2_ = f32[4,72,128]{2,1,0:T(8,128)S(1)} collective-permute-done((f32[4,72,128]{2,1,0:T(8,128)S(1)}, f32[4,72,128]{2,1,0:T(8,128)S(1)}, u32[]{:S(2)}, u32[]{:S(2)}) %collective-permute-start.15) | collective-permute-done | bytes 147488 | tf_op jit(solution)/shard_map/ppermute | solution.py:438
  77.4 1.3 %shard_map.43.refs_7_ = f32[16,72,128]{2,1,0:T(8,128)S(1)} custom-call(f32[16,80,128]{2,1,0:T(8,128)S(1)} %get-tuple-element.63.refs_0_.refs_6_, f32[4,72,128]{2,1,0:T(8,128)S(1)} %collective-permute-done.14.refs_1_, f32[4,72,128]{2,1,0:T(8,128)S(1)} %collective-permute-done.15.refs_2_, f32[24,80,128]{2,1,0:T(8,128)S(1)} %get-tuple-element.58.refs_10_.refs_3_, ...), custom_call_target="tpu_custom_call" | custom-call | flops 1 | bytes 4079616 | tf_op jit(solution)/shard_map/pallas_call | solution.py:31
  78.7 0.0 collective-permute-done.12.refs_1_
  78.8 4.4 %shard_map.44 = (f32[24,72,128]{2,1,0:T(8,128)}, f32[8,32,128]{2,1,0:T(8,128)S(1)}, f32[8,32,128]{2,1,0:T(8,128)S(1)}, f32[8,32,128]{2,1,0:T(8,128)S(1)}, f32[8,32,128]{2,1,0:T(8,128)S(1)}) custom-call(f32[16,88,128]{2,1,0:T(8,128)S(1)} %get-tuple-element.59.refs_0_, f32[8,72,128]{2,1,0:T(8,128)S(1)} %collective-permute-done.12.refs_1_, ...), custom_call_target="tpu_custom_call" | custom-call | flops 1 | bytes 7127040 | tf_op jit(solution)/shard_map/pallas_call | solution.py:31
  83.2 1.3 %collective-permute-start.16 = (f32[8,32,128]{2,1,0:T(8,128)S(1)}, f32[8,32,128]{2,1,0:T(8,128)S(1)}, u32[]{:S(2)}, u32[]{:S(2)}) collective-permute-start(f32[8,32,128]{2,1,0:T(8,128)S(1)} %get-tuple-element.68), channel_id=1, source_target_pairs={{0,8},{8,0},{16,24},{24,16},{1,9},{9,1},{17,25},{25,17},{2,10},{10... | collective-permute-start | bytes 393224 | tf_op jit(solution)/shard_map/ppermute | solution.py:540
  84.5 2.3 %collective-permute-start.17 = (f32[8,32,128]{2,1,0:T(8,128)S(1)}, f32[8,32,128]{2,1,0:T(8,128)S(1)}, u32[]{:S(2)}, u32[]{:S(2)}) collective-permute-start(f32[8,32,128]{2,1,0:T(8,128)S(1)} %get-tuple-element.69), channel_id=1, source_target_pairs={{0,16},{8,24},{16,0},{24,8},{1,17},{9,25},{17,1},{25,9},{2,18},{10... | collective-permute-start | bytes 393224 | tf_op jit(solution)/shard_map/ppermute | solution.py:540
  86.8 0.0 collective-permute-start.18
  86.8 2.4 %collective-permute-done.16.refs_1_ = f32[8,32,128]{2,1,0:T(8,128)S(1)} collective-permute-done((f32[8,32,128]{2,1,0:T(8,128)S(1)}, f32[8,32,128]{2,1,0:T(8,128)S(1)}, u32[]{:S(2)}, u32[]{:S(2)}) %collective-permute-start.16) | collective-permute-done | bytes 131104 | tf_op jit(solution)/shard_map/ppermute | solution.py:540
  89.2 4.0 %collective-permute-done.17.refs_2_ = f32[8,32,128]{2,1,0:T(8,128)S(1)} collective-permute-done((f32[8,32,128]{2,1,0:T(8,128)S(1)}, f32[8,32,128]{2,1,0:T(8,128)S(1)}, u32[]{:S(2)}, u32[]{:S(2)}) %collective-permute-start.17) | collective-permute-done | bytes 131104 | tf_op jit(solution)/shard_map/ppermute | solution.py:540
  93.2 0.0 collective-permute-done.18.refs_3_
  93.2 0.9 shard_map.45
  (8 shorter events, 0.0 us)
Async XLA Ops:
  0.0 8.0 %copy-start = (f32[1,1,2,16,128,128]{5,4,3,2,1,0:T(8,128)S(1)}, f32[1,1,2,16,128,128]{5,4,3,2,1,0:T(8,128)}, u32[]{:S(2)}) copy-start(f32[1,1,2,16,128,128]{5,4,3,2,1,0:T(8,128)} %states.1) | copy-start | bytes 6291460
  3.2 6.7 %copy-start.1 = (f32[16,128,128]{2,1,0:T(8,128)S(1)}, f32[16,128,128]{2,1,0:T(8,128)}, u32[]{:S(2)}) copy-start(f32[16,128,128]{2,1,0:T(8,128)} %courant.1) | copy-start | bytes 3145732
  3.2 7.5 %collective-permute-start = (f32[10,128,128]{2,1,0:T(8,128)}, f32[10,128,128]{2,1,0:T(8,128)S(1)}, u32[]{:S(2)}, u32[]{:S(2)}) collective-permute-start(f32[10,128,128]{2,1,0:T(8,128)} %get-tuple-element.41), channel_id=1, source_target_pairs={{0,1},{1,0},{2,3},{3,2},{4,5},{5,4},{6,7},{7,6},{8,9},{9,8},{10,11... | collective-permute-start | bytes 1966088 | tf_op jit(solution)/shard_map/ppermute | solution.py:439
  3.3 13.4 %collective-permute-start.1 = (f32[10,128,128]{2,1,0:T(8,128)}, f32[10,128,128]{2,1,0:T(8,128)S(1)}, u32[]{:S(2)}, u32[]{:S(2)}) collective-permute-start(f32[10,128,128]{2,1,0:T(8,128)} %get-tuple-element.42), channel_id=1, source_target_pairs={{1,2},{2,1},{5,6},{6,5},{9,10},{10,9},{13,14},{14,13},{17,18},{18,... | collective-permute-start | bytes 1966088 | tf_op jit(solution)/shard_map/ppermute | solution.py:438
  8.6 8.1 %copy-start.2 = (f32[1,12,16,128]{3,2,1,0:T(8,128)S(1)}, f32[1,12,16,128]{3,2,1,0:T(8,128)}, u32[]{:S(2)}) copy-start(f32[1,12,16,128]{3,2,1,0:T(8,128)} %rec.3) | copy-start | bytes 294916
  8.6 28.6 %collective-permute-start.5 = (f32[16,88,128]{2,1,0:T(8,128)S(1)}, f32[16,88,128]{2,1,0:T(8,128)S(1)}, u32[]{:S(2)}, u32[]{:S(2)}) collective-permute-start(f32[16,88,128]{2,1,0:T(8,128)S(1)} %get-tuple-element.46), channel_id=1, source_target_pairs={{0,4},{4,0},{1,5},{5,1},{2,6},{6,2},{3,7},{7,3},{8,12},{12,8},{9,1... | collective-permute-start | bytes 2162696 | tf_op jit(solution)/shard_map/ppermute | solution.py:442
  20.5 20.3 %collective-permute-start.2 = (f32[16,88,128]{2,1,0:T(8,128)S(1)}, f32[16,88,128]{2,1,0:T(8,128)S(1)}, u32[]{:S(2)}, u32[]{:S(2)}) collective-permute-start(f32[16,88,128]{2,1,0:T(8,128)S(1)} %get-tuple-element.43), channel_id=1, source_target_pairs={{0,4},{4,0},{1,5},{5,1},{2,6},{6,2},{3,7},{7,3},{8,12},{12,8},{9,1... | collective-permute-start | bytes 2162696 | tf_op jit(solution)/shard_map/ppermute | solution.py:442
  22.3 3.1 %collective-permute-start.6 = (f32[12,88,128]{2,1,0:T(8,128)S(1)}, f32[12,88,128]{2,1,0:T(8,128)S(1)}, u32[]{:S(2)}, u32[]{:S(2)}) collective-permute-start(f32[12,88,128]{2,1,0:T(8,128)S(1)} %get-tuple-element.48), channel_id=1, source_target_pairs={{0,1},{1,0},{2,3},{3,2},{4,5},{5,4},{6,7},{7,6},{8,9},{9,8},{10,11... | collective-permute-start | bytes 1622024 | tf_op jit(solution)/shard_map/ppermute | solution.py:439
  22.3 11.0 %collective-permute-start.7 = (f32[12,88,128]{2,1,0:T(8,128)S(1)}, f32[12,88,128]{2,1,0:T(8,128)S(1)}, u32[]{:S(2)}, u32[]{:S(2)}) collective-permute-start(f32[12,88,128]{2,1,0:T(8,128)S(1)} %get-tuple-element.49), channel_id=1, source_target_pairs={{1,2},{2,1},{5,6},{6,5},{9,10},{10,9},{13,14},{14,13},{17,18},{18,... | collective-permute-start | bytes 1622024 | tf_op jit(solution)/shard_map/ppermute | solution.py:438
  37.2 6.5 %collective-permute-start.10 = (f32[8,80,128]{2,1,0:T(8,128)S(1)}, f32[8,80,128]{2,1,0:T(8,128)S(1)}, u32[]{:S(2)}, u32[]{:S(2)}) collective-permute-start(f32[8,80,128]{2,1,0:T(8,128)S(1)} %get-tuple-element.56), channel_id=1, source_target_pairs={{0,1},{1,0},{2,3},{3,2},{4,5},{5,4},{6,7},{7,6},{8,9},{9,8},{10,11... | collective-permute-start | bytes 983048 | tf_op jit(solution)/shard_map/ppermute | solution.py:439
  37.4 23.9 %collective-permute-start.8 = (f32[12,88,128]{2,1,0:T(8,128)S(1)}, f32[12,88,128]{2,1,0:T(8,128)S(1)}, u32[]{:S(2)}, u32[]{:S(2)}) collective-permute-start(f32[12,88,128]{2,1,0:T(8,128)S(1)} %get-tuple-element.52), channel_id=1, source_target_pairs={{0,1},{1,0},{2,3},{3,2},{4,5},{5,4},{6,7},{7,6},{8,9},{9,8},{10,11... | collective-permute-start | bytes 1622024 | tf_op jit(solution)/shard_map/ppermute | solution.py:439
  37.9 23.4 %collective-permute-start.9 = (f32[12,88,128]{2,1,0:T(8,128)S(1)}, f32[12,88,128]{2,1,0:T(8,128)S(1)}, u32[]{:S(2)}, u32[]{:S(2)}) collective-permute-start(f32[12,88,128]{2,1,0:T(8,128)S(1)} %get-tuple-element.53), channel_id=1, source_target_pairs={{1,2},{2,1},{5,6},{6,5},{9,10},{10,9},{13,14},{14,13},{17,18},{18,... | collective-permute-start | bytes 1622024 | tf_op jit(solution)/shard_map/ppermute | solution.py:438
  40.9 20.4 %collective-permute-start.3 = (f32[12,88,128]{2,1,0:T(8,128)S(1)}, f32[12,88,128]{2,1,0:T(8,128)S(1)}, u32[]{:S(2)}, u32[]{:S(2)}) collective-permute-start(f32[12,88,128]{2,1,0:T(8,128)S(1)} %get-tuple-element.44), channel_id=1, source_target_pairs={{0,1},{1,0},{2,3},{3,2},{4,5},{5,4},{6,7},{7,6},{8,9},{9,8},{10,11... | collective-permute-start | bytes 1622024 | tf_op jit(solution)/shard_map/ppermute | solution.py:439
  40.9 20.3 %collective-permute-start.4 = (f32[12,88,128]{2,1,0:T(8,128)S(1)}, f32[12,88,128]{2,1,0:T(8,128)S(1)}, u32[]{:S(2)}, u32[]{:S(2)}) collective-permute-start(f32[12,88,128]{2,1,0:T(8,128)S(1)} %get-tuple-element.45), channel_id=1, source_target_pairs={{1,2},{2,1},{5,6},{6,5},{9,10},{10,9},{13,14},{14,13},{17,18},{18,... | collective-permute-start | bytes 1622024 | tf_op jit(solution)/shard_map/ppermute | solution.py:438
  43.7 14.2 %collective-permute-start.11 = (f32[8,80,128]{2,1,0:T(8,128)S(1)}, f32[8,80,128]{2,1,0:T(8,128)S(1)}, u32[]{:S(2)}, u32[]{:S(2)}) collective-permute-start(f32[8,80,128]{2,1,0:T(8,128)S(1)} %get-tuple-element.57), channel_id=1, source_target_pairs={{1,2},{2,1},{5,6},{6,5},{9,10},{10,9},{13,14},{14,13},{17,18},{18,... | collective-permute-start | bytes 983048 | tf_op jit(solution)/shard_map/ppermute | solution.py:438
  67.7 11.0 %collective-permute-start.12 = (f32[8,72,128]{2,1,0:T(8,128)S(1)}, f32[8,72,128]{2,1,0:T(8,128)S(1)}, u32[]{:S(2)}, u32[]{:S(2)}) collective-permute-start(f32[8,72,128]{2,1,0:T(8,128)S(1)} %get-tuple-element.60), channel_id=1, source_target_pairs={{0,1},{1,0},{2,3},{3,2},{4,5},{5,4},{6,7},{7,6},{8,9},{9,8},{10,11... | collective-permute-start | bytes 884744 | tf_op jit(solution)/shard_map/ppermute | solution.py:439
  67.8 11.0 %collective-permute-start.13 = (f32[8,72,128]{2,1,0:T(8,128)S(1)}, f32[8,72,128]{2,1,0:T(8,128)S(1)}, u32[]{:S(2)}, u32[]{:S(2)}) collective-permute-start(f32[8,72,128]{2,1,0:T(8,128)S(1)} %get-tuple-element.61), channel_id=1, source_target_pairs={{1,2},{2,1},{5,6},{6,5},{9,10},{10,9},{13,14},{14,13},{17,18},{18,... | collective-permute-start | bytes 884744 | tf_op jit(solution)/shard_map/ppermute | solution.py:438
  70.6 3.0 %collective-permute-start.14 = (f32[4,72,128]{2,1,0:T(8,128)S(1)}, f32[4,72,128]{2,1,0:T(8,128)S(1)}, u32[]{:S(2)}, u32[]{:S(2)}) collective-permute-start(f32[4,72,128]{2,1,0:T(8,128)S(1)} %get-tuple-element.64), channel_id=1, source_target_pairs={{0,1},{1,0},{2,3},{3,2},{4,5},{5,4},{6,7},{7,6},{8,9},{9,8},{10,11... | collective-permute-start | bytes 442376 | tf_op jit(solution)/shard_map/ppermute | solution.py:439
  70.7 6.7 %collective-permute-start.15 = (f32[4,72,128]{2,1,0:T(8,128)S(1)}, f32[4,72,128]{2,1,0:T(8,128)S(1)}, u32[]{:S(2)}, u32[]{:S(2)}) collective-permute-start(f32[4,72,128]{2,1,0:T(8,128)S(1)} %get-tuple-element.65), channel_id=1, source_target_pairs={{1,2},{2,1},{5,6},{6,5},{9,10},{10,9},{13,14},{14,13},{17,18},{18,... | collective-permute-start | bytes 442376 | tf_op jit(solution)/shard_map/ppermute | solution.py:438
  83.2 6.0 %collective-permute-start.16 = (f32[8,32,128]{2,1,0:T(8,128)S(1)}, f32[8,32,128]{2,1,0:T(8,128)S(1)}, u32[]{:S(2)}, u32[]{:S(2)}) collective-permute-start(f32[8,32,128]{2,1,0:T(8,128)S(1)} %get-tuple-element.68), channel_id=1, source_target_pairs={{0,8},{8,0},{16,24},{24,16},{1,9},{9,1},{17,25},{25,17},{2,10},{10... | collective-permute-start | bytes 393224 | tf_op jit(solution)/shard_map/ppermute | solution.py:540
  84.5 8.7 %collective-permute-start.17 = (f32[8,32,128]{2,1,0:T(8,128)S(1)}, f32[8,32,128]{2,1,0:T(8,128)S(1)}, u32[]{:S(2)}, u32[]{:S(2)}) collective-permute-start(f32[8,32,128]{2,1,0:T(8,128)S(1)} %get-tuple-element.69), channel_id=1, source_target_pairs={{0,16},{8,24},{16,0},{24,8},{1,17},{9,25},{17,1},{25,9},{2,18},{10... | collective-permute-start | bytes 393224 | tf_op jit(solution)/shard_map/ppermute | solution.py:540
  86.8 6.4 %collective-permute-start.18 = (f32[8,32,128]{2,1,0:T(8,128)S(1)}, f32[8,32,128]{2,1,0:T(8,128)S(1)}, u32[]{:S(2)}, u32[]{:S(2)}) collective-permute-start(f32[8,32,128]{2,1,0:T(8,128)S(1)} %get-tuple-element.70), channel_id=1, source_target_pairs={{0,24},{8,16},{16,8},{24,0},{1,25},{9,17},{17,9},{25,1},{2,26},{10... | collective-permute-start | bytes 393224 | tf_op jit(solution)/shard_map/ppermute | solution.py:540
